TPU v7x, 32 devices: a whole 2x2x4 slice. The times are simulated.
32 devices in a mesh: row: 4 (over y, x), col: 8 (over z, core).
Axes of the slice: x: 2, y: 2, z: 4, core: 2. Of those that a mesh axis runs over, the one named last changes fastest.
Arguments:
- tokens: bfloat16 [294912, 1024], P(('row', 'col')), may hold values from -6 to 6
- router_weight: bfloat16 [1024], P(('row', 'col')), may hold values from -0.1875 to 0.1875
- norm_first: bfloat16 [1024], P(('row', 'col')), may hold values from 0.099609375 to 1.8984375
- qkv_weight: bfloat16 [1024, 3072], P('row', 'col'), may hold values from -0.1875 to 0.1875
- out_weight: bfloat16 [1024, 1024], P('col', 'row'), may hold values from -0.75 to 0.75
- norm_second: bfloat16 [1024], P(('row', 'col')), may hold values from 0.099609375 to 1.8984375
- up_weight: bfloat16 [1024, 4096], P('row', 'col'), may hold values from -0.1875 to 0.1875
- down_weight: bfloat16 [4096, 1024], P('col', 'row'), may hold values from -0.09375 to 0.09375
- route_index: int32 [288, 128], P(('row', 'col')), may hold values from 0 to 1023, as said below
- out_cotangent: bfloat16 [294912, 1024], P(('row', 'col')), may hold values from -6 to 6
Outputs:
- output: bfloat16 [294912, 1024], P(('row', 'col'))
- input_grad: float32 [294912, 1024], P(('row', 'col'))
- router_grad: float32 [1024], P(('row', 'col'))
- norm_first_grad: float32 [1024], P(('row', 'col'))
- qkv_grad: float32 [1024, 3072], P('row', 'col')
- out_grad: float32 [1024, 1024], P('col', 'row')
- norm_second_grad: float32 [1024], P(('row', 'col'))
- up_grad: float32 [1024, 4096], P('row', 'col')
- down_grad: float32 [4096, 1024], P('col', 'row')
Inputs may be any that keep to these rules, and one draw needn't show every extreme that they name: `route_index`: each row lists 128 distinct positions of one sequence in increasing order; the first is 0 and the last 1023.
All inputs are finite; a program needn't handle non-finite values.
Results may differ from a plain program's by a relative error of at most 0.019.
Values may be sent and summed in bfloat16 or wider, within the bound.
No kernel may reach another device: no remote copies, remote signals or barrier semaphores. Data moves between devices by JAX's collectives and lax.ppermute only.
A program may use at most 320 MiB of HBM per device.

v0:
```python
import jax
import jax.numpy as jnp
from jax import lax
from jax.sharding import PartitionSpec as P

HEADS = 16
HD = 64


epsilon = 1e-06


def local(
    tokens,
    router_weight,
    norm_first,
    qkv_weight,
    out_weight,
    norm_second,
    up_weight,
    down_weight,
    route_index,
    out_cotangent,
):
    seq_local, routed = route_index.shape
    seq_length = tokens.shape[0] // seq_local
    width = tokens.shape[1]
    starts = jnp.arange(seq_local, dtype=jnp.int32) * seq_length
    token_rows = (route_index + starts[:, None]).reshape(-1)
    row_count = token_rows.shape[0]
    col_pieces = (
        lax.all_gather(qkv_weight, "col", axis=1, tiled=True),
        lax.all_gather(out_weight, "col", axis=0, tiled=True),
        lax.all_gather(up_weight, "col", axis=1, tiled=True),
        lax.all_gather(down_weight, "col", axis=0, tiled=True),
        lax.all_gather(norm_first, "col", axis=0, tiled=True),
        lax.all_gather(norm_second, "col", axis=0, tiled=True),
        lax.all_gather(router_weight, "col", axis=0, tiled=True),
    )
    gathered = (
        lax.all_gather(col_pieces[0], "row", axis=0, tiled=True),
        lax.all_gather(col_pieces[1], "row", axis=1, tiled=True),
        lax.all_gather(col_pieces[2], "row", axis=0, tiled=True),
        lax.all_gather(col_pieces[3], "row", axis=1, tiled=True),
        lax.all_gather(col_pieces[4], "row", axis=0, tiled=True),
        lax.all_gather(col_pieces[5], "row", axis=0, tiled=True),
        lax.all_gather(col_pieces[6], "row", axis=0, tiled=True),
    )
    w_qkv, w_out, w_up, w_down, first_full, second_full, router_full = gathered
    first_gain = first_full.astype(jnp.float32)
    second_gain = second_full.astype(jnp.float32)
    router_vec = router_full.astype(jnp.float32)
    picked_full = tokens[token_rows]
    h_full = picked_full.astype(jnp.float32)
    gate_value = jax.nn.sigmoid(
        jnp.dot(picked_full, router_full, preferred_element_type=jnp.float32)
    )
    inverse_first = lax.rsqrt(jnp.mean(h_full * h_full, axis=-1, keepdims=True) + epsilon)
    normed = (h_full * inverse_first * first_gain).astype(jnp.bfloat16)
    projected = jnp.dot(normed, w_qkv, preferred_element_type=jnp.float32).astype(jnp.bfloat16)
    heads_qkv = projected.reshape(seq_local, routed, HEADS, 3, HD)
    queries = heads_qkv[:, :, :, 0]
    key_rows = heads_qkv[:, :, :, 1]
    values = heads_qkv[:, :, :, 2]
    scaling = HD ** (-0.5)
    places = jnp.arange(routed, dtype=jnp.int32)
    causal = places[:, None] >= places[None, :]
    scores = (
        jnp.einsum("sqhe,skhe->shqk", queries, key_rows, preferred_element_type=jnp.float32)
        * scaling
    )
    scores = jnp.where(causal, scores, -1e30)
    highest = jnp.max(scores, axis=-1, keepdims=True)
    expanded = jnp.exp(scores - highest)
    totals = jnp.sum(expanded, axis=-1, keepdims=True)
    attn_probs = (expanded / totals).astype(jnp.bfloat16)
    log_total = highest + jnp.log(totals)
    mixed = jnp.einsum("shqk,skhe->sqhe", attn_probs, values, preferred_element_type=jnp.float32)
    context = mixed.reshape(row_count, width).astype(jnp.bfloat16)
    attn_out = jnp.dot(context, w_out, preferred_element_type=jnp.float32)
    middle = h_full + attn_out
    inverse_mid = lax.rsqrt(jnp.mean(middle * middle, axis=-1, keepdims=True) + epsilon)
    normed_mid = (middle * inverse_mid * second_gain).astype(jnp.bfloat16)
    pre_act = jnp.dot(normed_mid, w_up, preferred_element_type=jnp.float32)
    activated, gelu_back = jax.vjp(jax.nn.gelu, pre_act)
    hidden = activated.astype(jnp.bfloat16)
    mlp_out = jnp.dot(hidden, w_down, preferred_element_type=jnp.float32)
    branch = attn_out + mlp_out
    output = (
        tokens.astype(jnp.float32)
        .at[token_rows]
        .add(gate_value[:, None] * branch)
        .astype(jnp.bfloat16)
    )
    back_pieces = (
        lax.all_gather(qkv_weight, "col", axis=1, tiled=True),
        lax.all_gather(out_weight, "col", axis=0, tiled=True),
        lax.all_gather(up_weight, "col", axis=1, tiled=True),
        lax.all_gather(down_weight, "col", axis=0, tiled=True),
    )
    w_qkv, w_out, w_up, w_down = (
        lax.all_gather(back_pieces[0], "row", axis=0, tiled=True),
        lax.all_gather(back_pieces[1], "row", axis=1, tiled=True),
        lax.all_gather(back_pieces[2], "row", axis=0, tiled=True),
        lax.all_gather(back_pieces[3], "row", axis=1, tiled=True),
    )
    grad_out = out_cotangent.astype(jnp.float32)
    grad_rows = grad_out[token_rows]
    gate_grad = jnp.sum(grad_rows * branch, axis=-1)
    grad_branch = gate_value[:, None] * grad_rows
    grad_mlp = grad_branch.astype(jnp.bfloat16)
    grad_hidden = jnp.dot(grad_mlp, w_down.T, preferred_element_type=jnp.float32)
    down_part = jnp.dot(hidden.T, grad_mlp, preferred_element_type=jnp.float32)
    grad_pre = gelu_back(grad_hidden)[0].astype(jnp.bfloat16)
    up_part = jnp.dot(normed_mid.T, grad_pre, preferred_element_type=jnp.float32)
    grad_normed_mid = jnp.dot(grad_pre, w_up.T, preferred_element_type=jnp.float32)
    second_part = jnp.sum(grad_normed_mid * middle * inverse_mid, axis=0)
    grad_scaled_mid = grad_normed_mid * second_gain
    mid_sum = jnp.sum(grad_scaled_mid * middle, axis=-1, keepdims=True)
    grad_middle = inverse_mid * grad_scaled_mid - middle * inverse_mid**3 * mid_sum / width
    grad_attn = (grad_branch + grad_middle).astype(jnp.bfloat16)
    grad_context = jnp.dot(grad_attn, w_out.T, preferred_element_type=jnp.float32).astype(
        jnp.bfloat16
    )
    out_part = jnp.dot(context.T, grad_attn, preferred_element_type=jnp.float32)
    grad_heads = grad_context.reshape(seq_local, routed, HEADS, HD)
    again = (
        jnp.einsum("sqhe,skhe->shqk", queries, key_rows, preferred_element_type=jnp.float32)
        * scaling
    )
    again = jnp.where(causal, again, -1e30)
    probs_exact = jnp.exp(again - log_total)
    grad_probs = jnp.einsum(
        "sqhe,skhe->shqk", grad_heads, values, preferred_element_type=jnp.float32
    )
    inner_sum = jnp.sum(grad_probs * probs_exact, axis=-1, keepdims=True)
    grad_scores = (probs_exact * (grad_probs - inner_sum)).astype(jnp.bfloat16)
    grad_query = (
        jnp.einsum("shqk,skhe->sqhe", grad_scores, key_rows, preferred_element_type=jnp.float32)
        * scaling
    )
    grad_key = (
        jnp.einsum("shqk,sqhe->skhe", grad_scores, queries, preferred_element_type=jnp.float32)
        * scaling
    )
    grad_value = jnp.einsum(
        "shqk,sqhe->skhe", attn_probs, grad_heads, preferred_element_type=jnp.float32
    )
    grad_projected = (
        jnp.stack([grad_query, grad_key, grad_value], axis=3)
        .reshape(row_count, 3 * width)
        .astype(jnp.bfloat16)
    )
    qkv_part = jnp.dot(normed.T, grad_projected, preferred_element_type=jnp.float32)
    grad_normed = jnp.dot(grad_projected, w_qkv.T, preferred_element_type=jnp.float32)
    first_part = jnp.sum(grad_normed * h_full * inverse_first, axis=0)
    grad_scaled_first = grad_normed * first_gain
    first_sum = jnp.sum(grad_scaled_first * h_full, axis=-1, keepdims=True)
    grad_norm_in = inverse_first * grad_scaled_first - h_full * inverse_first**3 * first_sum / width
    grad_logit = gate_grad * gate_value * (1.0 - gate_value)
    router_part = jnp.sum(grad_logit[:, None] * h_full, axis=0)
    grad_picked = grad_middle + grad_norm_in + grad_logit[:, None] * router_vec
    input_grad = grad_out.at[token_rows].add(grad_picked)
    all_pieces = (
        lax.psum_scatter(
            qkv_part.astype(jnp.bfloat16), "row", scatter_dimension=0, tiled=True
        ).astype(jnp.float32),
        lax.psum_scatter(
            out_part.astype(jnp.bfloat16), "row", scatter_dimension=1, tiled=True
        ).astype(jnp.float32),
        lax.psum_scatter(
            up_part.astype(jnp.bfloat16), "row", scatter_dimension=0, tiled=True
        ).astype(jnp.float32),
        lax.psum_scatter(
            down_part.astype(jnp.bfloat16), "row", scatter_dimension=1, tiled=True
        ).astype(jnp.float32),
        lax.psum_scatter(
            first_part.astype(jnp.bfloat16), "row", scatter_dimension=0, tiled=True
        ).astype(jnp.float32),
        lax.psum_scatter(
            second_part.astype(jnp.bfloat16), "row", scatter_dimension=0, tiled=True
        ).astype(jnp.float32),
        lax.psum_scatter(
            router_part.astype(jnp.bfloat16), "row", scatter_dimension=0, tiled=True
        ).astype(jnp.float32),
    )
    summed = (
        lax.psum_scatter(
            all_pieces[0].astype(jnp.bfloat16), "col", scatter_dimension=1, tiled=True
        ).astype(jnp.float32),
        lax.psum_scatter(
            all_pieces[1].astype(jnp.bfloat16), "col", scatter_dimension=0, tiled=True
        ).astype(jnp.float32),
        lax.psum_scatter(
            all_pieces[2].astype(jnp.bfloat16), "col", scatter_dimension=1, tiled=True
        ).astype(jnp.float32),
        lax.psum_scatter(
            all_pieces[3].astype(jnp.bfloat16), "col", scatter_dimension=0, tiled=True
        ).astype(jnp.float32),
        lax.psum_scatter(
            all_pieces[4].astype(jnp.bfloat16), "col", scatter_dimension=0, tiled=True
        ).astype(jnp.float32),
        lax.psum_scatter(
            all_pieces[5].astype(jnp.bfloat16), "col", scatter_dimension=0, tiled=True
        ).astype(jnp.float32),
        lax.psum_scatter(
            all_pieces[6].astype(jnp.bfloat16), "col", scatter_dimension=0, tiled=True
        ).astype(jnp.float32),
    )
    qkv_grad, out_grad, up_grad, down_grad, norm_first_grad, norm_second_grad, router_grad = summed
    return (
        output,
        input_grad,
        router_grad,
        norm_first_grad,
        qkv_grad,
        out_grad,
        norm_second_grad,
        up_grad,
        down_grad,
    )


def solution(mesh):
    placed = (
        P(("row", "col"), None),
        P(("row", "col")),
        P(("row", "col")),
        P("row", "col"),
        P("col", "row"),
        P(("row", "col")),
        P("row", "col"),
        P("col", "row"),
        P(("row", "col"), None),
        P(("row", "col"), None),
    )
    return jax.shard_map(
        local,
        mesh=mesh,
        in_specs=placed,
        out_specs=(
            P(("row", "col"), None),
            P(("row", "col"), None),
            P(("row", "col")),
            P(("row", "col")),
            P("row", "col"),
            P("col", "row"),
            P(("row", "col")),
            P("row", "col"),
            P("col", "row"),
        ),
        check_vma=False,
    )
```

profile of v0, /device:TPU:0, one launch (start us, length us, event | category | flops | bytes accessed | tf_op | source)
XLA Modules:
  0.0 964.3 jit_solution(17025223967984651840)
XLA Ops:
  9.5 28.1 %all-gather.11.cloned.1.call-done = bf16[256,3072]{1,0:T(8,128)(2,1)} async-done(((bf16[256,384]{1,0:T(8,128)(2,1)}), bf16[256,3072]{1,0:T(8,128)(2,1)}) %all-gather.11.cloned.1.call-update) | async-done | bytes 1572880 | tf_op jit(solution)/shard_map/all_gather | solution.py:32
  37.7 16.9 %all_gather.56 = bf16[1024,256]{1,0:T(8,128)(2,1)} all-gather(bf16[128,256]{1,0:T(8,128)(2,1)} %param.14), channel_id=1, replica_groups=mesh['row'=4,'col'=8] {'col'}, dimensions={0}, use_global_device_ids=true | all-gather | bytes 589824 | tf_op jit(solution)/shard_map/all_gather | solution.py:33
  54.7 14.2 %all-gather.17.cloned.1.call-done = bf16[256,4096]{1,0:T(8,128)(2,1)} async-done(((bf16[256,512]{1,0:T(8,128)(2,1)}), bf16[256,4096]{1,0:T(8,128)(2,1)}) %all-gather.17.cloned.1.call-update) | async-done | bytes 2097168 | tf_op jit(solution)/shard_map/all_gather | solution.py:34
  71.0 15.3 %all-reduce.10 = (bf16[256]{0:T(256)(128)(2,1)S(1)}, bf16[256]{0:T(256)(128)(2,1)S(1)}, bf16[256]{0:T(256)(128)(2,1)S(1)}) all-reduce(bf16[256]{0:T(256)(128)(2,1)S(1)} %dynamic-update-slice.1, bf16[256]{0:T(256)(128)(2,1)S(1)} %dynamic-update-slice.2, bf16[256]{0:T(256)(128)(2,1)S(1)} %dynamic-update-slice), channel_id=1, replica_groups=mesh['row'=4,'col'=8] {'col'}, use_global_device_ids=true, to_apply=%add.1 | all-reduce | flops 768 | bytes 3072
  86.3 7.9 all-gather.2
  94.2 8.0 all-gather.1
  102.9 16.6 %gather_fusion = bf16[1152,1024]{1,0:T(8,128)(2,1)} fusion(bf16[9216,1024]{1,0:T(8,128)(2,1)} %param.10, s32[2048]{0:T(1024)S(1)} %pad_clamp_fusion), kind=kCustom, calls=%fused_computation | custom fusion | bytes 4723200 | tf_op jit(solution)/shard_map/gather | solution.py:53
  122.5 21.7 %convert_element_type.133 = f32[9216,1024]{1,0:T(8,128)} convert(bf16[9216,1024]{1,0:T(8,128)(2,1)} %param.19) | non-fusion elementwise | flops 9437184 | bytes 56623104 | tf_op jit(solution)/shard_map/convert_element_type | solution.py:107
  144.2 18.3 %gather_fusion.1 = f32[1152,1024]{1,0:T(8,128)} fusion(f32[9216,1024]{1,0:T(8,128)} %convert_element_type.133, s32[2048]{0:T(1024)S(1)} %pad_clamp_fusion), kind=kCustom, calls=%fused_computation.1 | custom fusion | bytes 9441792 | tf_op jit(solution)/shard_map/gather | solution.py:108
  162.6 6.1 copy.65
  168.7 6.7 all-gather
  179.3 12.8 %convolution_convert_fusion = bf16[1152,3072]{1,0:T(8,128)(2,1)} fusion(bf16[1024,3072]{1,0:T(8,128)(2,1)} %all-gather.13.cloned.1.call-done, bf16[1152,1024]{0,1:T(8,128)(2,1)S(1)} %copy.57, f32[1024]{0:T(1024)S(1)} %bitcast.115, f32[1152]{0:T(1024)S(1)} %get-tuple-element.32), kind=kOutput, calls=%fused_computation.21 | convolution fusion | flops 7256014848 | bytes 15737344 | tf_op jit(solution)/shard_map/dot_general | solution.py:60
  192.1 30.3 %reshape.178 = bf16[9,128,16,3,64]{4,3,2,1,0:T(4,128)(2,1)} reshape(bf16[1152,3072]{1,0:T(8,128)(2,1)} %convolution_convert_fusion) | data formatting | bytes 14155776 | tf_op jit(solution)/shard_map/reshape | solution.py:61
  222.4 35.7 %fusion.63 = (bf16[9,128,16,1,64]{4,3,2,1,0:T(2,128)(2,1)}, bf16[9,128,16,1,64]{4,3,2,1,0:T(2,128)(2,1)}, bf16[9,128,16,1,64]{4,3,2,1,0:T(2,128)(2,1)}) fusion(bf16[9,128,16,3,64]{4,3,2,1,0:T(4,128)(2,1)} %reshape.178), kind=kLoop, calls=%fused_computation.106 | loop fusion | bytes 14155776 | tf_op jit(solution)/shard_map/slice | solution.py:64
  258.1 18.9 %copy.91 = bf16[9,128,16,1,64]{1,4,2,0,3:T(8,128)(2,1)S(1)} copy(bf16[9,128,16,1,64]{4,3,2,1,0:T(2,128)(2,1)} %get-tuple-element.25) | data formatting | bytes 4718592
  277.0 20.0 %copy.92 = bf16[9,128,16,1,64]{1,4,2,0,3:T(8,128)(2,1)} copy(bf16[9,128,16,1,64]{4,3,2,1,0:T(2,128)(2,1)} %get-tuple-element.26) | data formatting | bytes 4718592
  297.0 20.3 %copy.93 = bf16[9,128,16,1,64]{1,4,2,0,3:T(8,128)(2,1)} copy(bf16[9,128,16,1,64]{4,3,2,1,0:T(2,128)(2,1)} %get-tuple-element.27) | data formatting | bytes 4718592
  334.7 10.3 %multiply_reduce_fusion.4 = (f32[1152]{0:T(1024)S(1)}, f32[1152,1024]{0,1:T(8,128)}, f32[1152,1024]{0,1:T(8,128)}) fusion(bf16[1152,1024]{0,1:T(8,128)(2,1)} %copy-done.4, bf16[1024,1024]{1,0:T(8,128)(2,1)} %all-gather.15.cloned.1.call-done, bf16[128,8,9,128]{3,2,1,0:T(8,128)(2,1)} %bitcast.106), kind=kOutput, calls=%fused_computation.58 | convolution fusion | flops 2420636672 | bytes 16257536 | tf_op jit(solution)/shard_map/dot_general | solution.py:80
  345.1 18.2 %fusion.62 = f32[1152,4096]{1,0:T(8,128)} fusion(bf16[1024,4096]{1,0:T(8,128)(2,1)} %all-gather.19.cloned.1.call-done, f32[1152,1024]{0,1:T(8,128)} %get-tuple-element.24, f32[1024]{0:T(1024)S(1)} %bitcast.110, f32[1152]{0:T(1024)S(1)} %get-tuple-element.34), kind=kOutput, calls=%fused_computation.105 | convolution fusion | flops 9667215360 | bytes 31990272 | tf_op jit(solution)/shard_map/dot_general | solution.py:84
  363.3 22.6 %all-gather.23.cloned.1.call-done = bf16[4096,1024]{1,0:T(8,128)(2,1)} async-done(((bf16[4096,256]{1,0:T(8,128)(2,1)}), bf16[4096,1024]{1,0:T(8,128)(2,1)}) %all-gather.23.cloned.1.call-update) | async-done | bytes 8388624 | tf_op jit(solution)/shard_map/all_gather | solution.py:44
  385.9 28.3 %fusion.6 = bf16[1152,4096]{1,0:T(8,128)(2,1)} fusion(f32[1152,4096]{1,0:T(8,128)} %fusion.62, bf16[4096,1024]{1,0:T(8,128)(2,1)} %all-gather.23.cloned.1.call-done, f32[1152,1024]{0,1:T(8,128)} %copy.65, f32[1152]{0:T(1024)S(1)} %add_divide_fusion), kind=kOutput, calls=%fused_computation.12 | convolution fusion | flops 9760407552 | bytes 41423360 | tf_op jit(solution)/shard_map/dot_general | solution.py:112
  414.1 19.3 %multiply_reduce_fusion.1 = (bf16[1024]{0:T(1024)(128)(2,1)}, f32[1152]{0:T(1024)S(1)}, f32[1152,1024]{0,1:T(8,128)}) fusion(f32[1152,1024]{0,1:T(8,128)} %get-tuple-element.24, f32[1152]{0:T(1024)S(1)} %get-tuple-element.34, f32[1024]{0:T(1024)S(1)} %bitcast.111, bf16[1152,4096]{1,0:T(8,128)(2,1)} %fusion.6, ...), kind=kOutput, calls=%fused_computation.50 | convolution fusion | flops 9670752256 | bytes 27278336 | tf_op jit(solution)/shard_map/dot_general | solution.py:116
  433.4 26.0 %multiply_reduce_fusion.2 = (f32[1152]{0:T(1024)}, f32[1152,1024]{0,1:T(8,128)}, bf16[1152,1024]{0,1:T(8,128)(2,1)}) fusion(f32[1152,1024]{0,1:T(8,128)} %copy.65, f32[1152]{0:T(1024)S(1)} %add_divide_fusion, f32[1152]{0:T(1024)S(1)} %get-tuple-element.10, f32[1152,1024]{0,1:T(8,128)} %get-tuple-element.24, f32[1152]{0:T(1024)S(1)} %get-tuple-element.33, ...), kind=kOutput, calls=%fused_computation.51 | convolution fusion | flops 9721478144 | bytes 53242368 | tf_op jit(solution)/shard_map/dot_general | solution.py:87
  459.4 7.2 fusion.53
  466.7 6.4 convolution_convert_fusion.3
  473.1 7.7 reshape.179
  480.8 6.9 copy.68
  487.7 7.9 convert_bitcast_fusion
  495.7 7.8 multiply_reduce_fusion
  503.4 11.7 %multiply_convert_fusion.1 = bf16[9,16,128,128]{2,3,1,0:T(8,128)(2,1)} fusion(f32[9,16,128,128]{2,3,1,0:T(8,128)} %get-tuple-element.42, f32[9,16,128,128]{2,3,1,0:T(8,128)} %copy-done, f32[9,16,128]{2,1,0:T(8,128)S(1)} %get-tuple-element.41, f32[9,16,128]{2,1,0:T(8,128)S(1)} %log_add_fusion, pred[128,128]{0,1:T(8,128)(4,1)S(1)} %iota_compare_fusion), kind=kLoop, calls=%fused_computation.22 | loop fusion | flops 14155776 | bytes 23756800 | tf_op jit(solution)/shard_map/convert_element_type | solution.py:137
  515.2 5.8 fusion.31
  523.5 8.8 copy.73
  536.8 10.7 %fusion.12 = bf16[1024,3072]{1,0:T(8,128)(2,1)} fusion(bf16[384,8,9,128]{3,2,1,0:T(8,128)(2,1)S(1)} %bitcast.103, bf16[1152,1024]{0,1:T(8,128)(2,1)S(1)} %copy-done.5, f32[1024]{0:T(1024)S(1)} %bitcast.116, f32[1152]{0:T(1024)S(1)} %copy-done.18), kind=kOutput, calls=%fused_computation.36 | convolution fusion | flops 7255621632 | bytes 15737344 | tf_op jit(solution)/shard_map/dot_general | solution.py:154
  547.6 21.4 %convolution_convert_fusion.1 = bf16[4096,1024]{1,0:T(8,128)(2,1)} fusion(f32[1152,1024]{0,1:T(8,128)} %copy.65, f32[1152]{0:T(1024)S(1)} %add_divide_fusion, f32[1152,4096]{1,0:T(8,128)} %fusion.62), kind=kOutput, calls=%fused_computation.29 | convolution fusion | flops 9712697344 | bytes 31986176 | tf_op jit(solution)/shard_map/dot_general | solution.py:113
  569.1 18.3 %convolution_convert_fusion.2 = bf16[1024,4096]{1,0:T(8,128)(2,1)} fusion(bf16[1152,4096]{1,0:T(8,128)(2,1)} %fusion.6, f32[1152,1024]{0,1:T(8,128)} %get-tuple-element.24, f32[1024]{0:T(1024)S(1)} %bitcast.113, f32[1152]{0:T(1024)S(1)} %get-tuple-element.34), kind=kOutput, calls=%fused_computation.30 | convolution fusion | flops 9671409664 | bytes 22553088 | tf_op jit(solution)/shard_map/dot_general | solution.py:115
  588.0 29.9 %reduce-scatter.11.cloned.1.call-done = bf16[256,3072]{1,0:T(8,128)(2,1)} async-done(((bf16[1024,3072]{1,0:T(8,128)(2,1)}), bf16[256,3072]{1,0:T(8,128)(2,1)}) %reduce-scatter.11.cloned.1.call-update) | async-done | bytes 1572880 | tf_op jit(solution)/shard_map/reduce_scatter | solution.py:165
  620.6 86.9 %reduce-scatter.21.cloned.1.call-done = bf16[4096,256]{1,0:T(8,128)(2,1)} async-done(((bf16[4096,1024]{1,0:T(8,128)(2,1)}), bf16[4096,256]{1,0:T(8,128)(2,1)}) %reduce-scatter.21.cloned.1.call-update) | async-done | bytes 2097168 | tf_op jit(solution)/shard_map/reduce_scatter | solution.py:174
  707.7 21.3 %convert_element_type.120 = f32[9216,1024]{1,0:T(8,128)} convert(bf16[9216,1024]{1,0:T(8,128)(2,1)} %param.10) | non-fusion elementwise | flops 9437184 | bytes 56623104 | tf_op jit(solution)/shard_map/convert_element_type | solution.py:90
  730.9 6.1 copy.64
  737.0 60.6 %reduce-scatter.17.cloned.1.call-done = bf16[256,4096]{1,0:T(8,128)(2,1)} async-done(((bf16[1024,4096]{1,0:T(8,128)(2,1)}), bf16[256,4096]{1,0:T(8,128)(2,1)}) %reduce-scatter.17.cloned.1.call-update) | async-done | bytes 2097168 | tf_op jit(solution)/shard_map/reduce_scatter | solution.py:171
  797.7 15.1 %fusion.27 = (bf16[1024]{0:T(1024)(128)(2,1)S(1)}, f32[1152]{0:T(1024)S(1)}, bf16[1024]{0:T(1024)(128)(2,1)S(1)}, f32[1152,1024]{0,1:T(8,128)S(1)}) fusion(bf16[1152,1024]{0,1:T(8,128)(2,1)S(1)} %copy-done.5, f32[1152]{0:T(1024)S(1)} %copy-done.18, f32[1024]{0:T(1024)S(1)} %bitcast.117, f32[1152]{0:T(1024)S(1)} %subtract_multiply_fusion, ...), kind=kOutput, calls=%fused_computation.49 | convolution fusion | flops 7258371072 | bytes 20469248 | tf_op jit(solution)/shard_map/dot_general | solution.py:155
  812.8 6.7 fusion.23
  819.5 6.1 copy.76
  825.7 39.5 %scatter_fusion.1 = f32[9216,1024]{1,0:T(8,128)} fusion(f32[9216,1024]{1,0:T(8,128)} %convert_element_type.133, s32[1152]{0:T(1024)S(1)} %copy-done.11, f32[1152,1024]{1,0:T(8,128)} %copy.76), kind=kCustom, calls=%fused_computation.3 | custom fusion | flops 1179648 | bytes 14160384 | tf_op jit(solution)/shard_map/scatter-add | solution.py:163
  865.2 9.4 all-reduce.11
  874.8 39.4 %scatter_fusion = f32[9216,1024]{1,0:T(8,128)} fusion(f32[9216,1024]{1,0:T(8,128)} %convert_element_type.120, s32[1152]{0:T(1024)S(1)} %copy-done.11, f32[1152,1024]{1,0:T(8,128)} %copy.64), kind=kCustom, calls=%fused_computation.2 | custom fusion | flops 1179648 | bytes 14160384 | tf_op jit(solution)/shard_map/scatter-add | solution.py:92
  914.1 20.9 %convert_element_type.132 = bf16[9216,1024]{1,0:T(8,128)(2,1)} convert(f32[9216,1024]{1,0:T(8,128)} %scatter_fusion) | non-fusion elementwise | flops 9437184 | bytes 56623104 | tf_op jit(solution)/shard_map/convert_element_type | solution.py:93
  935.0 14.2 %all-reduce.9 = (bf16[256]{0:T(256)(128)(2,1)S(1)}, bf16[256]{0:T(256)(128)(2,1)S(1)}, bf16[256]{0:T(256)(128)(2,1)S(1)}) all-reduce(bf16[256]{0:T(256)(128)(2,1)S(1)} %dynamic-slice.4, bf16[256]{0:T(256)(128)(2,1)S(1)} %dynamic-slice.8, bf16[256]{0:T(256)(128)(2,1)S(1)} %dynamic-slice.12), channel_id=3, replica_groups=mesh['row'=4,'col'=8] {'col'}, use_global_device_ids=true, to_apply=%region_12.13.clone | all-reduce | flops 768 | bytes 3072
  (152 shorter events, 48.2 us)
Async XLA Ops:
  7.2 61.8 %copy-start.28 = (u32[32]{0:T(128)S(1)}, u32[32]{0:T(128)}, u32[]{:S(2)}) copy-start(u32[32]{0:T(128)} %constant.40) | copy-start | bytes 388
  7.2 63.0 %copy-start.29 = (bf16[32]{0:T(256)(128)(2,1)S(1)}, bf16[32]{0:T(256)(128)(2,1)}, u32[]{:S(2)}) copy-start(bf16[32]{0:T(256)(128)(2,1)} %param.15) | copy-start | bytes 196
  7.2 63.3 %copy-start.30 = (bf16[32]{0:T(256)(128)(2,1)S(1)}, bf16[32]{0:T(256)(128)(2,1)}, u32[]{:S(2)}) copy-start(bf16[32]{0:T(256)(128)(2,1)} %param.12) | copy-start | bytes 196
  7.2 63.5 %copy-start.31 = (bf16[32]{0:T(256)(128)(2,1)S(1)}, bf16[32]{0:T(256)(128)(2,1)}, u32[]{:S(2)}) copy-start(bf16[32]{0:T(256)(128)(2,1)} %param.11) | copy-start | bytes 196
  7.2 95.0 %copy-start.26 = (s32[9,128]{1,0:T(8,128)S(1)}, s32[9,128]{1,0:T(8,128)}, u32[]{:S(2)}) copy-start(s32[9,128]{1,0:T(8,128)} %param.18) | copy-start | bytes 13828
  7.2 30.4 %all-gather.11.cloned.1.call-start = ((), (), s32[]{:S(2)}) async-start(), calls=%async_computation.8 | async-start | bytes 1769472 | tf_op jit(solution)/shard_map/all_gather | solution.py:32
  8.0 60.9 %all-gather.17.cloned.1.call-start = ((), (), s32[]{:S(2)}) async-start(), calls=%async_computation.11 | async-start | bytes 2359296 | tf_op jit(solution)/shard_map/all_gather | solution.py:34
  8.7 169.6 %all-gather.21.cloned.1.call-start = ((), (), s32[]{:S(2)}) async-start(), calls=%async_computation.13 | async-start | bytes 2359296 | tf_op jit(solution)/shard_map/all_gather | solution.py:35
  9.4 169.8 %all-gather.13.cloned.1.call-start = ((), (), s32[]{:S(2)}) async-start(), calls=%async_computation.9 | async-start | bytes 7864320 | tf_op jit(solution)/shard_map/all_gather | solution.py:41
  37.7 297.0 %all-gather.15.cloned.1.call-start = ((), (), s32[]{:S(2)}) async-start(), calls=%async_computation.10 | async-start | bytes 2621440 | tf_op jit(solution)/shard_map/all_gather | solution.py:42
  54.7 290.4 %all-gather.19.cloned.1.call-start = ((), (), s32[]{:S(2)}) async-start(), calls=%async_computation.12 | async-start | bytes 10485760 | tf_op jit(solution)/shard_map/all_gather | solution.py:43
  68.9 317.0 %all-gather.23.cloned.1.call-start = ((), (), s32[]{:S(2)}) async-start(), calls=%async_computation.14 | async-start | bytes 10485760 | tf_op jit(solution)/shard_map/all_gather | solution.py:44
  102.2 77.1 %copy-start.21 = (f32[4,1,256]{2,1,0:T(1,128)}, f32[4,1,256]{2,1,0:T(1,128)S(1)}, u32[]{:S(2)}) copy-start(f32[4,1,256]{2,1,0:T(1,128)S(1)} %convert_element_type.155) | copy-start | bytes 12292
  102.3 0.6 copy-start.10
  122.5 56.8 %copy-start.4 = (bf16[1152,1024]{0,1:T(8,128)(2,1)}, bf16[1152,1024]{0,1:T(8,128)(2,1)S(1)}, u32[]{:S(2)}) copy-start(bf16[1152,1024]{0,1:T(8,128)(2,1)S(1)} %copy.57) | copy-start | bytes 7077892
  175.4 16.7 %copy-start.14 = (bf16[4,1,256]{2,1,0:T(2,128)(2,1)}, bf16[4,1,256]{2,1,0:T(2,128)(2,1)S(1)}, u32[]{:S(2)}) copy-start(bf16[4,1,256]{2,1,0:T(2,128)(2,1)S(1)} %all-gather) | copy-start | bytes 6148
  177.8 14.3 %copy-start.12 = (f32[1152]{0:T(1024)}, f32[1152]{0:T(1024)S(1)}, u32[]{:S(2)}) copy-start(f32[1152]{0:T(1024)S(1)} %convolution_reduce_fusion) | copy-start | bytes 13828
  178.4 409.1 %reduce-scatter.13.cloned.1.call-start = ((), (), s32[]{:S(2)}) async-start(), calls=%async_computation.16 | async-start | bytes 2621440 | tf_op jit(solution)/shard_map/reduce_scatter | solution.py:168
  179.3 12.8 %copy-start.17 = (f32[1152]{0:T(1024)}, f32[1152]{0:T(1024)S(1)}, u32[]{:S(2)}) copy-start(f32[1152]{0:T(1024)S(1)} %get-tuple-element.32) | copy-start | bytes 13828
  321.7 3.7 copy-start
  328.2 2.1 copy-start.1
  345.0 88.4 %copy-start.19 = (f32[1152]{0:T(1024)}, f32[1152]{0:T(1024)S(1)}, u32[]{:S(2)}) copy-start(f32[1152]{0:T(1024)S(1)} %get-tuple-element.33) | copy-start | bytes 13828
  433.4 26.0 %copy-start.23 = (f32[1152]{0:T(1024)}, f32[1152]{0:T(1024)S(1)}, u32[]{:S(2)}) copy-start(f32[1152]{0:T(1024)S(1)} %get-tuple-element.10) | copy-start | bytes 13828
  466.6 151.3 %reduce-scatter.11.cloned.1.call-start = ((), (), s32[]{:S(2)}) async-start(), calls=%async_computation.15 | async-start | bytes 7864320 | tf_op jit(solution)/shard_map/reduce_scatter | solution.py:165
  487.7 7.9 copy-start.6
  503.4 11.7 %copy-start.7 = (bf16[9,128,16,1,64]{1,4,2,0,3:T(8,128)(2,1)S(1)}, bf16[9,128,16,1,64]{1,4,2,0,3:T(8,128)(2,1)}, u32[]{:S(2)}) copy-start(bf16[9,128,16,1,64]{1,4,2,0,3:T(8,128)(2,1)} %copy.92) | copy-start | bytes 7077892
  515.2 5.8 copy-start.2
  515.2 5.8 copy-start.3
  521.0 1.7 copy-start.9
  523.5 13.3 %copy-start.5 = (bf16[1152,1024]{0,1:T(8,128)(2,1)S(1)}, bf16[1152,1024]{0,1:T(8,128)(2,1)}, u32[]{:S(2)}) copy-start(bf16[1152,1024]{0,1:T(8,128)(2,1)} %copy-done.4) | copy-start | bytes 7077892
  523.5 13.3 %copy-start.18 = (f32[1152]{0:T(1024)S(1)}, f32[1152]{0:T(1024)}, u32[]{:S(2)}) copy-start(f32[1152]{0:T(1024)} %copy-done.17) | copy-start | bytes 13828
  523.5 13.3 %copy-start.22 = (f32[4,1,256]{2,1,0:T(1,128)S(1)}, f32[4,1,256]{2,1,0:T(1,128)}, u32[]{:S(2)}) copy-start(f32[4,1,256]{2,1,0:T(1,128)} %copy-done.21) | copy-start | bytes 12292
  532.4 4.5 copy-start.8
  547.6 160.0 %reduce-scatter.21.cloned.1.call-start = ((), (), s32[]{:S(2)}) async-start(), calls=%async_computation.20 | async-start | bytes 10485760 | tf_op jit(solution)/shard_map/reduce_scatter | solution.py:174
  569.1 228.6 %reduce-scatter.17.cloned.1.call-start = ((), (), s32[]{:S(2)}) async-start(), calls=%async_computation.18 | async-start | bytes 10485760 | tf_op jit(solution)/shard_map/reduce_scatter | solution.py:171
  587.4 363.0 %reduce-scatter.15.cloned.1.call-start = ((), (), s32[]{:S(2)}) async-start(), calls=%async_computation.17 | async-start | bytes 589824 | tf_op jit(solution)/shard_map/reduce_scatter | solution.py:191
  588.0 363.9 %reduce-scatter.25.cloned.1.call-start = ((), (), s32[]{:S(2)}) async-start(), calls=%async_computation.22 | async-start | bytes 1769472
  620.6 333.2 %reduce-scatter.23.cloned.1.call-start = ((), (), s32[]{:S(2)}) async-start(), calls=%async_computation.21 | async-start | bytes 2359296 | tf_op jit(solution)/shard_map/reduce_scatter | solution.py:197
  707.6 21.4 %copy-start.32 = (u32[32]{0:T(128)S(1)}, u32[32]{0:T(128)}, u32[]{:S(2)}) copy-start(u32[32]{0:T(128)} %constant.58) | copy-start | bytes 388
  707.6 22.6 %copy-start.15 = (bf16[4,1,256]{2,1,0:T(2,128)(2,1)S(1)}, bf16[4,1,256]{2,1,0:T(2,128)(2,1)}, u32[]{:S(2)}) copy-start(bf16[4,1,256]{2,1,0:T(2,128)(2,1)} %copy-done.14) | copy-start | bytes 6148
  707.6 247.9 %reduce-scatter.19.cloned.1.call-start = ((), (), s32[]{:S(2)}) async-start(), calls=%async_computation.19 | async-start | bytes 2359296 | tf_op jit(solution)/shard_map/reduce_scatter | solution.py:194
  730.9 66.7 %copy-start.13 = (f32[1152]{0:T(1024)S(1)}, f32[1152]{0:T(1024)}, u32[]{:S(2)}) copy-start(f32[1152]{0:T(1024)} %copy-done.12) | copy-start | bytes 13828
  730.9 66.7 %copy-start.25 = (f32[1152]{0:T(1024)S(1)}, f32[1152]{0:T(1024)}, u32[]{:S(2)}) copy-start(f32[1152]{0:T(1024)} %get-tuple-element.28) | copy-start | bytes 13828
  797.7 15.1 %copy-start.16 = (f32[1152]{0:T(1024)S(1)}, f32[1152]{0:T(1024)}, u32[]{:S(2)}) copy-start(f32[1152]{0:T(1024)} %get-tuple-element.31) | copy-start | bytes 13828
  797.7 15.1 %copy-start.20 = (f32[1152]{0:T(1024)S(1)}, f32[1152]{0:T(1024)}, u32[]{:S(2)}) copy-start(f32[1152]{0:T(1024)} %copy-done.19) | copy-start | bytes 13828
  797.7 15.1 %copy-start.24 = (f32[1152]{0:T(1024)S(1)}, f32[1152]{0:T(1024)}, u32[]{:S(2)}) copy-start(f32[1152]{0:T(1024)} %copy-done.23) | copy-start | bytes 13828
  819.5 6.2 copy-start.11
  825.7 39.5 %copy-start.27 = (bf16[1024]{0:T(1024)(128)(2,1)S(1)}, bf16[1024]{0:T(1024)(128)(2,1)}, u32[]{:S(2)}) copy-start(bf16[1024]{0:T(1024)(128)(2,1)} %get-tuple-element.9) | copy-start | bytes 6148
Sparse Core Ops, SparseCore 0:
  9.7 27.9 all-gather.10
  39.2 29.5 all-gather.16
  70.5 28.3 all-gather.20
  100.6 69.6 all-gather.12
  172.0 35.1 all-gather.14
  208.9 87.6 all-gather.18
  298.4 87.4 all-gather.22
  466.8 35.1 reduce-scatter.12
  547.7 70.2 reduce-scatter.10
  621.2 86.3 reduce-scatter.20
  711.2 86.3 reduce-scatter.16
  799.8 30.9 reduce-scatter.14
  833.1 32.4 reduce-scatter.24
  867.7 33.6 reduce-scatter.22
  903.5 34.3 reduce-scatter.18
where the time goes:
time: 975 us; the launch traced here: 964 us
  waiting for transfers between devices  245 us (25%)
  matrix products  226 us (23%)
  local copies, waits for them, and re-layouts  221 us (23%)
  other arithmetic  176 us (18%)
  blocking collectives  78.4 us (8%)
  between operations  16.9 us (2%)
    reduce_scatter x1, waiting for transfers between devices, local(): lax.psum_scatter(down_part.astype(jnp.bfloat16), 'row', scatter_dimension...  86.9 us
    unnamed x86, local copies, waits for them, and re-layouts  70.9 us
    reduce_scatter x1, waiting for transfers between devices, local(): lax.psum_scatter(up_part.astype(jnp.bfloat16), 'row', scatter_dimension=0...  60.6 us
    scatter-add x1, other arithmetic, local(): input_grad = grad_out.at[token_rows].add(grad_picked)  39.5 us
    scatter-add x1, other arithmetic, local(): output = tokens.astype(jnp.float32).at[token_rows].add(gate_value[:, None...  39.4 us
    unnamed x3, blocking collectives  38.8 us
    slice x1, local copies, waits for them, and re-layouts, local(): values = heads_qkv[:, :, :, 2]  35.7 us
    reshape x1, local copies, waits for them, and re-layouts, local(): heads_qkv = projected.reshape(seq_local, routed, HEADS, 3, HD)  30.3 us
  transfers between devices with their start and end apart: 15, of which 6 were waited for; matrix products, arithmetic and copies ran while one was open for 55% of the time, Pallas kernels for 0%

commit v1 on v0

v1 whole, which is shorter than its diff:
```python
import functools
import math

import jax
import jax.numpy as jnp
from jax import lax
from jax.experimental import pallas as pl
from jax.experimental.pallas import tpu as pltpu
from jax.sharding import PartitionSpec as P

HEADS = 16
HD = 64
EPSILON = 1e-06
F32 = jnp.float32
BF16 = jnp.bfloat16
BOTH = ("row", "col")
SLOW = 1

NN = (((1,), (0,)), ((), ()))
NT = (((1,), (1,)), ((), ()))
TN = (((0,), (0,)), ((), ()))


def mul(a, b, dims=NN):
    return lax.dot_general(a, b, dims, preferred_element_type=F32)


def call(
    body, name, grid, ins, outs, shapes, scratch=(), prefetch=0, flops=0, nbytes=0, deps=(), alias=None
):
    count = prefetch + len(ins)

    def run(*refs):
        body(*refs[:count], *refs[count + len(deps) :])

    made = pl.pallas_call(
        run,
        name=name,
        grid_spec=pltpu.PrefetchScalarGridSpec(
            num_scalar_prefetch=prefetch,
            grid=grid,
            in_specs=ins + [pl.BlockSpec(memory_space=pl.ANY)] * len(deps),
            out_specs=outs,
            scratch_shapes=list(scratch),
        ),
        out_shape=shapes,
        input_output_aliases=alias or {},
        compiler_params=pltpu.CompilerParams(
            dimension_semantics=("arbitrary",) * len(grid),
            vmem_limit_bytes=56 * 1024 * 1024,
        ),
        cost_estimate=pl.CostEstimate(
            flops=flops // SLOW, transcendentals=0, bytes_accessed=nbytes // SLOW
        ),
    )
    return lambda *args: made(*args, *deps)


def tied(value, *deps):
    return call(
        lambda given, out: None,
        "tied",
        (1,),
        [pl.BlockSpec(memory_space=pl.ANY)],
        pl.BlockSpec(memory_space=pl.ANY),
        shaped(value.shape, value.dtype),
        deps=deps,
        alias={0: 0},
    )(value)


def whole(shape):
    return pl.BlockSpec(shape, lambda *_: (0,) * len(shape))


def shaped(shape, dtype):
    return jax.ShapeDtypeStruct(shape, dtype)


def one_hot(index_ref, length):
    places = lax.broadcasted_iota(jnp.int32, (length, index_ref.shape[-1]), 0)
    return places == index_ref[0]


def pick_body(index, tok, cot, gain, router, picked, grows, normed, gmlp, gate, base):
    hot = jnp.where(one_hot(index, tok.shape[0]), 1.0, 0.0).astype(BF16)
    rows = mul(hot, tok[...], TN)
    back = mul(hot, cot[...], TN)
    opened = jax.nn.sigmoid(jnp.sum(rows * router[...], axis=-1, keepdims=True))
    inverse = lax.rsqrt(jnp.mean(rows * rows, axis=-1, keepdims=True) + EPSILON)
    picked[...] = rows.astype(BF16)
    grows[...] = back.astype(BF16)
    normed[...] = (rows * inverse * gain[...]).astype(BF16)
    gmlp[...] = (back * opened).astype(BF16)
    gate[...] = opened
    base[...] = cot[...].astype(F32)


def pick(tokens, cotangent, index, gain, router, deps=()):
    seqs, _, routed = index.shape
    length, width = tokens.shape[0] // seqs, tokens.shape[1]
    rows = seqs * routed
    whole_seq = pl.BlockSpec((length, width), lambda s: (s, 0))
    part = pl.BlockSpec((routed, width), lambda s: (s, 0))
    return call(
        pick_body,
        "pick",
        (seqs,),
        [pl.BlockSpec((1, 1, routed), lambda s: (s, 0, 0)), whole_seq, whole_seq]
        + [whole((1, width))] * 2,
        [part] * 4 + [pl.BlockSpec((routed, 1), lambda s: (s, 0)), whole_seq],
        [shaped((rows, width), BF16)] * 4 + [shaped((rows, 1), F32), shaped(tokens.shape, F32)],
        flops=4 * rows * length * width,
        nbytes=4 * tokens.size + 8 * rows * width,
        deps=deps,
    )(index, tokens, cotangent, gain, router)


def lay_rc(w, buf, kb):
    rs, cs, tall, wp = w.shape
    pieces = tall // kb
    for r in range(rs):
        for c in range(cs):
            for t in range(pieces):
                at = (c * pieces + t) * wp
                buf[r * kb : (r + 1) * kb, at : at + wp] = w[r, c, t * kb : (t + 1) * kb, :]


def lay_cr(w, buf, kb):
    rs, cs, tall, wp = w.shape
    pieces = tall // kb
    for r in range(rs):
        for c in range(cs):
            for t in range(pieces):
                at = (r * pieces + t) * wp
                buf[c * kb : (c + 1) * kb, at : at + wp] = w[r, c, t * kb : (t + 1) * kb, :]


def lay_turned(spots, own, other, place, rs, zs):
    bit = spots[2, 0]
    for core in range(2):

        @pl.when(bit == core)
        def _():
            for r in range(rs):
                for z in range(zs):
                    place(r, z, core, own)
                    place(r, z, 1 - core, other)


def project_body(kb, wp, count, spots, x, own_a, own_b, other_a, other_b, out, natural):
    rs = own_a.shape[0]
    tall = own_a.shape[2]

    def place(r, z, core, halves_of):
        size = kb // 2
        for t in range(2 * count):
            half, at = divmod(t * size, tall)
            value = halves_of[half][spots[half, r], 0, at : at + size, :]
            lane = (core * count + t // 2) * wp
            down = r * kb + t % 2 * size
            natural[down : down + size, lane : lane + wp] = value

    lay_turned(spots, (own_a, own_b), (other_a, other_b), place, rs, 1)
    out[...] = mul(x[...], natural[...]).astype(BF16)


def project(spots, x, parts, kb, count):
    rows, depth = x.shape
    rs, zs, tall, wp = parts[0].shape
    step = 2 * count * wp
    piece = pl.BlockSpec((rs, 1, tall, wp), lambda j, spots: (0, spots[3, j], 0, 0))
    return call(
        functools.partial(project_body, kb, wp, count),
        "project",
        (zs,),
        [pl.BlockSpec(x.shape, lambda j, _: (0, 0))] + [piece] * 4,
        [
            pl.BlockSpec((rows, step), lambda j, _: (0, j)),
            pl.BlockSpec((depth, step), lambda j, _: (0, j)),
        ],
        [shaped((rows, zs * step), BF16), shaped((depth, zs * step), BF16)],
        prefetch=1,
        flops=2 * rows * depth * zs * step,
        nbytes=2 * (x.size + 2 * depth * zs * step + rows * zs * step),
    )(spots, x, *parts)


def halves():
    lane = lax.broadcasted_iota(jnp.int32, (1, 2 * HD), 1)
    low = jnp.where(lane < HD, 1.0, 0.0).astype(BF16)
    high = jnp.where(lane < HD, 0.0, 1.0).astype(BF16)
    return low, high


def turned(x):
    return jnp.concatenate([x[:, HD:], x[:, :HD]], axis=1) * jnp.asarray(HD**-0.5, BF16)


def softmax(scores, causal):
    scores = jnp.where(causal, scores, -1e30)
    expanded = jnp.exp(scores - jnp.max(scores, axis=0, keepdims=True))
    return (expanded * (1.0 / jnp.sum(expanded, axis=0, keepdims=True))).astype(BF16)


def causal_of(routed):
    return lax.broadcasted_iota(jnp.int32, (routed, routed), 0) <= lax.broadcasted_iota(
        jnp.int32, (routed, routed), 1
    )


def attend_body(proj, context, probs):
    routed = proj.shape[0]
    low, high = halves()
    causal = causal_of(routed)
    for pair in range(HEADS // 2):
        a, b, c = (proj[:, (3 * pair + t) * 2 * HD : (3 * pair + t + 1) * 2 * HD] for t in range(3))
        first = softmax(mul(turned(a) * low, a, NT), causal)
        second = softmax(mul(turned(c) * high, b, NT), causal)
        both = jnp.concatenate([first, second], axis=0)
        probs[0, 2 * pair * routed : 2 * (pair + 1) * routed, :] = both
        mixed = mul(both, jnp.concatenate([b * low, c * high], axis=0), TN)
        context[:, pair * 2 * HD : (pair + 1) * 2 * HD] = mixed.astype(BF16)


def attend(projected, seqs):
    rows, wide = projected.shape
    routed = rows // seqs
    width = wide // 3
    return call(
        attend_body,
        "attend",
        (seqs,),
        [pl.BlockSpec((routed, wide), lambda s: (s, 0))],
        [
            pl.BlockSpec((routed, width), lambda s: (s, 0)),
            pl.BlockSpec((1, HEADS * routed, routed), lambda s: (s, 0, 0)),
        ],
        [shaped((rows, width), BF16), shaped((seqs, HEADS * routed, routed), BF16)],
        flops=20 * rows * wide * routed,
        nbytes=8 * projected.size,
    )(projected)


def mix_body(kb, context, w, picked, gain, attn, normed, natural):
    @pl.when(pl.program_id(0) == 0)
    def _():
        lay_cr(w, natural, kb)

    out = mul(context[...], natural[...])
    attn[...] = out
    middle = picked[...].astype(F32) + out
    inverse = lax.rsqrt(jnp.mean(middle * middle, axis=-1, keepdims=True) + EPSILON)
    normed[...] = (middle * inverse * gain[...]).astype(BF16)


def mix(context, w, at, tall, kb, picked, gain, steps):
    rows, width = context.shape
    rs, cs, _, wp = w.shape
    part = pl.BlockSpec((rows // steps, width), lambda s: (s, 0))
    return call(
        functools.partial(mix_body, kb),
        "mix",
        (steps,),
        [part, pl.BlockSpec((rs, cs, tall, wp), lambda s: (0, 0, at, 0)), part, whole(gain.shape)],
        [part, part, whole((width, width))],
        [shaped((rows, width), F32), shaped((rows, width), BF16), shaped((width, width), BF16)],
        flops=2 * rows * width * width,
        nbytes=14 * rows * width,
    )(context, w, picked, gain)


GELU_A = 0.7978845608028654
GELU_B = 0.044715


def raise_body(kb, x, w, hidden, slope, natural):
    lay_rc(w, natural, kb)
    rows, step = hidden.shape
    tall, tile = rows // 3, 256
    for n in range(step // tile):
        across = slice(n * tile, (n + 1) * tile)
        for m in range(rows // tall):
            down = slice(m * tall, (m + 1) * tall)
            pre = mul(x[down, :], natural[:, across])
            square = pre * pre
            bent = jnp.tanh(pre * (GELU_A + (GELU_A * GELU_B) * square))
            half = 0.5 + 0.5 * bent
            hidden[down, across] = (pre * half).astype(BF16)
            slope[down, across] = (
                half
                + (0.5 * pre)
                * (1.0 - bent * bent)
                * (GELU_A + (3 * GELU_A * GELU_B) * square)
            ).astype(BF16)


def raised(x, w, at, tall, kb, count):
    rows, depth = x.shape
    rs, cs, _, wp = w.shape
    wide = cs * (tall // kb) * wp
    many = cs // count
    step = wide // count
    out = pl.BlockSpec((rows, step), lambda j: (0, j))
    return call(
        functools.partial(raise_body, kb),
        "raise",
        (count,),
        [whole(x.shape), pl.BlockSpec((rs, many, tall, wp), lambda j: (0, j, at, 0))],
        [out, out, pl.BlockSpec((depth, step), lambda j: (0, j))],
        [shaped((rows, wide), BF16)] * 2 + [shaped((depth, wide), BF16)],
        flops=3 * rows * depth * wide,
        nbytes=2 * (x.size + 2 * depth * wide + 2 * rows * wide),
    )(x, w)


def split_out(bit, first, second, keep, send, at):
    @pl.when(bit == 0)
    def _():
        keep[at] = first
        send[at] = second

    @pl.when(bit != 0)
    def _():
        keep[at] = second
        send[at] = first


def grad_rc(bit, total, send, keep, kb, nb):
    rs, zs, _, wp = send.shape
    for r in range(rs):
        for j in range(zs):
            for t in range(nb // wp):
                at = 2 * j * nb + t * wp
                down = slice(r * kb, (r + 1) * kb)
                where = (r, j, slice(t * kb, (t + 1) * kb))
                split_out(
                    bit, total[down, at : at + wp], total[down, at + nb : at + nb + wp], keep, send, where
                )


def grad_rc_body(kb, nb, bit, x, y, send, keep):
    grad_rc(bit[0], mul(x[...], y[...], TN).astype(BF16), send, keep, kb, nb)


def grad_cr(bit, total, send, keep, kb, nb):
    rs, zs, _, wp = send.shape
    for r in range(rs):
        for j in range(zs):
            for t in range(nb // wp):
                across = slice(r * nb + t * wp, r * nb + (t + 1) * wp)
                where = (r, j, slice(t * kb, (t + 1) * kb))
                at = 2 * j * kb
                split_out(
                    bit, total[at : at + kb, across], total[at + kb : at + 2 * kb, across], keep, send, where
                )


def grad_cr_body(kb, nb, bit, x, y, send, keep):
    grad_cr(bit[0], mul(x[...], y[...], TN).astype(BF16), send, keep, kb, nb)


def weight_grad(name, bit, x, y, shape, wp, by_row, count, deps=()):
    rows = x.shape[0]
    rs, cs, kb, nb = shape
    zs = cs // 2
    many = zs // count
    tall = kb * nb // wp
    cut = pl.BlockSpec((rows, 2 * many * (nb if by_row else kb)), lambda j, _: (0, j))
    out = pl.BlockSpec((rs, many, tall, wp), lambda j, _: (0, j, 0, 0))
    return call(
        functools.partial(grad_rc_body if by_row else grad_cr_body, kb, nb),
        name,
        (count,),
        [whole(x.shape), cut] if by_row else [cut, whole(y.shape)],
        [out, out],
        [shaped((rs, zs, tall, wp), BF16)] * 2,
        prefetch=1,
        flops=2 * rows * rs * cs * kb * nb,
        nbytes=2 * (x.size + y.size + rs * cs * kb * nb),
        deps=deps,
    )(bit, x, y)


def qkv_grad_body(kb, nb, bit, x, y, w, send, keep, first):
    total = mul(x[...], y[...], TN)

    @pl.when(pl.program_id(0) == 0)
    def _():
        first[...] = jnp.zeros_like(first)

    first[...] += jnp.sum(total * w[...].astype(F32), axis=-1, keepdims=True)
    grad_rc(bit[0], total.astype(BF16), send, keep, kb, nb)


def qkv_weight_grad(bit, x, y, w, shape, wp, count):
    rows, depth = x.shape
    rs, cs, kb, nb = shape
    zs = cs // 2
    many = zs // count
    tall = kb * nb // wp
    step = 2 * many * nb
    out = pl.BlockSpec((rs, many, tall, wp), lambda j, _: (0, j, 0, 0))
    return call(
        functools.partial(qkv_grad_body, kb, nb),
        "qkv_grad",
        (count,),
        [
            whole(x.shape),
            pl.BlockSpec((rows, step), lambda j, _: (0, j)),
            pl.BlockSpec((depth, step), lambda j, _: (0, j)),
        ],
        [out, out, whole((depth, 1))],
        [shaped((rs, zs, tall, wp), BF16)] * 2 + [shaped((depth, 1), F32)],
        prefetch=1,
        flops=2 * rows * depth * cs * nb,
        nbytes=2 * (x.size + y.size + 2 * w.size),
    )(bit, x, y, w)


def lower_body(hidden, w, attn, picked, gate, kept):
    branch = attn[...] + mul(hidden[...], w[...])
    kept[...] = (picked[...].astype(F32) + gate[...] * branch).astype(BF16)


def lowered(hidden, w, attn, picked, gate, step, deps=()):
    rows, deep = hidden.shape
    width = w.shape[1]
    cut = pl.BlockSpec((rows, step), lambda j: (0, j))
    return call(
        lower_body,
        "lower",
        (width // step,),
        [whole(hidden.shape), pl.BlockSpec((deep, step), lambda j: (0, j))]
        + [cut] * 2
        + [whole(gate.shape)],
        cut,
        shaped((rows, width), BF16),
        flops=2 * rows * deep * width,
        nbytes=2 * (hidden.size + w.size) + 8 * attn.size,
        deps=deps,
    )(hidden, w, attn, picked, gate)


def hidden_back_body(kb, grows, w, slope, hidden, gate, out, natural, dots):
    lay_cr(w, natural, kb)
    tile = 128

    @pl.when(pl.program_id(0) == 0)
    def _():
        dots[...] = jnp.zeros_like(dots)

    back = mul(grows[...], natural[...], NT)
    out[...] = (back * gate[...] * slope[...].astype(F32)).astype(BF16)
    product = back * hidden[...].astype(F32)
    summed = product[:, :tile]
    for n in range(1, product.shape[1] // tile):
        summed = summed + product[:, n * tile : (n + 1) * tile]
    dots[...] += summed


def hidden_back(grows, w, tall, kb, slope, hidden, gate, count, deps=()):
    rows, width = grows.shape
    rs, cs, _, wp = w.shape
    many = cs // count
    step = many * kb
    cut = pl.BlockSpec((rows, step), lambda j: (0, j))
    return call(
        functools.partial(hidden_back_body, kb),
        "hidden_back",
        (count,),
        [whole(grows.shape), pl.BlockSpec((rs, many, tall, wp), lambda j: (0, j, 0, 0)), cut, cut]
        + [whole(gate.shape)],
        [cut, pl.BlockSpec((step, width), lambda j: (j, 0)), whole((rows, 128))],
        [
            shaped((rows, cs * kb), BF16),
            shaped((cs * kb, width), BF16),
            shaped((rows, 128), F32),
        ],
        flops=2 * rows * width * cs * kb,
        nbytes=2 * (grows.size + 2 * cs * kb * width + 3 * slope.size),
        deps=deps,
    )(grows, w, slope, hidden, gate)


def norm_back(grad, v, inverse, gain):
    scaled = grad * gain
    summed = jnp.sum(scaled * v, axis=-1, keepdims=True)
    return inverse * scaled - v * (inverse * inverse * inverse * summed / v.shape[-1])


def middle_back_body(
    gpre, w, attn, picked, grows, gate, gain, dots, gmid, gattn, gsmall, logit, total
):
    j = pl.program_id(0)
    step = w.shape[0]
    for i in range(total.shape[1] // step):

        @pl.when(j == i)
        def _():
            total[:, i * step : (i + 1) * step] = mul(gpre[...], w[...], NT)

    @pl.when(j == pl.num_programs(0) - 1)
    def _():
        summed = jnp.zeros_like(gain)
        routing = jnp.zeros_like(gain)
        chunk = 128
        for i in range(total.shape[0] // chunk):
            at = slice(i * chunk, (i + 1) * chunk)
            grad = total[at, :]
            rows = picked[at, :].astype(F32)
            middle = rows + attn[at, :]
            inverse = lax.rsqrt(jnp.mean(middle * middle, axis=-1, keepdims=True) + EPSILON)
            summed += jnp.sum(grad * middle * inverse, axis=0, keepdims=True)
            back = norm_back(grad, middle, inverse, gain[...])
            gmid[at, :] = back
            opened, dy = gate[at, :], grows[at, :].astype(F32)
            gattn[at, :] = (opened * dy + back).astype(BF16)
            opening = jnp.sum(dots[at, :], axis=-1, keepdims=True)
            opening += jnp.sum(dy * attn[at, :], axis=-1, keepdims=True)
            opening = opening * opened * (1.0 - opened)
            logit[at, :] = opening
            routing += jnp.sum(opening * rows, axis=0, keepdims=True)
        gsmall[0:1, :] = summed
        gsmall[1:2, :] = routing


def middle_back(gpre, w, attn, picked, grows, gate, gain, dots, step, deps=()):
    rows, deep = gpre.shape
    width = attn.shape[1]
    return call(
        middle_back_body,
        "middle_back",
        (width // step,),
        [whole(gpre.shape), pl.BlockSpec((step, deep), lambda j: (j, 0))]
        + [whole(t.shape) for t in (attn, picked, grows, gate, gain, dots)],
        [whole(attn.shape), whole(attn.shape), whole((2, width)), whole(gate.shape)],
        [
            shaped(attn.shape, F32),
            shaped(attn.shape, BF16),
            shaped((2, width), F32),
            shaped(gate.shape, F32),
        ],
        [pltpu.VMEM((rows, width), F32)],
        flops=2 * rows * deep * width,
        nbytes=2 * (gpre.size + w.size) + 14 * attn.size,
        deps=deps,
    )(gpre, w, attn, picked, grows, gate, gain, dots)


def context_back_body(kb, nb, bit, gattn, w, context, gcontext, send, keep):
    gcontext[...] = mul(gattn[...], w[...], NT).astype(BF16)
    grad_cr_body(kb, nb, bit, context, gattn, send, keep)


def context_back(bit, gattn, w, context, shape, wp):
    rows, width = gattn.shape
    rs, cs, kb, nb = shape
    half = (rs, cs // 2, kb * nb // wp, wp)
    return call(
        functools.partial(context_back_body, kb, nb),
        "context_back",
        (1,),
        [whole(gattn.shape), whole(w.shape), whole(context.shape)],
        [whole(context.shape), whole(half), whole(half)],
        [shaped(context.shape, BF16), shaped(half, BF16), shaped(half, BF16)],
        prefetch=1,
        flops=4 * rows * width * width,
        nbytes=6 * rows * width + 4 * width * width,
    )(bit, gattn, w, context)


def attend_back_body(proj, gcontext, probs, out):
    routed = proj.shape[0]
    low, high = halves()

    def scores_back(grad_probs, weights):
        weights = weights.astype(F32)
        inner = jnp.sum(grad_probs * weights, axis=0, keepdims=True)
        return (weights * (grad_probs - inner)).astype(BF16)

    for pair in range(HEADS // 2):
        at = [slice((3 * pair + t) * 2 * HD, (3 * pair + t + 1) * 2 * HD) for t in range(3)]
        a, b, c = (proj[:, cut] for cut in at)
        grad = gcontext[:, pair * 2 * HD : (pair + 1) * 2 * HD]
        grad_low, grad_high = grad * low, grad * high
        a_turned, b_turned, c_turned = turned(a), turned(b), turned(c)
        first = probs[0, 2 * pair * routed : (2 * pair + 1) * routed, :]
        second = probs[0, (2 * pair + 1) * routed : 2 * (pair + 1) * routed, :]
        back_first = scores_back(mul(b, grad_low, NT), first)
        back_second = scores_back(mul(c, grad_high, NT), second)
        out[:, at[0]] = (
            mul(back_first, a_turned * low, TN) + mul(back_first, a_turned * high)
        ).astype(BF16)
        out[:, at[1]] = (
            mul(first, grad_low) + mul(back_second, c_turned * high, TN)
        ).astype(BF16)
        out[:, at[2]] = (mul(back_second, b_turned * low) + mul(second, grad_high)).astype(BF16)


def attend_back(projected, gcontext, probs, seqs, deps=()):
    rows, wide = projected.shape
    routed = rows // seqs
    return call(
        attend_back_body,
        "attend_back",
        (seqs,),
        [
            pl.BlockSpec((routed, wide), lambda s: (s, 0)),
            pl.BlockSpec((routed, wide // 3), lambda s: (s, 0)),
            pl.BlockSpec((1, HEADS * routed, routed), lambda s: (s, 0, 0)),
        ],
        pl.BlockSpec((routed, wide), lambda s: (s, 0)),
        shaped((rows, wide), BF16),
        flops=40 * rows * wide * routed,
        nbytes=16 * projected.size,
        deps=deps,
    )(projected, gcontext, probs)


def picked_back_body(
    places, gproj, w, picked, gmid, logit, grows, gain, router, base, out, total, arrived
):
    j = pl.program_id(0)
    step = w.shape[0]
    for i in range(total.shape[1] // step):

        @pl.when(j == i)
        def _():
            total[:, i * step : (i + 1) * step] = mul(gproj[...], w[...], NT)

    @pl.when(j == pl.num_programs(0) - 1)
    def _():
        chunk = 128
        for i in range(total.shape[0] // chunk):
            at = slice(i * chunk, (i + 1) * chunk)
            grad = total[at, :]
            rows = picked[at, :].astype(F32)
            inverse = lax.rsqrt(jnp.mean(rows * rows, axis=-1, keepdims=True) + EPSILON)
            back = norm_back(grad, rows, inverse, gain[...])
            total[at, :] = (
                gmid[at, :] + back + (logit[at, :] * router[...] + grows[at, :].astype(F32))
            )

            def send(k, carry):
                pltpu.make_async_copy(
                    total.at[pl.ds(k, 1)], out.at[pl.ds(places[k], 1)], arrived
                ).start()
                return carry

            lax.fori_loop(i * chunk, (i + 1) * chunk, send, 0, unroll=8)
        pltpu.make_async_copy(total, out.at[pl.ds(0, total.shape[0])], arrived).wait()


def picked_back(places, gproj, w, picked, gmid, logit, grows, gain, router, base, step, deps=()):
    rows, deep = gproj.shape
    width = picked.shape[1]
    return call(
        picked_back_body,
        "picked_back",
        (width // step,),
        [whole(gproj.shape), pl.BlockSpec((step, deep), lambda j, _: (j, 0))]
        + [whole(t.shape) for t in (picked, gmid, logit, grows, gain, router)]
        + [pl.BlockSpec(memory_space=pl.ANY)],
        pl.BlockSpec(memory_space=pl.ANY),
        shaped(base.shape, F32),
        [pltpu.VMEM((rows, width), F32), pltpu.SemaphoreType.DMA],
        prefetch=1,
        flops=2 * rows * deep * width,
        nbytes=2 * (gproj.size + w.size) + 10 * picked.size,
        alias={9: 0},
        deps=deps,
    )(places, gproj, w, picked, gmid, logit, grows, gain, router, base)


def join_body(count, *refs):
    out, at = refs[-1], 0
    for keep, got in zip(refs[:count], refs[count : 2 * count]):
        tall = keep.shape[2]
        out[:, :, at : at + tall] = (keep[...].astype(F32) + got[...].astype(F32)).astype(BF16)
        at += tall


def joined(keeps, gots, deps=()):
    rs, zs, _, wp = keeps[0].shape
    talls = [k.shape[2] for k in keeps]
    blocks = [pl.BlockSpec((1, zs, tall, wp), lambda r: (r, 0, 0, 0)) for tall in talls]
    tall = sum(talls)
    return call(
        functools.partial(join_body, len(keeps)),
        "join",
        (rs,),
        blocks * 2,
        pl.BlockSpec((1, zs, tall, wp), lambda r: (r, 0, 0, 0)),
        shaped((rs, zs, tall, wp), BF16),
        flops=rs * zs * tall * wp,
        nbytes=6 * rs * zs * tall * wp,
        deps=deps,
    )(*keeps, *gots)


def place_body(index, tok, kept, output):
    found = one_hot(index, tok.shape[0])
    hot = jnp.where(found, 1.0, 0.0)
    routed = jnp.sum(hot, axis=-1, keepdims=True) > 0.5
    output[...] = jnp.where(
        routed, mul(hot.astype(BF16), kept[...]), tok[...].astype(F32)
    ).astype(BF16)


def place(tokens, index, kept, deps=()):
    seqs, _, routed = index.shape
    length, width = tokens.shape[0] // seqs, tokens.shape[1]
    whole_seq = pl.BlockSpec((length, width), lambda s: (s, 0))
    return call(
        place_body,
        "place",
        (seqs,),
        [
            pl.BlockSpec((1, 1, routed), lambda s: (s, 0, 0)),
            whole_seq,
            pl.BlockSpec((routed, width), lambda s: (s, 0)),
        ],
        whole_seq,
        shaped(tokens.shape, BF16),
        flops=2 * seqs * routed * length * width,
        nbytes=4 * tokens.size,
        deps=deps,
    )(index, tokens, kept)


def pieces(block, wp):
    return [block[:, i : i + wp] for i in range(0, block.shape[1], wp)]


def gathered(flat, rs, cs):
    return lax.all_gather(flat, BOTH, axis=0, tiled=True).reshape(rs, cs, *flat.shape)


def shifted(value, part, shift, rs, cs):
    side = math.isqrt(rs)
    if part == "x":
        moves = [(r, r // side * side + (r + shift) % side) for r in range(rs)]
    elif part == "y":
        moves = [(r, (r + shift * side) % rs) for r in range(rs)]
    else:
        moves = [(c, (c + 2 * shift) % cs) for c in range(cs)]
    return lax.ppermute(value, "col" if part == "z" else "row", moves)


def permuted(flat, rs, cs, early, beside):
    side, zs = math.isqrt(rs), cs // 2
    line = [flat] + [shifted(flat, "z", i, rs, cs) for i in range(1, zs)]
    tall = flat.shape[0] // 2
    held = [jnp.stack([part[h * tall : (h + 1) * tall] for part in line])[None] for h in range(2)]
    held[0] = tied(held[0], early)
    held = [
        jnp.concatenate([h] + [shifted(h, part, i, rs, cs) for i in range(1, side)])
        for h, part in zip(held, "xy")
    ]
    moved = [
        [shifted(h, part, i, rs, cs) for i in range(1, side)] for h, part in zip(held, "yx")
    ]
    extra = beside(held[1])
    held = [jnp.concatenate([tied(h, extra[0])] + m) for h, m in zip(held, moved)]
    pairs = [(c, c ^ 1) for c in range(cs)]
    return held + [lax.ppermute(h, "col", pairs) for h in held], extra


def spots_of(rs, cs):
    side, zs = math.isqrt(rs), cs // 2
    row, column = lax.axis_index("row"), lax.axis_index("col")
    r, z = jnp.arange(rs), jnp.arange(zs)
    y, x = (row // side - r // side) % side, (row - r) % side
    table = jnp.zeros((4, max(rs, zs)), jnp.int32)
    table = table.at[0, :rs].set(y * side + x).at[1, :rs].set(x * side + y)
    return table.at[2, :].set(column % 2).at[3, :zs].set((column // 2 - z) % zs)


def after(value, *others):
    return lax.optimization_barrier((value, *others))[0]


def local(
    tokens,
    router_weight,
    norm_first,
    qkv_weight,
    out_weight,
    norm_second,
    up_weight,
    down_weight,
    route_index,
    out_cotangent,
    rs,
    cs,
):
    seqs, routed = route_index.shape
    width = tokens.shape[1]
    index = route_index.reshape(seqs, 1, routed)
    column = lax.axis_index("col")
    core, depth = column % 2, column // 2
    zs = cs // 2
    bit = core.astype(jnp.int32).reshape(1)
    pairs = [(c, c ^ 1) for c in range(cs)]
    blocks = [w.shape for w in (qkv_weight, out_weight, up_weight, down_weight)]
    shape_qkv, shape_out, shape_up, shape_down = ((rs, cs) + b for b in blocks)
    wp = math.gcd(128, *(b[1] for b in blocks))
    tall_qkv, tall_out, tall_up, tall_down = (b[0] * b[1] // wp for b in blocks)

    spots = spots_of(rs, cs)
    small = jnp.stack([router_weight, norm_first, norm_second])
    small = lax.all_gather(lax.all_gather(small, "col", axis=0), "row", axis=0)
    small = small.reshape(rs * cs, 3, -1).transpose(1, 0, 2).reshape(3, 1, width).astype(F32)
    router, first_gain, second_gain = small[0], small[1], small[2]
    parts, (picked, grows, normed, gmlp, gate, base) = permuted(
        jnp.concatenate(pieces(qkv_weight, wp)),
        rs,
        cs,
        small,
        lambda dep: pick(tokens, out_cotangent, index, first_gain, router, deps=(dep,)),
    )
    next_parts = gathered(jnp.concatenate(pieces(up_weight, wp) + pieces(out_weight, wp)), rs, cs)
    down_parts = gathered(jnp.concatenate(pieces(down_weight, wp)), rs, cs)

    def exchanged(send):
        return lax.ppermute(send, "col", pairs)

    def by_row(keep):
        r, z, tall, _ = keep.shape
        mine = lax.psum_scatter(
            keep.reshape(r * z * tall, wp), "row", scatter_dimension=0, tiled=True
        )
        return mine.reshape(z, tall, wp)

    def by_depth(mine):
        total = lax.dynamic_index_in_dim(mine, depth, 0, keepdims=False).astype(F32)
        for shift in range(1, zs):
            part = lax.dynamic_index_in_dim(mine, (depth + shift) % zs, 0, keepdims=False)
            total = total + shifted(part, "z", shift, rs, cs).astype(F32)
        return total

    def block(total, shape):
        kb, nb = shape[2:]
        return jnp.concatenate([total[i : i + kb] for i in range(0, kb * nb // wp, kb)], axis=1)

    projected, w_qkv = project(spots, normed, parts, blocks[0][0], blocks[0][1] // wp)
    context, probs = attend(projected, seqs)
    attn, normed_mid, w_out = mix(
        context, next_parts, tall_up // tall_out, tall_out, blocks[1][0], picked, second_gain, 3
    )
    hidden, slope, w_up = raised(normed_mid, next_parts, 0, tall_up, blocks[2][0], 4)

    down_send, down_keep = weight_grad("down_grad", bit, hidden, gmlp, shape_down, wp, False, 4)
    gpre, w_down, dots = hidden_back(
        grows, down_parts, tall_down, blocks[3][0], slope, hidden, gate, 4, deps=(down_send,)
    )
    down_keep = joined([down_keep], [exchanged(down_send)], deps=(gpre,))
    down_rows = by_row(down_keep)

    up_send, up_keep = weight_grad(
        "up_grad", bit, normed_mid, gpre, shape_up, wp, True, 4, deps=(down_keep,)
    )
    gmid, gattn, gsmall, logit = middle_back(
        gpre, w_up, attn, picked, grows, gate, second_gain, dots, 256, deps=(up_send,)
    )
    up_keep = joined([up_keep], [exchanged(up_send)], deps=(gattn,))
    up_rows = by_row(up_keep)
    gattn = tied(gattn, up_keep)
    gcontext, out_send, out_keep = context_back(bit, gattn, w_out, context, shape_out, wp)

    gproj = attend_back(projected, gcontext, probs, seqs, deps=(up_keep,))
    qkv_send, qkv_keep, gfirst = qkv_weight_grad(bit, normed, gproj, w_qkv, shape_qkv, wp, 4)
    little = jnp.concatenate([gsmall, (gfirst / first_gain.reshape(width, 1)).reshape(1, width)])
    little = little.reshape(3, rs, zs, 2, -1).transpose(1, 2, 3, 0, 4)
    little = little.reshape(rs, zs, 2, -1).astype(BF16)
    lines = -(-little.shape[-1] // wp)
    little = jnp.pad(little, ((0, 0),) * 3 + ((0, lines * wp - little.shape[-1]),))
    little = jnp.pad(little.reshape(rs, zs, 2, lines, wp), ((0, 0),) * 3 + ((0, 16 - lines), (0, 0)))
    little_keep = lax.dynamic_index_in_dim(little, core, 2, keepdims=False)
    little_send = lax.dynamic_index_in_dim(little, 1 - core, 2, keepdims=False)
    qkv_keep = joined(
        [qkv_keep, out_keep, little_keep],
        [exchanged(qkv_send), exchanged(out_send), exchanged(little_send)],
    )
    qkv_rows = by_row(qkv_keep)

    kept = lowered(hidden, w_down, attn, picked, gate, 256, deps=(qkv_keep, down_rows))
    down_grad = block(by_depth(down_rows), shape_down)
    starts = jnp.arange(seqs, dtype=jnp.int32) * (tokens.shape[0] // seqs)
    places = (route_index + starts[:, None]).reshape(-1)
    input_grad = picked_back(
        places, gproj, w_qkv, picked, gmid, logit, grows, first_gain, router, base, 256,
        deps=(kept, up_rows),
    )
    up_total = by_depth(up_rows)
    output = place(tokens, index, kept, deps=(input_grad, up_total))
    qkv_total = by_depth(qkv_rows)
    up_grad = block(up_total, shape_up)
    out_grad = block(qkv_total[tall_qkv : tall_qkv + tall_out], shape_out)
    qkv_grad = block(qkv_total[:tall_qkv], shape_qkv)
    lowest = tall_qkv + tall_out
    sums = qkv_total[lowest : lowest + lines].reshape(-1)[: 3 * width // (rs * cs)].reshape(3, -1)
    return (
        output,
        input_grad,
        sums[1],
        sums[2],
        qkv_grad,
        out_grad,
        sums[0],
        up_grad,
        down_grad,
    )


def solution(mesh):
    both, by_row, by_col = P(BOTH), P("row", "col"), P("col", "row")
    tall = P(BOTH, None)
    return jax.shard_map(
        functools.partial(local, rs=mesh.shape["row"], cs=mesh.shape["col"]),
        mesh=mesh,
        in_specs=(tall, both, both, by_row, by_col, both, by_row, by_col, tall, tall),
        out_specs=(tall, tall, both, both, by_row, by_col, both, by_row, by_col),
        check_vma=False,
    )
```

time: 975 us -> 450 us (0.46)
  Pallas kernels: 0 us -> 314 us
  matrix products: 226 us -> 0 us
  waiting for transfers between devices: 245 us -> 19.7 us
  local copies, waits for them, and re-layouts: 221 us -> 22.6 us
  other arithmetic: 176 us -> 16.4 us
  blocking collectives: 78.4 us -> 28.5 us
  starting transfers between devices: 0.81 us -> 29.6 us
    pallas_call x0 -> x22, Pallas kernels: none -> 314 us  [call(): return lambda *args: made(*args, *deps)]
    dot_general x19 -> x0, matrix products: 226 us -> none  [the longest x1 28.3 us: local(): jnp.dot(grad_mlp, w_down.T, preferred_element_type=jnp.float32)]
    reduce_scatter x7 -> x3, waiting for transfers between devices: 177 us -> 0.02 us  [by_row(): lax.psum_scatter(keep.reshape(r * z * tall, wp), 'row', scatter_dimension...]
    convert_element_type x14 -> x2, other arithmetic: 85.5 us -> 0.06 us  [the longest x1 0.05 us: local(): little = little.reshape(rs, zs, 2, -1).astype(BF16)]
    scatter-add x2 -> x0, other arithmetic: 78.9 us -> none  [the longest x1 39.5 us: local(): input_grad = grad_out.at[token_rows].add(grad_picked)]
    all_gather x7 -> x2, waiting for transfers between devices: 64.9 us -> 0.32 us  [gathered(): lax.all_gather(flat, BOTH, axis=0, tiled=True).reshape(rs, cs, *flat.shape)]
    unnamed x86 -> x29, local copies, waits for them, and re-layouts: 70.9 us -> 9.48 us
    reshape x3 -> x2, local copies, waits for them, and re-layouts: 44.9 us -> 0.61 us  [the longest x1 0.59 us: local(): index = route_index.reshape(seqs, 1, routed)]
  transfers between devices with their start and end apart: 15 -> 28, of which waited for: 6 -> 6; matrix products, arithmetic and copies ran while one was open for 55% -> 5% of each run, Pallas kernels for 0% -> 69%
where the time goes in v1:
time: 450 us; the launch traced here: 445 us
  Pallas kernels  314 us (70%)
  starting transfers between devices  29.6 us (7%)
  blocking collectives  28.5 us (6%)
  local copies, waits for them, and re-layouts  22.6 us (5%)
  waiting for transfers between devices  19.7 us (4%)
  other arithmetic  16.4 us (4%)
  between operations  14.5 us (3%)
    pallas_call x22, Pallas kernels, call(): return lambda *args: made(*args, *deps)  314 us
    all_gather x2, blocking collectives, local(): small = lax.all_gather(lax.all_gather(small, 'col', axis=0), 'row', axis=0)  28.5 us
    ppermute x16, starting transfers between devices, shifted(): return lax.ppermute(value, 'col' if part == 'z' else 'row', moves)  28.2 us
    ppermute x16, waiting for transfers between devices, shifted(): return lax.ppermute(value, 'col' if part == 'z' else 'row', moves)  13.9 us
    unnamed x29, local copies, waits for them, and re-layouts  9.48 us
  transfers between devices with their start and end apart: 28, of which 6 were waited for; matrix products, arithmetic and copies ran while one was open for 5% of the time, Pallas kernels for 69%

profile of v1, /device:TPU:0, one launch (start us, length us, event | category | flops | bytes accessed | tf_op | source)
XLA Modules:
  0.0 445.2 jit_solution(12001759851823651124)
XLA Ops:
  15.7 3.1 collective-permute-start
  18.8 2.6 collective-permute-start.1
  21.4 1.3 collective-permute-start.2
  23.4 20.1 %all-gather.2 = bf16[8,3,32]{2,1,0:T(4,128)(2,1)S(1)} all-gather(bf16[1,3,32]{2,1,0:T(4,128)(2,1)S(1)} %maximum_bitcast_fusion.3), channel_id=2, replica_groups=mesh['row'=4,'col'=8] {'col'}, dimensions={0}, use_global_device_ids=true | all-gather | bytes 1728 | tf_op jit(solution)/shard_map/all_gather | solution.py:813
  43.5 8.4 %all-gather.1 = bf16[32,3,32]{2,0,1:T(8,128)(2,1)S(1)} all-gather(bf16[8,3,32]{2,0,1:T(8,128)(2,1)S(1)} %copy.32), channel_id=3, replica_groups=mesh['row'=4,'col'=8] {'row'}, dimensions={0}, use_global_device_ids=true | all-gather | bytes 7680 | tf_op jit(solution)/shard_map/all_gather | solution.py:813
  53.6 1.4 collective-permute-start.4
  55.7 13.9 %collective-permute-done.4 = bf16[1,4,384,128]{3,2,1,0:T(8,128)(2,1)S(1)} collective-permute-done((bf16[1,4,384,128]{3,2,1,0:T(8,128)(2,1)}, bf16[1,4,384,128]{3,2,1,0:T(8,128)(2,1)S(1)}, u32[]{:S(2)}, u32[]{:S(2)}) %collective-permute-start.4) | collective-permute-done | bytes 393248 | tf_op jit(solution)/shard_map/ppermute | solution.py:748
  70.7 1.5 collective-permute-start.5
  74.9 31.4 %pick.1 = (bf16[1152,1024]{1,0:T(8,128)(2,1)}, bf16[1152,1024]{1,0:T(8,128)(2,1)}, bf16[1152,1024]{1,0:T(8,128)(2,1)}, bf16[1152,1024]{1,0:T(8,128)(2,1)}, f32[1152,1]{1,0:T(8,128)}, /*index=5*/f32[9216,1024]{1,0:T(8,128)}) custom-call(s32[9,1,128]{2,1,0:T(1,128)} %reshape.305.refs_0_, bf16[9216,1024]{1,0:T(8,128)(2,1)} %refs_1_.3, ...), custom_call_target="tpu_custom_call" | custom-call | flops 4831838208 | bytes 47185920 | tf_op jit(solution)/shard_map/pick/pallas_call | solution.py:56
  107.2 1.5 pad_maximum_fusion.refs_2_
  108.8 2.9 pad_maximum_fusion.1.refs_3_
  112.8 2.7 collective-permute-done.8.refs_5_
  115.5 13.8 %project.1 = (bf16[1152,3072]{1,0:T(8,128)(2,1)}, bf16[1024,3072]{1,0:T(8,128)(2,1)}) custom-call(s32[4,4]{1,0:T(4,128)} %copy-done.11, bf16[1152,1024]{1,0:T(8,128)(2,1)} %get-tuple-element.90.refs_1_, bf16[4,4,384,128]{3,2,1,0:T(8,128)(2,1)} %copy-done.5, bf16[4,4,384,128]{3,2,1,0:T(8,128)(2,1)} %pad_maximum_fusion.1.refs_3_, ...), custom_call_target="tpu_custom_call" | custom-call | flops 7247757312 | bytes 22020096 | tf_op jit(solution)/shard_map/project/pallas_call | solution.py:56
  129.3 23.6 %attend.1 = (bf16[1152,1024]{1,0:T(8,128)(2,1)}, bf16[9,2048,128]{2,1,0:T(8,128)(2,1)}) custom-call(bf16[1152,3072]{1,0:T(8,128)(2,1)} %get-tuple-element.92.refs_0_), custom_call_target="tpu_custom_call" | custom-call | flops 9059696640 | bytes 28311552 | tf_op jit(solution)/shard_map/attend/pallas_call | solution.py:56
  152.9 8.7 %mix.1 = (f32[1152,1024]{1,0:T(8,128)}, bf16[1152,1024]{1,0:T(8,128)(2,1)}, bf16[1024,1024]{1,0:T(8,128)(2,1)}) custom-call(bf16[1152,1024]{1,0:T(8,128)(2,1)} %get-tuple-element.93.refs_0_.refs_3_, bf16[4,8,1280,128]{3,2,1,0:T(8,128)(2,1)} %bitcast.84, bf16[1152,1024]{1,0:T(8,128)(2,1)} %get-tuple-element.91.refs_1_.refs_2_.refs_3_, ...), custom_call_target="tpu_custom_call" | custom-call | flops 2415919104 | bytes 16515072 | tf_op jit(solution)/shard_map/mix/pallas_call | solution.py:56
  161.6 24.8 %raise.1 = (bf16[1152,4096]{1,0:T(8,128)(2,1)}, bf16[1152,4096]{1,0:T(8,128)(2,1)}, bf16[1024,4096]{1,0:T(8,128)(2,1)}) custom-call(bf16[1152,1024]{1,0:T(8,128)(2,1)} %get-tuple-element.94.refs_0_.refs_1_, bf16[4,8,1280,128]{3,2,1,0:T(8,128)(2,1)} %bitcast.85), custom_call_target="tpu_custom_call" | custom-call | flops 14495514624 | bytes 38010880 | tf_op jit(solution)/shard_map/raise/pallas_call | solution.py:56
  186.4 16.9 %down_grad.1 = (bf16[4,4,1024,128]{3,2,1,0:T(8,128)(2,1)}, bf16[4,4,1024,128]{3,2,1,0:T(8,128)(2,1)}) custom-call(s32[1]{0:T(128)} %bitcast.17.refs_0_, bf16[1152,4096]{1,0:T(8,128)(2,1)} %get-tuple-element.95.refs_1_.refs_3_.refs_0_, bf16[1152,1024]{1,0:T(8,128)(2,1)} %get-tuple-element.99.refs_2_), custom_call_target="tpu_custom_call" | custom-call | flops 9663676416 | bytes 20185088 | tf_op jit(solution)/shard_map/down_grad/pallas_call | solution.py:56
  203.7 21.4 %hidden_back.1 = (bf16[1152,4096]{1,0:T(8,128)(2,1)}, bf16[4096,1024]{1,0:T(8,128)(2,1)}, f32[1152,128]{1,0:T(8,128)}) custom-call(bf16[1152,1024]{1,0:T(8,128)(2,1)} %get-tuple-element.96.refs_0_.refs_4_.refs_6_, bf16[4,8,1024,128]{3,2,1,0:T(8,128)(2,1)} %bitcast.99, bf16[1152,4096]{1,0:T(8,128)(2,1)} %get-tuple-element.97.refs_2_, ...), custom_call_target="tpu_custom_call" | custom-call | flops 9663676416 | bytes 47448064 | tf_op jit(solution)/shard_map/hidden_back/pallas_call | solution.py:56
  225.1 6.0 %join.3.refs_3_ = bf16[4,4,1024,128]{3,2,1,0:T(8,128)(2,1)} custom-call(bf16[4,4,1024,128]{3,2,1,0:T(8,128)(2,1)} %get-tuple-element.106.refs_0_, bf16[4,4,1024,128]{3,2,1,0:T(8,128)(2,1)} %collective-permute-done.9.refs_1_, bf16[1152,4096]{1,0:T(8,128)(2,1)} %get-tuple-element.103.refs_2_.refs_0_), custom_call_target="tpu_custom_call" | custom-call | flops 2097152 | bytes 12582912 | tf_op jit(solution)/shard_map/join/pallas_call | solution.py:56
  231.2 17.0 %up_grad.1 = (bf16[4,4,1024,128]{3,2,1,0:T(8,128)(2,1)}, bf16[4,4,1024,128]{3,2,1,0:T(8,128)(2,1)}) custom-call(s32[1]{0:T(128)} %bitcast.17.refs_0_, bf16[1152,1024]{1,0:T(8,128)(2,1)} %get-tuple-element.94.refs_0_.refs_1_, bf16[1152,4096]{1,0:T(8,128)(2,1)} %get-tuple-element.103.refs_2_.refs_0_, bf16[4,4,1024,128]{3,2,1,0:T(8,128)(2,1)} %join.3.refs_3_), custom_call_target="tpu_custom_call" | custom-call | flops 9663676416 | bytes 20185088 | tf_op jit(solution)/shard_map/up_grad/pallas_call | solution.py:56
  248.4 25.1 %middle_back.1 = (f32[1152,1024]{1,0:T(8,128)}, bf16[1152,1024]{1,0:T(8,128)(2,1)}, f32[2,1024]{1,0:T(2,128)}, f32[1152,1]{1,0:T(8,128)}) custom-call(bf16[1152,4096]{1,0:T(8,128)(2,1)} %get-tuple-element.103.refs_2_.refs_0_, bf16[1024,4096]{1,0:T(8,128)(2,1)} %get-tuple-element.104.refs_1_, f32[1152,1024]{1,0:T(8,128)} %get-tuple-element.102.refs_2_, ...), custom_call_target="tpu_custom_call" | custom-call | flops 9663676416 | bytes 34340864 | tf_op jit(solution)/shard_map/middle_back/pallas_call | solution.py:56
  273.6 2.0 copy-done.3
  275.6 6.1 %join.4.refs_1_.refs_3_ = bf16[4,4,1024,128]{3,2,1,0:T(8,128)(2,1)} custom-call(bf16[4,4,1024,128]{3,2,1,0:T(8,128)(2,1)} %get-tuple-element.109.refs_0_, bf16[4,4,1024,128]{3,2,1,0:T(8,128)(2,1)} %copy-done.3, bf16[1152,1024]{1,0:T(8,128)(2,1)} %get-tuple-element.108.refs_2_.refs_0_), custom_call_target="tpu_custom_call" | custom-call | flops 2097152 | bytes 12582912 | tf_op jit(solution)/shard_map/join/pallas_call | solution.py:56
  281.8 11.0 %context_back.1 = (bf16[1152,1024]{1,0:T(8,128)(2,1)}, bf16[4,4,256,128]{3,2,1,0:T(8,128)(2,1)}, bf16[4,4,256,128]{3,2,1,0:T(8,128)(2,1)}) custom-call(s32[1]{0:T(128)} %bitcast.17.refs_0_, bf16[1152,1024]{1,0:T(8,128)(2,1)} %tied.7.refs_1_, bf16[1024,1024]{1,0:T(8,128)(2,1)} %get-tuple-element.110.refs_2_, bf16[1152,1024]{1,0:T(8,128)(2,1)} %get-tuple-element.93.refs_0_.refs_3_), custom_call_target="tpu_custom_call" | custom-call | flops 4831838208 | bytes 11272192 | tf_op jit(solution)/shard_map/context_back/pallas_call | solution.py:56
  292.8 24.1 %attend_back.1.refs_2_.refs_1_ = bf16[1152,3072]{1,0:T(8,128)(2,1)} custom-call(bf16[1152,3072]{1,0:T(8,128)(2,1)} %get-tuple-element.92.refs_0_, bf16[1152,1024]{1,0:T(8,128)(2,1)} %get-tuple-element.111.refs_1_, bf16[9,2048,128]{2,1,0:T(8,128)(2,1)} %get-tuple-element.112.refs_2_, bf16[4,4,1024,128]{3,2,1,0:T(8,128)(2,1)} %join.4.refs_1_.refs_3_), custom_call_target="tpu_custom_call" | custom-call | flops 18119393280 | bytes 56623104 | tf_op jit(solution)/shard_map/attend_back/pallas_call | solution.py:56
  316.9 15.7 %qkv_grad.1 = (bf16[4,4,768,128]{3,2,1,0:T(8,128)(2,1)}, bf16[4,4,768,128]{3,2,1,0:T(8,128)(2,1)}, f32[1024,1]{1,0:T(8,128)}) custom-call(s32[1]{0:T(128)} %bitcast.17.refs_0_, bf16[1152,1024]{1,0:T(8,128)(2,1)} %get-tuple-element.90.refs_1_, bf16[1152,3072]{1,0:T(8,128)(2,1)} %attend_back.1.refs_2_.refs_1_, ...), custom_call_target="tpu_custom_call" | custom-call | flops 7247757312 | bytes 22020096 | tf_op jit(solution)/shard_map/qkv_grad/pallas_call | solution.py:56
  333.2 1.3 reshape_squeeze.4
  334.6 1.4 fusion.6
  337.5 2.4 collective-permute-done.13.refs_5_
  340.5 1.3 copy-done.4
  341.8 6.0 %join.5.refs_5_ = bf16[4,4,1040,128]{3,2,1,0:T(8,128)(2,1)} custom-call(bf16[4,4,768,128]{3,2,1,0:T(8,128)(2,1)} %get-tuple-element.114.refs_0_, bf16[4,4,256,128]{3,2,1,0:T(8,128)(2,1)} %get-tuple-element.115.refs_1_, bf16[4,4,16,128]{3,2,1,0:T(8,128)(2,1)} %bitcast.94, bf16[4,4,768,128]{3,2,1,0:T(8,128)(2,1)} %copy-done.4, ...), custom_call_target="tpu_custom_call" | custom-call | flops 2129920 | bytes 12779520 | tf_op jit(solution)/shard_map/join/pallas_call | solution.py:56
  348.6 1.2 dynamic-slice_bitcast_fusion.5
  349.8 1.5 collective-permute-start.20
  351.3 2.3 collective-permute-start.21
  353.5 1.4 collective-permute-start.22
  354.9 17.3 %lower.1.refs_10_.refs_2_ = bf16[1152,1024]{1,0:T(8,128)(2,1)} custom-call(bf16[1152,4096]{1,0:T(8,128)(2,1)} %get-tuple-element.95.refs_1_.refs_3_.refs_0_, bf16[4096,1024]{1,0:T(8,128)(2,1)} %get-tuple-element.101.refs_1_, f32[1152,1024]{1,0:T(8,128)} %get-tuple-element.102.refs_2_, bf16[1152,1024]{1,0:T(8,128)(2,1)} %get-tuple-element.91.refs_1_.refs_2_.refs_3_, ...), custom_call_target="tpu_custom_call" | custom-call | flops 9663676416 | bytes 27262976 | tf_op jit(solution)/shard_map/lower/pallas_call | solution.py:56
  372.2 1.1 fusion.3
  374.2 1.2 dynamic-slice_bitcast_fusion.8
  375.3 5.5 %collective-permute-start.14 = (bf16[1024,128]{1,0:T(8,128)(2,1)S(1)}, bf16[1024,128]{1,0:T(8,128)(2,1)S(1)}, u32[]{:S(2)}, u32[]{:S(2)}) collective-permute-start(bf16[1024,128]{1,0:T(8,128)(2,1)S(1)} %get-tuple-element.129), channel_id=1, source_target_pairs={{0,2},{1,3},{2,4},{3,5},{4,6},{5,7},{6,0},{7,1},{8,10},{9,11},{10,... | collective-permute-start | bytes 786440 | tf_op jit(solution)/shard_map/ppermute | solution.py:748
  380.8 1.1 collective-permute-start.15
  381.9 1.4 collective-permute-start.16
  383.2 25.9 %picked_back.1.refs_3_ = f32[9216,1024]{1,0:T(8,128)} custom-call(s32[1152]{0:T(1024)} %add_bitcast_fusion.refs_0_, bf16[1152,3072]{1,0:T(8,128)(2,1)} %attend_back.1.refs_2_.refs_1_, bf16[1024,3072]{1,0:T(8,128)(2,1)} %get-tuple-element.113.refs_3_.refs_2_, ...), custom_call_target="tpu_custom_call", output_to_operand_aliasing={{}: (9, {})} | custom-call | flops 7247757312 | bytes 25165824 | tf_op jit(solution)/shard_map/picked_back/pallas_call | solution.py:56
  409.2 1.1 fusion.5.refs_4_
  410.3 1.3 dynamic-slice_bitcast_fusion.2
  412.4 1.9 collective-permute-start.18
  414.2 1.3 collective-permute-start.19
  416.3 18.9 %place.1 = bf16[9216,1024]{1,0:T(8,128)(2,1)} custom-call(s32[9,1,128]{2,1,0:T(1,128)} %reshape.305.refs_0_, bf16[9216,1024]{1,0:T(8,128)(2,1)} %refs_1_.3, bf16[1152,1024]{1,0:T(8,128)(2,1)} %lower.1.refs_10_.refs_2_, f32[9216,1024]{1,0:T(8,128)} %picked_back.1.refs_3_, f32[1024,128]{1,0:T(8,128)} %copy-done.2), custom_call_target="tpu_custom_call" | custom-call | flops 2415919104 | bytes 37748736 | tf_op jit(solution)/shard_map/place/pallas_call | solution.py:56
  435.2 1.1 fusion.1
  (126 shorter events, 26.0 us)
Async XLA Ops:
  7.2 145.7 %all-gather.6.cloned.1.call-start = ((), (), s32[]{:S(2)}) async-start(), calls=%async_computation.3 | async-start | bytes 10813440 | tf_op jit(solution)/shard_map/all_gather | solution.py:737
  12.2 0.7 copy-start.7
  12.9 190.8 %all-gather.8.cloned.1.call-start = ((), (), s32[]{:S(2)}) async-start(), calls=%async_computation.4 | async-start | bytes 8650752 | tf_op jit(solution)/shard_map/all_gather | solution.py:737
  14.7 59.6 %copy-start.9 = (s32[9,128]{1,0:T(8,128)S(1)}, s32[9,128]{1,0:T(8,128)}, u32[]{:S(2)}) copy-start(s32[9,128]{1,0:T(8,128)} %param.26) | copy-start | bytes 13828
  14.7 333.9 %reduce-scatter.4.cloned.1.call-start = ((), (), s32[]{:S(2)}) async-start(), calls=%async_computation.5 | async-start | bytes 5242880 | tf_op jit(solution)/shard_map/reduce_scatter | solution.py:831
  15.7 37.0 %collective-permute-start = (bf16[768,128]{1,0:T(8,128)(2,1)S(1)}, bf16[768,128]{1,0:T(8,128)(2,1)S(1)}, u32[]{:S(2)}, u32[]{:S(2)}) collective-permute-start(bf16[768,128]{1,0:T(8,128)(2,1)S(1)} %pad_maximum_fusion.8), channel_id=1, source_target_pairs={{0,2},{1,3},{2,4},{3,5},{4,6},{5,7},{6,0},{7,1},{8,10},{9,11},{10,... | collective-permute-start | bytes 589832 | tf_op jit(solution)/shard_map/ppermute | solution.py:748
  18.8 33.9 %collective-permute-start.1 = (bf16[768,128]{1,0:T(8,128)(2,1)S(1)}, bf16[768,128]{1,0:T(8,128)(2,1)S(1)}, u32[]{:S(2)}, u32[]{:S(2)}) collective-permute-start(bf16[768,128]{1,0:T(8,128)(2,1)S(1)} %pad_maximum_fusion.8), channel_id=1, source_target_pairs={{0,4},{1,5},{2,6},{3,7},{4,0},{5,1},{6,2},{7,3},{8,12},{9,13},{10,... | collective-permute-start | bytes 589832 | tf_op jit(solution)/shard_map/ppermute | solution.py:748
  21.4 31.4 %collective-permute-start.2 = (bf16[768,128]{1,0:T(8,128)(2,1)S(1)}, bf16[768,128]{1,0:T(8,128)(2,1)S(1)}, u32[]{:S(2)}, u32[]{:S(2)}) collective-permute-start(bf16[768,128]{1,0:T(8,128)(2,1)S(1)} %pad_maximum_fusion.8), channel_id=1, source_target_pairs={{0,6},{1,7},{2,0},{3,1},{4,2},{5,3},{6,4},{7,5},{8,14},{9,15},{10,... | collective-permute-start | bytes 589832 | tf_op jit(solution)/shard_map/ppermute | solution.py:748
  53.6 16.0 %collective-permute-start.4 = (bf16[1,4,384,128]{3,2,1,0:T(8,128)(2,1)}, bf16[1,4,384,128]{3,2,1,0:T(8,128)(2,1)S(1)}, u32[]{:S(2)}, u32[]{:S(2)}) collective-permute-start(bf16[1,4,384,128]{3,2,1,0:T(8,128)(2,1)} %tied.4), channel_id=1, source_target_pairs={{0,8},{8,0},{16,24},{24,16},{1,9},{9,1},{17,25},{25,17},{2,10},{10... | collective-permute-start | bytes 1179656 | tf_op jit(solution)/shard_map/ppermute | solution.py:748
  55.0 17.2 %collective-permute-start.3 = (bf16[1,4,384,128]{3,2,1,0:T(8,128)(2,1)S(1)}, bf16[1,4,384,128]{3,2,1,0:T(8,128)(2,1)S(1)}, u32[]{:S(2)}, u32[]{:S(2)}) collective-permute-start(bf16[1,4,384,128]{3,2,1,0:T(8,128)(2,1)S(1)} %maximum_bitcast_fusion), channel_id=1, source_target_pairs={{0,16},{8,24},{16,0},{24,8},{1,17},{9,25},{17,1},{25,9},{2,18},{10... | collective-permute-start | bytes 1179656 | tf_op jit(solution)/shard_map/ppermute | solution.py:748
  70.7 35.6 %copy-start.1 = (bf16[2,4,384,128]{3,2,1,0:T(8,128)(2,1)}, bf16[2,4,384,128]{3,2,1,0:T(8,128)(2,1)S(1)}, u32[]{:S(2)}) copy-start(bf16[2,4,384,128]{3,2,1,0:T(8,128)(2,1)S(1)} %pad_maximum_fusion.3.refs_0_) | copy-start | bytes 2359300
  70.7 35.6 %collective-permute-start.5 = (bf16[2,4,384,128]{3,2,1,0:T(8,128)(2,1)S(1)}, bf16[2,4,384,128]{3,2,1,0:T(8,128)(2,1)S(1)}, u32[]{:S(2)}, u32[]{:S(2)}) collective-permute-start(bf16[2,4,384,128]{3,2,1,0:T(8,128)(2,1)S(1)} %pad_maximum_fusion.3.refs_0_), channel_id=1, source_target_pairs={{0,16},{8,24},{16,0},{24,8},{1,17},{9,25},{17,1},{25,9},{2,18},{10... | collective-permute-start | bytes 2359304 | tf_op jit(solution)/shard_map/ppermute | solution.py:748
  72.2 2.6 copy-start
  72.2 36.6 %collective-permute-start.6 = (bf16[2,4,384,128]{3,2,1,0:T(8,128)(2,1)S(1)}, bf16[2,4,384,128]{3,2,1,0:T(8,128)(2,1)S(1)}, u32[]{:S(2)}, u32[]{:S(2)}) collective-permute-start(bf16[2,4,384,128]{3,2,1,0:T(8,128)(2,1)S(1)} %pad_maximum_fusion.2.refs_5_.refs_0_), channel_id=1, source_target_pairs={{0,8},{8,0},{16,24},{24,16},{1,9},{9,1},{17,25},{25,17},{2,10},{10... | collective-permute-start | bytes 2359304 | tf_op jit(solution)/shard_map/ppermute | solution.py:748
  106.3 0.9 copy-start.6
  108.7 6.8 %copy-start.5 = (bf16[4,4,384,128]{3,2,1,0:T(8,128)(2,1)}, bf16[4,4,384,128]{3,2,1,0:T(8,128)(2,1)S(1)}, u32[]{:S(2)}) copy-start(bf16[4,4,384,128]{3,2,1,0:T(8,128)(2,1)S(1)} %pad_maximum_fusion.refs_2_) | copy-start | bytes 4718596
  108.7 4.0 collective-permute-start.7
  111.7 3.8 collective-permute-start.8
  112.7 2.7 copy-start.11
  203.3 21.7 %collective-permute-start.9 = (bf16[4,4,1024,128]{3,2,1,0:T(8,128)(2,1)}, bf16[4,4,1024,128]{3,2,1,0:T(8,128)(2,1)}, u32[]{:S(2)}, u32[]{:S(2)}) collective-permute-start(bf16[4,4,1024,128]{3,2,1,0:T(8,128)(2,1)} %get-tuple-element.100.refs_5_), channel_id=1, source_target_pairs={{0,1},{1,0},{2,3},{3,2},{4,5},{5,4},{6,7},{7,6},{8,9},{9,8},{10,11... | collective-permute-start | bytes 12582920 | tf_op jit(solution)/shard_map/ppermute | solution.py:827
  231.1 143.0 %reduce-scatter.6.cloned.1.call-start = ((), (), s32[]{:S(2)}) async-start(), calls=%async_computation.6 | async-start | bytes 5242880 | tf_op jit(solution)/shard_map/reduce_scatter | solution.py:831
  248.2 25.4 %collective-permute-start.10 = (bf16[4,4,1024,128]{3,2,1,0:T(8,128)(2,1)}, bf16[4,4,1024,128]{3,2,1,0:T(8,128)(2,1)S(1)}, u32[]{:S(2)}, u32[]{:S(2)}) collective-permute-start(bf16[4,4,1024,128]{3,2,1,0:T(8,128)(2,1)} %get-tuple-element.107.refs_8_), channel_id=1, source_target_pairs={{0,1},{1,0},{2,3},{3,2},{4,5},{5,4},{6,7},{7,6},{8,9},{9,8},{10,11... | collective-permute-start | bytes 12582920 | tf_op jit(solution)/shard_map/ppermute | solution.py:827
  273.6 2.0 copy-start.3
  281.7 128.6 %reduce-scatter.8.cloned.1.call-start = ((), (), s32[]{:S(2)}) async-start(), calls=%async_computation.7 | async-start | bytes 5324800 | tf_op jit(solution)/shard_map/reduce_scatter | solution.py:831
  316.9 17.6 %copy-start.10 = (f32[2,1024]{1,0:T(2,128)S(1)}, f32[2,1024]{1,0:T(2,128)}, u32[]{:S(2)}) copy-start(f32[2,1024]{1,0:T(2,128)} %get-tuple-element.116) | copy-start | bytes 24580
  332.6 7.5 %collective-permute-start.11 = (bf16[4,4,768,128]{3,2,1,0:T(8,128)(2,1)}, bf16[4,4,768,128]{3,2,1,0:T(8,128)(2,1)S(1)}, u32[]{:S(2)}, u32[]{:S(2)}) collective-permute-start(bf16[4,4,768,128]{3,2,1,0:T(8,128)(2,1)} %get-tuple-element.118), channel_id=1, source_target_pairs={{0,1},{1,0},{2,3},{3,2},{4,5},{5,4},{6,7},{7,6},{8,9},{9,8},{10,11... | collective-permute-start | bytes 9437192 | tf_op jit(solution)/shard_map/ppermute | solution.py:827
  333.0 7.1 %collective-permute-start.12 = (bf16[4,4,256,128]{3,2,1,0:T(8,128)(2,1)}, bf16[4,4,256,128]{3,2,1,0:T(8,128)(2,1)}, u32[]{:S(2)}, u32[]{:S(2)}) collective-permute-start(bf16[4,4,256,128]{3,2,1,0:T(8,128)(2,1)} %get-tuple-element.119), channel_id=1, source_target_pairs={{0,1},{1,0},{2,3},{3,2},{4,5},{5,4},{6,7},{7,6},{8,9},{9,8},{10,11... | collective-permute-start | bytes 3145736 | tf_op jit(solution)/shard_map/ppermute | solution.py:827
  336.5 3.4 collective-permute-start.13
  339.9 0.6 copy-start.8
  340.1 1.7 copy-start.4
  349.8 22.4 %collective-permute-start.20 = (bf16[1024,128]{1,0:T(8,128)(2,1)S(1)}, bf16[1024,128]{1,0:T(8,128)(2,1)S(1)}, u32[]{:S(2)}, u32[]{:S(2)}) collective-permute-start(bf16[1024,128]{1,0:T(8,128)(2,1)S(1)} %get-tuple-element.126), channel_id=1, source_target_pairs={{0,2},{1,3},{2,4},{3,5},{4,6},{5,7},{6,0},{7,1},{8,10},{9,11},{10,... | collective-permute-start | bytes 786440 | tf_op jit(solution)/shard_map/ppermute | solution.py:748
  351.3 20.9 %collective-permute-start.21 = (bf16[1024,128]{1,0:T(8,128)(2,1)S(1)}, bf16[1024,128]{1,0:T(8,128)(2,1)S(1)}, u32[]{:S(2)}, u32[]{:S(2)}) collective-permute-start(bf16[1024,128]{1,0:T(8,128)(2,1)S(1)} %get-tuple-element.128), channel_id=1, source_target_pairs={{0,4},{1,5},{2,6},{3,7},{4,0},{5,1},{6,2},{7,3},{8,12},{9,13},{10,... | collective-permute-start | bytes 786440 | tf_op jit(solution)/shard_map/ppermute | solution.py:748
  353.5 18.6 %collective-permute-start.22 = (bf16[1024,128]{1,0:T(8,128)(2,1)S(1)}, bf16[1024,128]{1,0:T(8,128)(2,1)S(1)}, u32[]{:S(2)}, u32[]{:S(2)}) collective-permute-start(bf16[1024,128]{1,0:T(8,128)(2,1)S(1)} %get-tuple-element.127), channel_id=1, source_target_pairs={{0,6},{1,7},{2,0},{3,1},{4,2},{5,3},{6,4},{7,5},{8,14},{9,15},{10,... | collective-permute-start | bytes 786440 | tf_op jit(solution)/shard_map/ppermute | solution.py:748
  375.3 33.8 %collective-permute-start.14 = (bf16[1024,128]{1,0:T(8,128)(2,1)S(1)}, bf16[1024,128]{1,0:T(8,128)(2,1)S(1)}, u32[]{:S(2)}, u32[]{:S(2)}) collective-permute-start(bf16[1024,128]{1,0:T(8,128)(2,1)S(1)} %get-tuple-element.129), channel_id=1, source_target_pairs={{0,2},{1,3},{2,4},{3,5},{4,6},{5,7},{6,0},{7,1},{8,10},{9,11},{10,... | collective-permute-start | bytes 786440 | tf_op jit(solution)/shard_map/ppermute | solution.py:748
  380.8 28.4 %collective-permute-start.15 = (bf16[1024,128]{1,0:T(8,128)(2,1)S(1)}, bf16[1024,128]{1,0:T(8,128)(2,1)S(1)}, u32[]{:S(2)}, u32[]{:S(2)}) collective-permute-start(bf16[1024,128]{1,0:T(8,128)(2,1)S(1)} %get-tuple-element.131), channel_id=1, source_target_pairs={{0,4},{1,5},{2,6},{3,7},{4,0},{5,1},{6,2},{7,3},{8,12},{9,13},{10,... | collective-permute-start | bytes 786440 | tf_op jit(solution)/shard_map/ppermute | solution.py:748
  381.9 27.3 %collective-permute-start.16 = (bf16[1024,128]{1,0:T(8,128)(2,1)S(1)}, bf16[1024,128]{1,0:T(8,128)(2,1)S(1)}, u32[]{:S(2)}, u32[]{:S(2)}) collective-permute-start(bf16[1024,128]{1,0:T(8,128)(2,1)S(1)} %get-tuple-element.130), channel_id=1, source_target_pairs={{0,6},{1,7},{2,0},{3,1},{4,2},{5,3},{6,4},{7,5},{8,14},{9,15},{10,... | collective-permute-start | bytes 786440 | tf_op jit(solution)/shard_map/ppermute | solution.py:748
  410.3 6.1 %copy-start.2 = (f32[1024,128]{1,0:T(8,128)}, f32[1024,128]{1,0:T(8,128)S(1)}, u32[]{:S(2)}) copy-start(f32[1024,128]{1,0:T(8,128)S(1)} %fusion.5.refs_4_) | copy-start | bytes 1572868
  411.6 23.6 %collective-permute-start.17 = (bf16[1040,128]{1,0:T(8,128)(2,1)S(1)}, bf16[1040,128]{1,0:T(8,128)(2,1)S(1)}, u32[]{:S(2)}, u32[]{:S(2)}) collective-permute-start(bf16[1040,128]{1,0:T(8,128)(2,1)S(1)} %get-tuple-element.123), channel_id=1, source_target_pairs={{0,2},{1,3},{2,4},{3,5},{4,6},{5,7},{6,0},{7,1},{8,10},{9,11},{10,... | collective-permute-start | bytes 798728 | tf_op jit(solution)/shard_map/ppermute | solution.py:748
  412.4 22.9 %collective-permute-start.18 = (bf16[1040,128]{1,0:T(8,128)(2,1)S(1)}, bf16[1040,128]{1,0:T(8,128)(2,1)S(1)}, u32[]{:S(2)}, u32[]{:S(2)}) collective-permute-start(bf16[1040,128]{1,0:T(8,128)(2,1)S(1)} %get-tuple-element.125), channel_id=1, source_target_pairs={{0,4},{1,5},{2,6},{3,7},{4,0},{5,1},{6,2},{7,3},{8,12},{9,13},{10,... | collective-permute-start | bytes 798728 | tf_op jit(solution)/shard_map/ppermute | solution.py:748
  414.2 21.0 %collective-permute-start.19 = (bf16[1040,128]{1,0:T(8,128)(2,1)S(1)}, bf16[1040,128]{1,0:T(8,128)(2,1)S(1)}, u32[]{:S(2)}, u32[]{:S(2)}) collective-permute-start(bf16[1040,128]{1,0:T(8,128)(2,1)S(1)} %get-tuple-element.124), channel_id=1, source_target_pairs={{0,6},{1,7},{2,0},{3,1},{4,2},{5,3},{6,4},{7,5},{8,14},{9,15},{10,... | collective-permute-start | bytes 798728 | tf_op jit(solution)/shard_map/ppermute | solution.py:748
Sparse Core Ops, SparseCore 0:
  13.0 112.3 all-gather.5
  129.0 74.6 all-gather.7
  231.3 53.0 reduce-scatter.3
  287.4 52.6 reduce-scatter.5
  348.0 53.4 reduce-scatter.7

commit v2 on v1

v2 whole, which is shorter than its diff:
```python
import functools
import math

import jax
import jax.numpy as jnp
from jax import lax
from jax.experimental import pallas as pl
from jax.experimental.pallas import tpu as pltpu
from jax.sharding import PartitionSpec as P

HEADS = 16
HD = 64
EPSILON = 1e-06
F32 = jnp.float32
BF16 = jnp.bfloat16
BOTH = ("row", "col")
SLOW = 1

NN = (((1,), (0,)), ((), ()))
NT = (((1,), (1,)), ((), ()))
TN = (((0,), (0,)), ((), ()))


def mul(a, b, dims=NN):
    return lax.dot_general(a, b, dims, preferred_element_type=F32)


def call(
    body, name, grid, ins, outs, shapes, scratch=(), prefetch=0, flops=0, nbytes=0, deps=(), alias=None, vmem=56
):
    count = prefetch + len(ins)

    def run(*refs):
        body(*refs[:count], *refs[count + len(deps) :])

    made = pl.pallas_call(
        run,
        name=name,
        grid_spec=pltpu.PrefetchScalarGridSpec(
            num_scalar_prefetch=prefetch,
            grid=grid,
            in_specs=ins + [pl.BlockSpec(memory_space=pl.ANY)] * len(deps),
            out_specs=outs,
            scratch_shapes=list(scratch),
        ),
        out_shape=shapes,
        input_output_aliases=alias or {},
        compiler_params=pltpu.CompilerParams(
            dimension_semantics=("arbitrary",) * len(grid),
            vmem_limit_bytes=vmem * 2**20,
        ),
        cost_estimate=pl.CostEstimate(
            flops=flops // SLOW, transcendentals=0, bytes_accessed=nbytes // SLOW
        ),
    )
    return lambda *args: made(*args, *deps)


def tied(value, *deps):
    return call(
        lambda given, out: None,
        "tied",
        (1,),
        [pl.BlockSpec(memory_space=pl.ANY)],
        pl.BlockSpec(memory_space=pl.ANY),
        shaped(value.shape, value.dtype),
        deps=deps,
        alias={0: 0},
        vmem=60,
    )(value)


def whole(shape):
    return pl.BlockSpec(shape, lambda *_: (0,) * len(shape))


def once(shape):
    return pl.BlockSpec(shape, lambda *_: (0,) * len(shape), pipeline_mode=pl.Buffered(1))


def shaped(shape, dtype):
    return jax.ShapeDtypeStruct(shape, dtype)


def one_hot(index_ref, length):
    places = lax.broadcasted_iota(jnp.int32, (length, index_ref.shape[-1]), 0)
    return places == index_ref[0]


def pick_cot_body(index, cot, grows, base):
    hot = jnp.where(one_hot(index, cot.shape[0]), 1.0, 0.0).astype(BF16)
    grows[...] = mul(hot, cot[...], TN).astype(BF16)
    base[...] = cot[...].astype(F32)


def pick_body(index, tok, picked):
    hot = jnp.where(one_hot(index, tok.shape[0]), 1.0, 0.0).astype(BF16)
    picked[...] = mul(hot, tok[...], TN).astype(BF16)


def pick(name, source, index, with_copy, start=0, stop=None, begun=(), deps=()):
    seqs, _, routed = index.shape
    length, width = source.shape[0] // seqs, source.shape[1]
    whole_seq = pl.BlockSpec((length, width), lambda s: (s + start, 0))
    part = pl.BlockSpec((routed, width), lambda s: (s + start, 0))
    rows = shaped((seqs * routed, width), BF16)
    return call(
        functools.partial(begun_body, pick_cot_body if with_copy else pick_body, len(begun)),
        name,
        ((stop or seqs) - start,),
        [pl.BlockSpec((1, 1, routed), lambda s: (s + start, 0, 0)), whole_seq]
        + [pl.BlockSpec(memory_space=pl.ANY)] * len(begun),
        [part, whole_seq] if with_copy else part,
        [rows, shaped(source.shape, F32)] if with_copy else rows,
        flops=2 * seqs * routed * length * width,
        nbytes=6 * source.size,
        deps=deps,
        alias={2 + i: i for i in range(len(begun))},
    )(index, source, *begun)


def begun_body(body, count, index, source, *refs):
    body(index, source, *refs[count:])


def lay_rc(w, buf, kb):
    rs, cs, tall, wp = w.shape
    pieces = tall // kb
    for r in range(rs):
        for c in range(cs):
            for t in range(pieces):
                at = (c * pieces + t) * wp
                buf[r * kb : (r + 1) * kb, at : at + wp] = w[r, c, t * kb : (t + 1) * kb, :]


def lay_cr(w, buf, kb):
    rs, cs, tall, wp = w.shape
    pieces = tall // kb
    for r in range(rs):
        for c in range(cs):
            for t in range(pieces):
                at = (r * pieces + t) * wp
                buf[c * kb : (c + 1) * kb, at : at + wp] = w[r, c, t * kb : (t + 1) * kb, :]


def lay_turned(spots, own, other, place, rs, zs, looped=False):
    bit = spots[2, 0]
    for core in range(2):

        def lay(r, carry):
            for z in range(zs):
                place(r, z, core, own)
                place(r, z, 1 - core, other)
            return carry

        @pl.when(bit == core)
        def _():
            if looped:
                lax.fori_loop(0, rs, lay, 0)
            else:
                for r in range(rs):
                    lay(r, 0)


def project_body(
    kb, wp, count, spots, picked, grows, own_a, own_b, other_a, other_b, own_s, other_s,
    out, natural, normed, gmlp, gate, small,
):
    rs, zs = own_s.shape[:2]
    tall = kb * count // 2
    rows, width = picked.shape
    each = width // (rs * zs * 2)

    def place_small(r, z, core, source):
        at = (r * zs * 2 + 2 * z + core) * each
        line = source[spots[0, r], spots[3, z], 0:16, :].astype(F32)
        for k in range(3):
            small[k : k + 1, at : at + each] = line[0:1, k * each : (k + 1) * each]

    @pl.when(pl.program_id(0) == 0)
    def _():
        lay_turned(spots, own_s, other_s, place_small, rs, zs)
        chunk = 128

        def prepare(i, carry):
            at = pl.ds(pl.multiple_of(i * chunk, chunk), chunk)
            value = picked[at, :].astype(F32)
            opened = jax.nn.sigmoid(jnp.sum(value * small[0:1, :], axis=-1, keepdims=True))
            inverse = lax.rsqrt(jnp.mean(value * value, axis=-1, keepdims=True) + EPSILON)
            normed[at, :] = (value * inverse * small[1:2, :]).astype(BF16)
            gmlp[at, :] = (grows[at, :].astype(F32) * opened).astype(BF16)
            gate[at, :] = opened
            return carry

        lax.fori_loop(0, rows // chunk, prepare, 0)

    def place(r, z, core, halves_of):
        size = kb // 2
        for t in range(2 * count):
            half, at = divmod(t * size, tall)
            value = halves_of[half][spots[half, r], 0, at : at + size, :]
            lane = (core * count + t // 2) * wp
            down = pl.multiple_of(r * kb + t % 2 * size, size)
            natural[pl.ds(down, size), lane : lane + wp] = value

    lay_turned(spots, (own_a, own_b), (other_a, other_b), place, rs, 1, looped=True)
    out[...] = mul(normed[...], natural[...]).astype(BF16)


def project(spots, picked, grows, parts, kb, count):
    rows, depth = picked.shape
    rs, zs, tall, wp = parts[0].shape
    step = 2 * count * wp
    piece = pl.BlockSpec((rs, 1, tall, wp), lambda j, spots: (0, spots[3, j], 0, 0))
    last = pl.BlockSpec((rs, zs, 16, wp), lambda j, _: (0, 0, tall // 16 - 1, 0))
    return call(
        functools.partial(project_body, kb, wp, count),
        "project",
        (zs,),
        [whole(picked.shape)] * 2 + [piece] * 4 + [last] * 2,
        [
            pl.BlockSpec((rows, step), lambda j, _: (0, j)),
            pl.BlockSpec((depth, step), lambda j, _: (0, j)),
            whole(picked.shape),
            whole(picked.shape),
            whole((rows, 1)),
            whole((3, depth)),
        ],
        [
            shaped((rows, zs * step), BF16),
            shaped((depth, zs * step), BF16),
            shaped(picked.shape, BF16),
            shaped(picked.shape, BF16),
            shaped((rows, 1), F32),
            shaped((3, depth), F32),
        ],
        prefetch=1,
        flops=2 * rows * depth * zs * step,
        nbytes=2 * (4 * picked.size + 2 * depth * zs * step + rows * zs * step),
    )(spots, picked, grows, *parts, parts[0], parts[2])


def halves():
    lane = lax.broadcasted_iota(jnp.int32, (1, 2 * HD), 1)
    low = jnp.where(lane < HD, 1.0, 0.0).astype(BF16)
    high = jnp.where(lane < HD, 0.0, 1.0).astype(BF16)
    return low, high


def turned(x):
    return jnp.concatenate([x[:, HD:], x[:, :HD]], axis=1) * jnp.asarray(HD**-0.5, BF16)


def causal_of(routed):
    return lax.broadcasted_iota(jnp.int32, (routed, routed), 0) <= lax.broadcasted_iota(
        jnp.int32, (routed, routed), 1
    )


def attend_body(proj, context, probs):
    routed = proj.shape[0]
    low, high = halves()
    causal = causal_of(routed)
    tiles = [proj[:, i * 2 * HD : (i + 1) * 2 * HD] for i in range(3 * HEADS // 2)]
    scores = []
    for a, b, c in zip(tiles[::3], tiles[1::3], tiles[2::3]):
        scores.append(mul(turned(a) * low, a, NT))
        scores.append(mul(turned(c) * high, b, NT))
    scores = [jnp.where(causal, score, -1e30) for score in scores]
    highest = [jnp.max(score, axis=0, keepdims=True) for score in scores]
    expanded = [jnp.exp(score - top) for score, top in zip(scores, highest)]
    inverse = [1.0 / jnp.sum(e, axis=0, keepdims=True) for e in expanded]
    weights = [(e * i).astype(BF16) for e, i in zip(expanded, inverse)]
    for pair in range(HEADS // 2):
        b, c = tiles[3 * pair + 1], tiles[3 * pair + 2]
        both = jnp.concatenate(weights[2 * pair : 2 * pair + 2], axis=0)
        probs[0, 2 * pair * routed : 2 * (pair + 1) * routed, :] = both
        mixed = mul(both, jnp.concatenate([b * low, c * high], axis=0), TN)
        context[:, pair * 2 * HD : (pair + 1) * 2 * HD] = mixed.astype(BF16)


def attend(projected, seqs):
    rows, wide = projected.shape
    routed = rows // seqs
    width = wide // 3
    return call(
        attend_body,
        "attend",
        (seqs,),
        [pl.BlockSpec((routed, wide), lambda s: (s, 0))],
        [
            pl.BlockSpec((routed, width), lambda s: (s, 0)),
            pl.BlockSpec((1, HEADS * routed, routed), lambda s: (s, 0, 0)),
        ],
        [shaped((rows, width), BF16), shaped((seqs, HEADS * routed, routed), BF16)],
        flops=20 * rows * wide * routed,
        nbytes=8 * projected.size,
    )(projected)


def mix_body(kb, context, w, picked, gain, attn, normed, natural):
    @pl.when(pl.program_id(0) == 0)
    def _():
        lay_cr(w, natural, kb)

    out = mul(context[...], natural[...])
    attn[...] = out
    middle = picked[...].astype(F32) + out
    inverse = lax.rsqrt(jnp.mean(middle * middle, axis=-1, keepdims=True) + EPSILON)
    normed[...] = (middle * inverse * gain[...]).astype(BF16)


def mix(context, w, at, tall, kb, picked, gain, steps):
    rows, width = context.shape
    rs, cs, _, wp = w.shape
    part = pl.BlockSpec((rows // steps, width), lambda s: (s, 0))
    return call(
        functools.partial(mix_body, kb),
        "mix",
        (steps,),
        [part, pl.BlockSpec((rs, cs, tall, wp), lambda s: (0, 0, at, 0)), part, whole(gain.shape)],
        [part, part, whole((width, width))],
        [shaped((rows, width), F32), shaped((rows, width), BF16), shaped((width, width), BF16)],
        flops=2 * rows * width * width,
        nbytes=14 * rows * width,
    )(context, w, picked, gain)


GELU_A = 0.7978845608028654
GELU_B = 0.044715


def raise_body(kb, bit, x, gmlp, w, hidden, slope, natural, send, keep):
    lay_rc(w, natural, kb)
    rs, _, tall, wp = send.shape
    fb = hidden.shape[1] // 2

    def half_of(h, carry):
        across = pl.ds(pl.multiple_of(h * fb, fb), fb)
        pre = mul(x[...], natural[:, across])
        square = pre * pre
        half = 0.5 + 0.5 * jnp.tanh(pre * (GELU_A + (GELU_A * GELU_B) * square))
        value = pre * half
        hidden[:, across] = value.astype(BF16)
        slope[:, across] = (
            half + value * (1.0 - half) * (2 * GELU_A + (6 * GELU_A * GELU_B) * square)
        ).astype(BF16)
        total = mul(hidden[:, across], gmlp[...], TN).astype(BF16)
        many = tall // fb

        def put(target):
            for r in range(rs):
                for t in range(many):
                    lane = (r * many + t) * wp
                    target[r, 0, t * fb : (t + 1) * fb, :] = total[:, lane : lane + wp]

        @pl.when(bit[0] == h)
        def _():
            put(keep)

        @pl.when(bit[0] != h)
        def _():
            put(send)

        return carry

    lax.fori_loop(0, 2, half_of, 0)


def raised(bit, x, gmlp, w, at, tall, kb, shape):
    rows, depth = x.shape
    rs, cs, _, wp = w.shape
    fb = (tall // kb) * wp
    zs = cs // 2
    out = pl.BlockSpec((rows, 2 * fb), lambda j, _: (0, j))
    half = (rs, zs, shape[2] * shape[3] // wp, wp)
    grad = pl.BlockSpec((rs, 1) + half[2:], lambda j, _: (0, j, 0, 0))
    return call(
        functools.partial(raise_body, kb),
        "raise",
        (zs,),
        [once(x.shape), once(gmlp.shape)]
        + [pl.BlockSpec((rs, 2, tall, wp), lambda j, _: (0, j, at, 0))],
        [out, out, pl.BlockSpec((depth, 2 * fb), lambda j, _: (0, j)), grad, grad],
        [shaped((rows, cs * fb), BF16)] * 2
        + [shaped((depth, cs * fb), BF16)]
        + [shaped(half, BF16)] * 2,
        prefetch=1,
        flops=5 * rows * depth * cs * fb,
        nbytes=2 * (x.size + 3 * depth * cs * fb + 2 * rows * cs * fb),
    )(bit, x, gmlp, w)


def split_out(bit, first, second, keep, send, at):
    @pl.when(bit == 0)
    def _():
        keep[at] = first
        send[at] = second

    @pl.when(bit != 0)
    def _():
        keep[at] = second
        send[at] = first


def grad_rc(bit, total, send, keep, kb, nb):
    rs, zs, _, wp = send.shape
    for r in range(rs):
        for j in range(zs):
            for t in range(nb // wp):
                at = 2 * j * nb + t * wp
                down = slice(r * kb, (r + 1) * kb)
                where = (r, j, slice(t * kb, (t + 1) * kb))
                split_out(
                    bit, total[down, at : at + wp], total[down, at + nb : at + nb + wp], keep, send, where
                )


def grad_cr(bit, total, send, keep, kb, nb):
    rs, zs, _, wp = send.shape
    for r in range(rs):
        for j in range(zs):
            for t in range(nb // wp):
                across = slice(r * nb + t * wp, r * nb + (t + 1) * wp)
                where = (r, j, slice(t * kb, (t + 1) * kb))
                at = 2 * j * kb
                split_out(
                    bit, total[at : at + kb, across], total[at + kb : at + 2 * kb, across], keep, send, where
                )


def qkv_grad_body(
    kb, nb, bit, x, y, w, gsmall, gain, send, keep, little_send, little_keep, first
):
    step = pl.program_id(0)
    total = mul(x[...], y[...], TN)

    @pl.when(step == 0)
    def _():
        first[...] = jnp.zeros_like(first)

    first[...] += jnp.sum(total * w[...].astype(F32), axis=-1, keepdims=True)
    grad_rc(bit[0], total.astype(BF16), send, keep, kb, nb)

    @pl.when(step == pl.num_programs(0) - 1)
    def _():
        rs, zs, tall, wp = little_send.shape
        size = 128
        eye = lax.broadcasted_iota(jnp.int32, (size, size), 0) == lax.broadcasted_iota(
            jnp.int32, (size, size), 1
        )
        column = [first[i : i + size, :] for i in range(0, first.shape[0], size)]
        column = [jnp.sum(jnp.where(eye, part, 0.0), axis=0, keepdims=True) for part in column]
        lines = [gsmall[0:1, :], gsmall[1:2, :], jnp.concatenate(column, axis=1) / gain[...]]
        each = gain.shape[1] // (rs * zs * 2)

        def line_of(r, c):
            at = (r * zs * 2 + c) * each
            parts = [line[:, at : at + each] for line in lines]
            parts.append(jnp.zeros((1, wp - 3 * each), F32))
            return jnp.broadcast_to(jnp.concatenate(parts, axis=1), (tall, wp)).astype(BF16)

        for r in range(rs):
            for z in range(zs):
                pair = line_of(r, 2 * z), line_of(r, 2 * z + 1)
                split_out(bit[0], *pair, little_keep, little_send, (r, z))


def qkv_weight_grad(bit, x, y, w, gsmall, gain, shape, wp, count, deps=()):
    rows, depth = x.shape
    rs, cs, kb, nb = shape
    zs = cs // 2
    many = zs // count
    tall = kb * nb // wp
    step = 2 * many * nb
    out = pl.BlockSpec((rs, many, tall, wp), lambda j, _: (0, j, 0, 0))
    little = (rs, zs, 16, wp)
    return call(
        functools.partial(qkv_grad_body, kb, nb),
        "qkv_grad",
        (count,),
        [
            whole(x.shape),
            pl.BlockSpec((rows, step), lambda j, _: (0, j)),
            pl.BlockSpec((depth, step), lambda j, _: (0, j)),
            whole(gsmall.shape),
            whole(gain.shape),
        ],
        [out, out, whole(little), whole(little)],
        [shaped((rs, zs, tall, wp), BF16)] * 2 + [shaped(little, BF16)] * 2,
        [pltpu.VMEM((depth, 1), F32)],
        prefetch=1,
        flops=2 * rows * depth * cs * nb,
        nbytes=2 * (x.size + y.size + 2 * w.size),
        deps=deps,
    )(bit, x, y, w, gsmall, gain)


def feed_back_body(
    kb, ub, bit, grows, w, slope, hidden, gate, x, w_up,
    natural, dots, send, keep, total, x_turned,
):
    rs, _, tall, wp = w.shape
    pieces_up = kb // wp
    step = pl.program_id(0)
    lay_cr(w, natural, kb)

    @pl.when(step == 0)
    def _():
        x_turned[...] = x[...].T
        dots[...] = jnp.zeros_like(dots)
        total[...] = jnp.zeros_like(total)

    def half(h, carry):
        at = pl.ds(pl.multiple_of(h * kb, kb), kb)
        back = mul(grows[...], natural[at, :], NT)
        gpre = (back * gate[...] * slope[:, at].astype(F32)).astype(BF16)
        product = back * hidden[:, at].astype(F32)
        summed = product[:, :128]
        for n in range(1, kb // 128):
            summed = summed + product[:, n * 128 : (n + 1) * 128]
        dots[...] += summed
        part = mul(x_turned[...], gpre).astype(BF16)

        def put(target):
            for r in range(rs):
                for t in range(pieces_up):
                    value = part[r * ub : (r + 1) * ub, t * wp : (t + 1) * wp]
                    target[r, 0, t * ub : (t + 1) * ub, :] = value

        @pl.when(bit[0] == h)
        def _():
            put(keep)

        @pl.when(bit[0] != h)
        def _():
            put(send)

        total[...] += mul(gpre, w_up[:, at], NT)
        return carry

    lax.fori_loop(0, 2, half, 0)


def feed_back(bit, grows, w, slope, hidden, gate, x, w_up, kb, ub, deps=()):
    rows, width = grows.shape
    rs, cs, tall, wp = w.shape
    zs = cs // 2
    deep = hidden.shape[1]
    fb = 2 * kb
    cut = pl.BlockSpec((rows, fb), lambda j, _: (0, j))
    half = (rs, zs, ub * kb // wp, wp)
    grad = pl.BlockSpec((rs, 1) + half[2:], lambda j, _: (0, j, 0, 0))
    return call(
        functools.partial(feed_back_body, kb, ub),
        "feed_back",
        (zs,),
        [once(grows.shape), pl.BlockSpec((rs, 2, tall, wp), lambda j, _: (0, j, 0, 0)), cut, cut]
        + [once(gate.shape), once(x.shape), pl.BlockSpec((width, fb), lambda j, _: (0, j))],
        [
            pl.BlockSpec((fb, width), lambda j, _: (j, 0)),
            whole((rows, 128)),
            grad,
            grad,
            whole((rows, width)),
        ],
        [shaped((deep, width), BF16), shaped((rows, 128), F32)]
        + [shaped(half, BF16)] * 2
        + [shaped((rows, width), F32)],
        [pltpu.VMEM((width, rows), BF16)],
        prefetch=1,
        flops=6 * rows * width * deep,
        nbytes=2 * (3 * width * deep + 2 * rows * deep + 4 * rows * width),
        deps=deps,
    )(bit, grows, w, slope, hidden, gate, x, w_up)


def norm_back(grad, v, inverse, gain):
    scaled = grad * gain
    summed = jnp.sum(scaled * v, axis=-1, keepdims=True)
    return inverse * scaled - v * (inverse * inverse * inverse * summed / v.shape[-1])


def context_back_body(
    kb, nb, bit, total, attn, picked, grows, gate, dots, context, gain, w,
    gmid, gcontext, logit, gsmall, send, keep, gattn, gout,
):
    step = pl.program_id(0)

    @pl.when(step == 0)
    def _():
        gsmall[...] = jnp.zeros_like(gsmall)
        gout[...] = jnp.zeros_like(gout)

    chunk = 128

    def rows_back(i, carry):
        at = pl.ds(pl.multiple_of(i * chunk, chunk), chunk)
        grad = total[at, :]
        rows = picked[at, :].astype(F32)
        middle = rows + attn[at, :]
        inverse = lax.rsqrt(jnp.mean(middle * middle, axis=-1, keepdims=True) + EPSILON)
        gsmall[0:1, :] += jnp.sum(grad * middle * inverse, axis=0, keepdims=True)
        back = norm_back(grad, middle, inverse, gain[...])
        gmid[at, :] = back
        opened, dy = gate[at, :], grows[at, :].astype(F32)
        gattn[at, :] = (opened * dy + back).astype(BF16)
        opening = jnp.sum(dots[at, :], axis=-1, keepdims=True)
        opening += jnp.sum(dy * attn[at, :], axis=-1, keepdims=True)
        opening = opening * opened * (1.0 - opened)
        logit[at, :] = opening
        gsmall[1:2, :] += jnp.sum(opening * rows, axis=0, keepdims=True)
        return carry

    lax.fori_loop(0, total.shape[0] // chunk, rows_back, 0)
    gcontext[...] = mul(gattn[...], w[...], NT).astype(BF16)
    gout[...] += mul(context[...], gattn[...], TN)

    @pl.when(step == pl.num_programs(0) - 1)
    def _():
        grad_cr(bit[0], gout[...].astype(BF16), send, keep, kb, nb)


def context_back(bit, total, attn, picked, grows, gate, dots, context, gain, w, shape, wp, steps):
    rows, width = attn.shape
    rs, cs, kb, nb = shape
    half = (rs, cs // 2, kb * nb // wp, wp)
    size = rows // steps
    part = pl.BlockSpec((size, width), lambda j, _: (j, 0))
    thin = pl.BlockSpec((size, 1), lambda j, _: (j, 0))
    return call(
        functools.partial(context_back_body, kb, nb),
        "context_back",
        (steps,),
        [part] * 4
        + [thin, pl.BlockSpec((size, 128), lambda j, _: (j, 0)), part]
        + [once(gain.shape), once(w.shape)],
        [part, part, thin, whole((2, width)), whole(half), whole(half)],
        [
            shaped(attn.shape, F32),
            shaped(attn.shape, BF16),
            shaped(gate.shape, F32),
            shaped((2, width), F32),
            shaped(half, BF16),
            shaped(half, BF16),
        ],
        [pltpu.VMEM((size, width), BF16), pltpu.VMEM((width, width), F32)],
        prefetch=1,
        flops=4 * rows * width * width,
        nbytes=26 * rows * width + 6 * width * width,
    )(bit, total, attn, picked, grows, gate, dots, context, gain, w)


def attend_back_body(proj, gcontext, probs, out):
    routed = proj.shape[0]
    low, high = halves()
    tiles = [proj[:, i * 2 * HD : (i + 1) * 2 * HD] for i in range(3 * HEADS // 2)]
    grads, weights, grad_probs = [], [], []
    for pair in range(HEADS // 2):
        b, c = tiles[3 * pair + 1], tiles[3 * pair + 2]
        grad = gcontext[:, pair * 2 * HD : (pair + 1) * 2 * HD]
        grads += [grad * low, grad * high]
        for head in (2 * pair, 2 * pair + 1):
            weights.append(probs[0, head * routed : (head + 1) * routed, :])
        grad_probs += [mul(b, grads[-2], NT), mul(c, grads[-1], NT)]
    wide = [weight.astype(F32) for weight in weights]
    inner = [jnp.sum(g * w, axis=0, keepdims=True) for g, w in zip(grad_probs, wide)]
    backs = [(w * (g - i)).astype(BF16) for g, w, i in zip(grad_probs, wide, inner)]
    for pair in range(HEADS // 2):
        a, b, c = (turned(tile) for tile in tiles[3 * pair : 3 * pair + 3])
        (first, second), (low_grad, high_grad) = (
            each[2 * pair : 2 * pair + 2] for each in (backs, grads)
        )
        at = [slice((3 * pair + t) * 2 * HD, (3 * pair + t + 1) * 2 * HD) for t in range(3)]
        out[:, at[0]] = (mul(first, a * low, TN) + mul(first, a * high)).astype(BF16)
        out[:, at[1]] = (mul(weights[2 * pair], low_grad) + mul(second, c * high, TN)).astype(BF16)
        left = jnp.concatenate([second, weights[2 * pair + 1]], axis=1)
        right = jnp.concatenate([b * low, high_grad], axis=0)
        out[:, at[2]] = mul(left, right).astype(BF16)


def attend_back(projected, gcontext, probs, seqs, deps=()):
    rows, wide = projected.shape
    routed = rows // seqs
    return call(
        attend_back_body,
        "attend_back",
        (seqs,),
        [
            pl.BlockSpec((routed, wide), lambda s: (s, 0)),
            pl.BlockSpec((routed, wide // 3), lambda s: (s, 0)),
            pl.BlockSpec((1, HEADS * routed, routed), lambda s: (s, 0, 0)),
        ],
        pl.BlockSpec((routed, wide), lambda s: (s, 0)),
        shaped((rows, wide), BF16),
        flops=40 * rows * wide * routed,
        nbytes=16 * projected.size,
        deps=deps,
    )(projected, gcontext, probs)


def picked_back_body(
    places, gproj, w, logit, gain, router, picked, gmid, grows, base,
    out, total, picked_in, gmid_in, grows_in, fetched, arrived,
):
    j = pl.program_id(0)
    step = w.shape[0]
    loads = [
        pltpu.make_async_copy(source, target, fetched.at[i])
        for i, (source, target) in enumerate(
            ((picked, picked_in), (gmid, gmid_in), (grows, grows_in))
        )
    ]

    @pl.when(j == 0)
    def _():
        for load in loads:
            load.start()

    total[j] = mul(gproj[...], w[...], NT)

    @pl.when(j == pl.num_programs(0) - 1)
    def _():
        for load in loads:
            load.wait()
        chunk = 128
        count = total.shape[1] // chunk

        def compute(i):
            at = pl.ds(pl.multiple_of(i * chunk, chunk), chunk)
            grad = jnp.concatenate([total[n, at, :] for n in range(total.shape[0])], axis=1)
            rows = picked_in[at, :].astype(F32)
            inverse = lax.rsqrt(jnp.mean(rows * rows, axis=-1, keepdims=True) + EPSILON)
            back = norm_back(grad, rows, inverse, gain[...])
            gmid_in[at, :] = (
                gmid_in[at, :]
                + back
                + (logit[at, :] * router[...] + grows_in[at, :].astype(F32))
            )

        def copy(row):
            pltpu.make_async_copy(
                gmid_in.at[pl.ds(row, 1)], out.at[pl.ds(places[row], 1)], arrived
            ).start()

        def both(i, carry):
            for k in range(chunk):
                copy((i - 1) * chunk + k)
            compute(i)
            return carry

        def last(row, carry):
            copy(row)
            return carry

        compute(0)
        lax.fori_loop(1, count, both, 0)
        lax.fori_loop((count - 1) * chunk, count * chunk, last, 0, unroll=8)
        pltpu.make_async_copy(gmid_in, out.at[pl.ds(0, gmid_in.shape[0])], arrived).wait()


def picked_back(places, gproj, w, picked, gmid, logit, grows, gain, router, base, step, deps=()):
    rows, deep = gproj.shape
    width = picked.shape[1]
    return call(
        picked_back_body,
        "picked_back",
        (width // step,),
        [once(gproj.shape), pl.BlockSpec((step, deep), lambda j, _: (j, 0))]
        + [once(t.shape) for t in (logit, gain, router)]
        + [pl.BlockSpec(memory_space=pl.ANY)] * 4,
        pl.BlockSpec(memory_space=pl.ANY),
        shaped(base.shape, F32),
        [
            pltpu.VMEM((width // step, rows, step), F32),
            pltpu.VMEM((rows, width), BF16),
            pltpu.VMEM((rows, width), F32),
            pltpu.VMEM((rows, width), BF16),
            pltpu.SemaphoreType.DMA((3,)),
            pltpu.SemaphoreType.DMA,
        ],
        prefetch=1,
        flops=2 * rows * deep * width,
        nbytes=2 * (gproj.size + w.size) + 10 * picked.size,
        alias={9: 0},
        deps=deps,
    )(places, gproj, w, logit, gain, router, picked, gmid, grows, base)


def join_body(count, *refs):
    out, at = refs[-1], 0
    for keep, got in zip(refs[:count], refs[count : 2 * count]):
        tall = keep.shape[2]

        def add(z, carry):
            total = keep[0, z].astype(F32) + got[0, z].astype(F32)
            out[0, z, at : at + tall, :] = total.astype(BF16)
            return carry

        lax.fori_loop(0, keep.shape[1], add, 0)
        at += tall


def joined(keeps, gots, deps=()):
    rs, zs, _, wp = keeps[0].shape
    talls = [k.shape[2] for k in keeps]
    blocks = [pl.BlockSpec((1, zs, tall, wp), lambda r: (r, 0, 0, 0)) for tall in talls]
    tall = sum(talls)
    return call(
        functools.partial(join_body, len(keeps)),
        "join",
        (rs,),
        blocks * 2,
        pl.BlockSpec((1, zs, tall, wp), lambda r: (r, 0, 0, 0)),
        shaped((rs, zs, tall, wp), BF16),
        flops=rs * zs * tall * wp,
        nbytes=6 * rs * zs * tall * wp,
        vmem=16,
        deps=deps,
    )(*keeps, *gots)


def lower_body(hidden, w, attn, picked, gate, kept):
    branch = attn[...] + mul(hidden[...], w[...])
    kept[...] = (picked[...].astype(F32) + gate[...] * branch).astype(BF16)


def lowered(hidden, w, attn, picked, gate, step, deps=()):
    rows, deep = hidden.shape
    width = w.shape[1]
    cut = pl.BlockSpec((rows, step), lambda j: (0, j))
    return call(
        lower_body,
        "lower",
        (width // step,),
        [whole(hidden.shape), pl.BlockSpec((deep, step), lambda j: (0, j))]
        + [cut] * 2
        + [whole(gate.shape)],
        cut,
        shaped((rows, width), BF16),
        flops=2 * rows * deep * width,
        nbytes=2 * (hidden.size + w.size) + 8 * attn.size,
        deps=deps,
    )(hidden, w, attn, picked, gate)


def place_body(index, tok, kept, output):
    found = one_hot(index, tok.shape[0])
    hot = jnp.where(found, 1.0, 0.0)
    routed = jnp.sum(hot, axis=-1, keepdims=True) > 0.5
    output[...] = jnp.where(
        routed, mul(hot.astype(BF16), kept[...]), tok[...].astype(F32)
    ).astype(BF16)


def place(tokens, index, kept, deps=()):
    seqs, _, routed = index.shape
    length, width = tokens.shape[0] // seqs, tokens.shape[1]
    whole_seq = pl.BlockSpec((length, width), lambda s: (s, 0))
    return call(
        place_body,
        "place",
        (seqs,),
        [
            pl.BlockSpec((1, 1, routed), lambda s: (s, 0, 0)),
            whole_seq,
            pl.BlockSpec((routed, width), lambda s: (s, 0)),
        ],
        whole_seq,
        shaped(tokens.shape, BF16),
        flops=2 * seqs * routed * length * width,
        nbytes=4 * tokens.size,
        deps=deps,
    )(index, tokens, kept)


def pieces_body(qkv, out, up, down, small, first, second, third):
    def lay(target, at, block):
        kb, nb = block.shape
        wp = target.shape[1]
        for t in range(nb // wp):
            target[at + t * kb : at + (t + 1) * kb, :] = block[:, t * wp : (t + 1) * wp]

    kb, nb = qkv.shape
    wp = first.shape[1]
    size = kb // 2
    middle = kb * nb // wp // 2
    for t in range(2 * nb // wp):
        at = t * size + (16 if t * size >= middle else 0)
        value = qkv[t % 2 * size : (t % 2 + 1) * size, t // 2 * wp : (t // 2 + 1) * wp]
        first[at : at + size, :] = value
    first[middle : middle + 16, :] = small[...]
    first[2 * middle + 16 :, :] = jnp.zeros_like(small)
    lay(second, 0, up)
    lay(second, up.shape[0] * up.shape[1] // wp, out)
    lay(third, 0, down)


def pieces(qkv, out, up, down, small):
    wp = small.shape[1]
    talls = (qkv.size // wp + 32, (up.size + out.size) // wp, down.size // wp)
    return call(
        pieces_body,
        "pieces",
        (1,),
        [whole(w.shape) for w in (qkv, out, up, down, small)],
        [whole((tall, wp)) for tall in talls],
        [shaped((tall, wp), BF16) for tall in talls],
        nbytes=4 * sum(talls) * wp,
        vmem=60,
    )(qkv, out, up, down, small)


def gathered(flat, rs, cs):
    return lax.all_gather(flat, BOTH, axis=0, tiled=True).reshape(rs, cs, *flat.shape)


def shifted(value, part, shift, rs, cs):
    side = math.isqrt(rs)
    if part == "x":
        moves = [(r, r // side * side + (r + shift) % side) for r in range(rs)]
    elif part == "y":
        moves = [(r, (r + shift * side) % rs) for r in range(rs)]
    else:
        moves = [(c, (c + 2 * shift) % cs) for c in range(cs)]
    return lax.ppermute(value, "col" if part == "z" else "row", moves)


def permuted(flat, rs, cs, during):
    side, zs = math.isqrt(rs), cs // 2
    line = [flat] + [shifted(flat, "z", i, rs, cs) for i in range(1, zs)]
    line[0] = tied(flat, during[0])
    tall = flat.shape[0] // 2
    held = [jnp.stack([part[h * tall : (h + 1) * tall] for part in line])[None] for h in range(2)]
    for order in ("xy", "yx"):
        moved = [
            [shifted(h, part, i, rs, cs) for i in range(1, side)] for h, part in zip(held, order)
        ]
        if order == "xy":
            done, result = during[1](held[0])
        else:
            done, result = during[2](held[0], result)
        held[0] = tied(held[0], done)
        held = [jnp.concatenate([h] + m) for h, m in zip(held, moved)]
    pairs = [(c, c ^ 1) for c in range(cs)]
    return held + [lax.ppermute(h, "col", pairs) for h in held], result


def spots_of(rs, cs):
    side, zs = math.isqrt(rs), cs // 2
    row, column = lax.axis_index("row"), lax.axis_index("col")
    r, z = jnp.arange(rs), jnp.arange(zs)
    y, x = (row // side - r // side) % side, (row - r) % side
    table = jnp.zeros((4, max(rs, zs)), jnp.int32)
    table = table.at[0, :rs].set(y * side + x).at[1, :rs].set(x * side + y)
    return table.at[2, :].set(column % 2).at[3, :zs].set((column // 2 - z) % zs)


def local(
    tokens,
    router_weight,
    norm_first,
    qkv_weight,
    out_weight,
    norm_second,
    up_weight,
    down_weight,
    route_index,
    out_cotangent,
    rs,
    cs,
):
    seqs, routed = route_index.shape
    width = tokens.shape[1]
    index = route_index.reshape(seqs, 1, routed)
    column = lax.axis_index("col")
    core, depth = column % 2, column // 2
    zs = cs // 2
    bit = core.astype(jnp.int32).reshape(1)
    pairs = [(c, c ^ 1) for c in range(cs)]
    blocks = [w.shape for w in (qkv_weight, out_weight, up_weight, down_weight)]
    shape_qkv, shape_out, shape_up, shape_down = ((rs, cs) + b for b in blocks)
    wp = math.gcd(128, *(b[1] for b in blocks))
    tall_qkv, tall_out, tall_up, tall_down = (b[0] * b[1] // wp for b in blocks)

    spots = spots_of(rs, cs)
    small = jnp.concatenate([router_weight, norm_first, norm_second])
    small = jnp.pad(small.reshape(1, -1), ((0, 15), (0, wp - small.shape[0])))
    flat, next_flat, down_flat = pieces(qkv_weight, out_weight, up_weight, down_weight, small)

    def pick_first(dep):
        result = pick("pick_first", out_cotangent, index, True, 0, seqs // 3, deps=(dep,))
        return result[0], result

    def pick_rest(dep, begun):
        result = pick("pick_rest", out_cotangent, index, True, seqs // 3, None, begun, deps=(dep,))
        return result[0], result

    picked = pick("pick", tokens, index, False)
    parts, (grows, base) = permuted(flat, rs, cs, (picked, pick_first, pick_rest))
    next_parts = gathered(next_flat, rs, cs)
    down_parts = gathered(down_flat, rs, cs)

    def exchanged(send):
        return lax.ppermute(send, "col", pairs)

    def by_row(keep):
        r, z, tall, _ = keep.shape
        mine = lax.psum_scatter(
            keep.reshape(r * z * tall, wp), "row", scatter_dimension=0, tiled=True
        )
        return mine.reshape(z, tall, wp)

    def depth_parts(mine):
        return [
            lax.dynamic_index_in_dim(mine, (depth + shift) % zs, 0, keepdims=False)
            for shift in range(zs)
        ]

    def depth_sum(parts, *deps):
        total = (tied(parts[0], *deps) if deps else parts[0]).astype(F32)
        for shift in range(1, zs):
            total = total + shifted(parts[shift], "z", shift, rs, cs).astype(F32)
        return total

    def block(total, shape):
        kb, nb = shape[2:]
        return jnp.concatenate([total[i : i + kb] for i in range(0, kb * nb // wp, kb)], axis=1)

    projected, w_qkv, normed, gmlp, gate, small = project(
        spots, picked, grows, parts, blocks[0][0], blocks[0][1] // wp
    )
    router, first_gain, second_gain = small[0:1], small[1:2], small[2:3]
    context, probs = attend(projected, seqs)
    attn, normed_mid, w_out = mix(
        context, next_parts, tall_up // tall_out, tall_out, blocks[1][0], picked, second_gain, 3
    )
    hidden, slope, w_up, down_send, down_keep = raised(
        bit, normed_mid, gmlp, next_parts, 0, tall_up, blocks[2][0], shape_down
    )
    down_keep = joined([down_keep], [exchanged(down_send)])
    down_rows = by_row(down_keep)

    w_down, dots, up_send, up_keep, gnormed = feed_back(
        bit, grows, down_parts, slope, hidden, gate, normed_mid, w_up,
        blocks[3][0], blocks[2][0], deps=(down_keep,),
    )
    gmid, gcontext, logit, gsmall, out_send, out_keep = context_back(
        bit, gnormed, attn, picked, grows, gate, dots, context, second_gain, w_out, shape_out, wp, 3
    )
    up_keep = joined(
        [up_keep, out_keep], [exchanged(up_send), exchanged(out_send)], deps=(gcontext,)
    )
    up_rows = by_row(up_keep)
    down_sums = depth_parts(down_rows)

    gproj = attend_back(projected, gcontext, probs, seqs, deps=(up_keep, *down_sums))
    down_total = depth_sum(down_sums, gproj)
    qkv_send, qkv_keep, little_send, little_keep = qkv_weight_grad(
        bit, normed, gproj, w_qkv, gsmall, first_gain, shape_qkv, wp, 4, deps=(down_total,)
    )
    qkv_keep = joined(
        [qkv_keep, little_keep], [exchanged(qkv_send), exchanged(little_send)]
    )
    qkv_rows = by_row(qkv_keep)

    up_parts = depth_parts(up_rows)
    starts = jnp.arange(seqs, dtype=jnp.int32) * (tokens.shape[0] // seqs)
    places = (route_index + starts[:, None]).reshape(-1)
    input_grad = picked_back(
        places, gproj, w_qkv, picked, gmid, logit, grows, first_gain, router, base, 256,
        deps=(qkv_keep, *up_parts),
    )
    kept = lowered(hidden, w_down, attn, picked, gate, 256, deps=(input_grad,))
    up_total = depth_sum(up_parts, kept)
    qkv_parts = depth_parts(qkv_rows)
    output = place(tokens, index, kept, deps=(up_total, *qkv_parts))
    down_grad, up_grad = block(down_total, shape_down), block(up_total[:tall_up], shape_up)
    qkv_total = depth_sum(qkv_parts, output)
    out_grad = block(up_total[tall_up:], shape_out)
    qkv_grad = block(qkv_total[:tall_qkv], shape_qkv)
    sums = qkv_total[tall_qkv, : 3 * width // (rs * cs)].reshape(3, -1)
    return (
        output,
        input_grad,
        sums[1],
        sums[2],
        qkv_grad,
        out_grad,
        sums[0],
        up_grad,
        down_grad,
    )


def solution(mesh):
    both, by_row, by_col = P(BOTH), P("row", "col"), P("col", "row")
    tall = P(BOTH, None)
    return jax.shard_map(
        functools.partial(local, rs=mesh.shape["row"], cs=mesh.shape["col"]),
        mesh=mesh,
        in_specs=(tall, both, both, by_row, by_col, both, by_row, by_col, tall, tall),
        out_specs=(tall, tall, both, both, by_row, by_col, both, by_row, by_col),
        check_vma=False,
    )
```

time: 450 us -> 417 us (0.927)
  Pallas kernels: 314 us -> 277 us
  waiting for transfers between devices: 19.7 us -> 56.1 us
  blocking collectives: 28.5 us -> 0 us
    pallas_call x22 -> x24, Pallas kernels: 314 us -> 277 us  [call(): return lambda *args: made(*args, *deps)]
    all_gather x2 -> x0, blocking collectives: 28.5 us -> none  [local(): small = lax.all_gather(lax.all_gather(small, 'col', axis=0), 'row', axis=0)]
    ppermute x5, waiting for transfers between devices: 2.6 us -> 18 us  [exchanged(): return lax.ppermute(send, 'col', pairs)]
    all_gather x2, waiting for transfers between devices: 0.32 us -> 15.5 us  [gathered(): lax.all_gather(flat, BOTH, axis=0, tiled=True).reshape(rs, cs, *flat.shape)]
    unnamed x29 -> x50, local copies, waits for them, and re-layouts: 9.48 us -> 13.8 us
  transfers between devices with their start and end apart: 28 -> 28, of which waited for: 6 -> 10; matrix products, arithmetic and copies ran while one was open for 5% -> 5% of each run, Pallas kernels for 69% -> 66%
where the time goes in v2:
time: 417 us; the launch traced here: 415 us
  Pallas kernels  277 us (66%)
  waiting for transfers between devices  56.1 us (13%)
  starting transfers between devices  29.5 us (7%)
  local copies, waits for them, and re-layouts  25 us (6%)
  between operations  14.2 us (3%)
  other arithmetic  13.7 us (3%)
    pallas_call x24, Pallas kernels, call(): return lambda *args: made(*args, *deps)  277 us
    ppermute x16, starting transfers between devices, shifted(): return lax.ppermute(value, 'col' if part == 'z' else 'row', moves)  27.7 us
    ppermute x5, waiting for transfers between devices, exchanged(): return lax.ppermute(send, 'col', pairs)  18 us
    all_gather x2, waiting for transfers between devices, gathered(): lax.all_gather(flat, BOTH, axis=0, tiled=True).reshape(rs, cs, *flat.shape)  15.5 us
    unnamed x50, local copies, waits for them, and re-layouts  13.8 us
    ppermute x16, waiting for transfers between devices, shifted(): return lax.ppermute(value, 'col' if part == 'z' else 'row', moves)  12 us
  transfers between devices with their start and end apart: 28, of which 10 were waited for; matrix products, arithmetic and copies ran while one was open for 5% of the time, Pallas kernels for 66%

profile of v2, /device:TPU:0, one launch (start us, length us, event | category | flops | bytes accessed | tf_op | source)
XLA Modules:
  0.0 415.4 jit_solution(15705582297039285652)
XLA Ops:
  8.6 2.2 pieces.1
  11.6 3.1 collective-permute-start
  14.7 2.6 collective-permute-start.1
  19.9 12.0 %pick.1.refs_1_.refs_2_.refs_3_.refs_6_ = bf16[1152,1024]{1,0:T(8,128)(2,1)} custom-call(s32[9,1,128]{2,1,0:T(1,128)} %reshape.262.refs_0_, bf16[9216,1024]{1,0:T(8,128)(2,1)} %refs_1_.9), custom_call_target="tpu_custom_call" | custom-call | flops 2415919104 | bytes 56623104 | tf_op jit(solution)/shard_map/pick/pallas_call | solution.py:56
  31.9 3.1 collective-permute-done.1
  36.1 1.5 collective-permute-start.3
  37.7 1.6 collective-permute-start.5
  39.3 8.1 %pick_first.1 = (bf16[1152,1024]{1,0:T(8,128)(2,1)}, f32[9216,1024]{1,0:T(8,128)}) custom-call(s32[9,1,128]{2,1,0:T(1,128)} %reshape.262.refs_0_, bf16[9216,1024]{1,0:T(8,128)(2,1)} %refs_1_.8, bf16[1,4,400,128]{3,2,1,0:T(8,128)(2,1)} %copy-done.9), custom_call_target="tpu_custom_call" | custom-call | flops 2415919104 | bytes 56623104 | tf_op jit(solution)/shard_map/pick_first/pallas_call | solution.py:56
  48.5 1.7 collective-permute-start.4
  51.2 1.5 collective-permute-start.6
  52.7 14.9 %pick_rest.1 = (bf16[1152,1024]{1,0:T(8,128)(2,1)}, f32[9216,1024]{1,0:T(8,128)}) custom-call(s32[9,1,128]{2,1,0:T(1,128)} %reshape.262.refs_0_, bf16[9216,1024]{1,0:T(8,128)(2,1)} %refs_1_.8, bf16[1152,1024]{1,0:T(8,128)(2,1)} %get-tuple-element.96.refs_1_.refs_2_, ...), custom_call_target="tpu_custom_call", output_to_operand_aliasing={{0}: (2, {}), {1}: (3, {})} | custom-call | flops 2415919104 | bytes 56623104 | tf_op jit(solution)/shard_map/pick_rest/pallas_call | solution.py:56
  67.6 4.2 %collective-permute-done.4 = bf16[2,4,400,128]{3,2,1,0:T(8,128)(2,1)S(1)} collective-permute-done((bf16[2,4,400,128]{3,2,1,0:T(8,128)(2,1)S(1)}, bf16[2,4,400,128]{3,2,1,0:T(8,128)(2,1)S(1)}, u32[]{:S(2)}, u32[]{:S(2)}) %collective-permute-start.4) | collective-permute-done | bytes 819232 | tf_op jit(solution)/shard_map/ppermute | solution.py:926
  72.7 1.5 pad_maximum_fusion.refs_3_.refs_7_
  74.3 2.1 collective-permute-done.6
  77.9 5.8 %collective-permute-done.8.refs_6_ = bf16[4,4,400,128]{3,2,1,0:T(8,128)(2,1)} collective-permute-done((bf16[4,4,400,128]{3,2,1,0:T(8,128)(2,1)}, bf16[4,4,400,128]{3,2,1,0:T(8,128)(2,1)}, u32[]{:S(2)}, u32[]{:S(2)}) %collective-permute-start.8) | collective-permute-done | bytes 1638432 | tf_op jit(solution)/shard_map/ppermute | solution.py:946
  83.8 17.1 %project.1 = (bf16[1152,3072]{1,0:T(8,128)(2,1)}, bf16[1024,3072]{1,0:T(8,128)(2,1)}, bf16[1152,1024]{1,0:T(8,128)(2,1)}, bf16[1152,1024]{1,0:T(8,128)(2,1)}, f32[1152,1]{1,0:T(8,128)}, /*index=5*/f32[3,1024]{1,0:T(4,128)}) custom-call(s32[4,4]{1,0:T(4,128)} %copy-done.24, bf16[1152,1024]{1,0:T(8,128)(2,1)} %pick.1.refs_1_.refs_2_.refs_3_.refs_6_, ...), custom_call_target="tpu_custom_call" | custom-call | flops 7247757312 | bytes 29097984 | tf_op jit(solution)/shard_map/project/pallas_call | solution.py:56
  102.3 11.3 %attend.1 = (bf16[1152,1024]{1,0:T(8,128)(2,1)}, bf16[9,2048,128]{2,1,0:T(8,128)(2,1)}) custom-call(bf16[1152,3072]{1,0:T(8,128)(2,1)} %get-tuple-element.99.refs_0_), custom_call_target="tpu_custom_call" | custom-call | flops 9059696640 | bytes 28311552 | tf_op jit(solution)/shard_map/attend/pallas_call | solution.py:56
  113.6 8.6 %mix.1 = (f32[1152,1024]{1,0:T(8,128)}, bf16[1152,1024]{1,0:T(8,128)(2,1)}, bf16[1024,1024]{1,0:T(8,128)(2,1)}) custom-call(bf16[1152,1024]{1,0:T(8,128)(2,1)} %get-tuple-element.100.refs_0_.refs_7_, bf16[4,8,1280,128]{3,2,1,0:T(8,128)(2,1)} %bitcast.65, bf16[1152,1024]{1,0:T(8,128)(2,1)} %pick.1.refs_1_.refs_2_.refs_3_.refs_6_, ...), custom_call_target="tpu_custom_call" | custom-call | flops 2415919104 | bytes 16515072 | tf_op jit(solution)/shard_map/mix/pallas_call | solution.py:56
  122.2 39.9 %raise.1 = (bf16[1152,4096]{1,0:T(8,128)(2,1)}, bf16[1152,4096]{1,0:T(8,128)(2,1)}, bf16[1024,4096]{1,0:T(8,128)(2,1)}, bf16[4,4,1024,128]{3,2,1,0:T(8,128)(2,1)}, bf16[4,4,1024,128]{3,2,1,0:T(8,128)(2,1)}) custom-call(s32[1]{0:T(128)} %bitcast.refs_0_, bf16[1152,1024]{1,0:T(8,128)(2,1)} %get-tuple-element.103.refs_1_.refs_6_, ...), custom_call_target="tpu_custom_call" | custom-call | flops 24159191040 | bytes 46399488 | tf_op jit(solution)/shard_map/raise/pallas_call | solution.py:56
  162.2 10.0 %collective-permute-done.9.refs_1_ = bf16[4,4,1024,128]{3,2,1,0:T(8,128)(2,1)S(1)} collective-permute-done((bf16[4,4,1024,128]{3,2,1,0:T(8,128)(2,1)}, bf16[4,4,1024,128]{3,2,1,0:T(8,128)(2,1)S(1)}, u32[]{:S(2)}, u32[]{:S(2)}) %collective-permute-start.9) | collective-permute-done | bytes 4194336 | tf_op jit(solution)/shard_map/ppermute | solution.py:1005
  172.2 2.2 copy-done.3
  175.5 2.0 copy-done.1
  177.7 15.5 %all-gather.5.cloned.1.call-done = bf16[32768,128]{1,0:T(8,128)(2,1)} async-done(((bf16[1024,128]{1,0:T(8,128)(2,1)}), bf16[32768,128]{1,0:T(8,128)(2,1)}) %all-gather.5.cloned.1.call-update) | async-done | bytes 8388624 | tf_op jit(solution)/shard_map/all_gather | solution.py:915
  193.2 48.1 %feed_back.1 = (bf16[4096,1024]{1,0:T(8,128)(2,1)}, f32[1152,128]{1,0:T(8,128)}, bf16[4,4,1024,128]{3,2,1,0:T(8,128)(2,1)}, bf16[4,4,1024,128]{3,2,1,0:T(8,128)(2,1)}, f32[1152,1024]{1,0:T(8,128)}) custom-call(s32[1]{0:T(128)} %bitcast.refs_0_, bf16[1152,1024]{1,0:T(8,128)(2,1)} %get-tuple-element.98.refs_1_.refs_2_.refs_4_.refs_8_, ...), custom_call_target="tpu_custom_call" | custom-call | flops 28991029248 | bytes 53477376 | tf_op jit(solution)/shard_map/feed_back/pallas_call | solution.py:56
  241.7 18.9 %context_back.1 = (f32[1152,1024]{1,0:T(8,128)}, bf16[1152,1024]{1,0:T(8,128)(2,1)}, f32[1152,1]{1,0:T(8,128)}, f32[2,1024]{1,0:T(2,128)}, bf16[4,4,256,128]{3,2...) custom-call(s32[1]{0:T(128)} %bitcast.refs_0_, f32[1152,1024]{1,0:T(8,128)} %get-tuple-element.114.refs_1_, ...), custom_call_target="tpu_custom_call" | custom-call | flops 4831838208 | bytes 36962304 | tf_op jit(solution)/shard_map/context_back/pallas_call | solution.py:56
  260.9 2.6 collective-permute-done.11.refs_3_
  263.5 1.7 copy-done.5
  266.4 3.6 join.4.refs_3_
  270.0 2.3 copy-done
  272.5 2.0 dynamic-slice_bitcast_fusion.4
  274.4 1.6 collective-permute-start.12
  277.0 2.4 collective-permute-start.14
  279.4 14.2 %attend_back.1.refs_1_.refs_2_ = bf16[1152,3072]{1,0:T(8,128)(2,1)} custom-call(bf16[1152,3072]{1,0:T(8,128)(2,1)} %get-tuple-element.99.refs_0_, bf16[1152,1024]{1,0:T(8,128)(2,1)} %get-tuple-element.117.refs_4_.refs_1_, bf16[9,2048,128]{2,1,0:T(8,128)(2,1)} %get-tuple-element.118.refs_2_, bf16[4,4,1280,128]{3,2,1,0:T(8,128)(2,1)} %copy-done, ...), custom_call_target="tpu_custom_call" | custom-call | flops 18119393280 | bytes 56623104 | tf_op jit(solution)/shard_map/attend_back/pallas_call | solution.py:56
  293.6 2.6 collective-permute-done.13
  296.1 1.9 convert_add_fusion.1.refs_6_
  298.0 17.0 %qkv_grad.1 = (bf16[4,4,768,128]{3,2,1,0:T(8,128)(2,1)}, bf16[4,4,768,128]{3,2,1,0:T(8,128)(2,1)}, bf16[4,4,16,128]{3,2,1,0:T(8,128)(2,1)}, bf16[4,4,16,128]{3,2,1,0:T(8,128)(2,1)}) custom-call(s32[1]{0:T(128)} %bitcast.refs_0_, bf16[1152,1024]{1,0:T(8,128)(2,1)} %get-tuple-element.127.refs_1_, bf16[1152,3072]{1,0:T(8,128)(2,1)} %attend_back.1.refs_1_.refs_2_, ...), custom_call_target="tpu_custom_call" | custom-call | flops 7247757312 | bytes 22020096 | tf_op jit(solution)/shard_map/qkv_grad/pallas_call | solution.py:56
  315.6 5.5 %collective-permute-done.16.refs_3_ = bf16[4,4,16,128]{3,2,1,0:T(8,128)(2,1)S(1)} collective-permute-done((bf16[4,4,16,128]{3,2,1,0:T(8,128)(2,1)}, bf16[4,4,16,128]{3,2,1,0:T(8,128)(2,1)S(1)}, u32[]{:S(2)}, u32[]{:S(2)}) %collective-permute-start.16) | collective-permute-done | bytes 65568 | tf_op jit(solution)/shard_map/ppermute | solution.py:1005
  321.0 2.0 copy-done.4
  323.9 2.5 join.5.refs_10_
  328.6 3.9 reduce-scatter.6.cloned.1.call-done
  332.6 2.1 dynamic-slice_bitcast_fusion
  334.7 2.0 collective-permute-start.17
  336.6 2.0 collective-permute-start.18
  340.1 21.6 %picked_back.1.refs_5_ = f32[9216,1024]{1,0:T(8,128)} custom-call(s32[1152]{0:T(1024)} %add_bitcast_fusion.refs_0_, bf16[1152,3072]{1,0:T(8,128)(2,1)} %attend_back.1.refs_1_.refs_2_, bf16[1024,3072]{1,0:T(8,128)(2,1)} %get-tuple-element.123.refs_3_.refs_2_, f32[1152,1]{1,0:T(8,128)} %get-tuple-element.124.refs_3_, ...), custom_call_target="tpu_custom_call", output_to_operand_aliasing={{}: (9, {})} | custom-call | flops 7247757312 | bytes 25165824 | tf_op jit(solution)/shard_map/picked_back/pallas_call | solution.py:56
  361.7 17.1 %lower.1.refs_1_.refs_2_ = bf16[1152,1024]{1,0:T(8,128)(2,1)} custom-call(bf16[1152,4096]{1,0:T(8,128)(2,1)} %get-tuple-element.105.refs_4_.refs_0_, bf16[4096,1024]{1,0:T(8,128)(2,1)} %get-tuple-element.112.refs_1_, f32[1152,1024]{1,0:T(8,128)} %get-tuple-element.113.refs_2_, bf16[1152,1024]{1,0:T(8,128)(2,1)} %pick.1.refs_1_.refs_2_.refs_3_.refs_6_, ...), custom_call_target="tpu_custom_call" | custom-call | flops 9663676416 | bytes 27262976 | tf_op jit(solution)/shard_map/lower/pallas_call | solution.py:56
  381.6 2.0 dynamic-slice_bitcast_fusion.8
  384.0 2.1 collective-permute-start.21
  387.6 18.9 %place.1.refs_1_ = bf16[9216,1024]{1,0:T(8,128)(2,1)} custom-call(s32[9,1,128]{2,1,0:T(1,128)} %reshape.262.refs_0_, bf16[9216,1024]{1,0:T(8,128)(2,1)} %refs_1_.9, bf16[1152,1024]{1,0:T(8,128)(2,1)} %lower.1.refs_1_.refs_2_, f32[1280,128]{1,0:T(8,128)} %copy-done.10, bf16[784,128]{1,0:T(8,128)(2,1)} %get-tuple-element.144.refs_4_.refs_0_, ...), custom_call_target="tpu_custom_call" | custom-call | flops 2415919104 | bytes 37748736 | tf_op jit(solution)/shard_map/place/pallas_call | solution.py:56
  (125 shorter events, 28.5 us)
Async XLA Ops:
  7.2 106.4 %all-gather.3.cloned.1.call-start = ((), (), s32[]{:S(2)}) async-start(), calls=%async_computation.3 | async-start | bytes 10813440 | tf_op jit(solution)/shard_map/all_gather | solution.py:915
  10.8 182.4 %all-gather.5.cloned.1.call-start = ((), (), s32[]{:S(2)}) async-start(), calls=%async_computation.4 | async-start | bytes 8650752 | tf_op jit(solution)/shard_map/all_gather | solution.py:915
  11.5 260.9 %reduce-scatter.4.cloned.1.call-start = ((), (), s32[]{:S(2)}) async-start(), calls=%async_computation.5 | async-start | bytes 5242880 | tf_op jit(solution)/shard_map/reduce_scatter | solution.py:1009
  11.6 20.3 %collective-permute-start = (bf16[800,128]{1,0:T(8,128)(2,1)}, bf16[800,128]{1,0:T(8,128)(2,1)S(1)}, u32[]{:S(2)}, u32[]{:S(2)}) collective-permute-start(bf16[800,128]{1,0:T(8,128)(2,1)} %get-tuple-element.95.refs_0_), channel_id=1, source_target_pairs={{0,2},{1,3},{2,4},{3,5},{4,6},{5,7},{6,0},{7,1},{8,10},{9,11},{10,... | collective-permute-start | bytes 614408 | tf_op jit(solution)/shard_map/ppermute | solution.py:926
  14.7 20.3 %collective-permute-start.1 = (bf16[800,128]{1,0:T(8,128)(2,1)}, bf16[800,128]{1,0:T(8,128)(2,1)S(1)}, u32[]{:S(2)}, u32[]{:S(2)}) collective-permute-start(bf16[800,128]{1,0:T(8,128)(2,1)} %get-tuple-element.95.refs_0_), channel_id=1, source_target_pairs={{0,4},{1,5},{2,6},{3,7},{4,0},{5,1},{6,2},{7,3},{8,12},{9,13},{10,... | collective-permute-start | bytes 614408 | tf_op jit(solution)/shard_map/ppermute | solution.py:926
  17.3 17.7 %collective-permute-start.2 = (bf16[800,128]{1,0:T(8,128)(2,1)}, bf16[800,128]{1,0:T(8,128)(2,1)S(1)}, u32[]{:S(2)}, u32[]{:S(2)}) collective-permute-start(bf16[800,128]{1,0:T(8,128)(2,1)} %get-tuple-element.95.refs_0_), channel_id=1, source_target_pairs={{0,6},{1,7},{2,0},{3,1},{4,2},{5,3},{6,4},{7,5},{8,14},{9,15},{10,... | collective-permute-start | bytes 614408 | tf_op jit(solution)/shard_map/ppermute | solution.py:926
  36.1 3.2 copy-start.9
  36.1 11.3 %collective-permute-start.3 = (bf16[1,4,400,128]{3,2,1,0:T(8,128)(2,1)S(1)}, bf16[1,4,400,128]{3,2,1,0:T(8,128)(2,1)S(1)}, u32[]{:S(2)}, u32[]{:S(2)}) collective-permute-start(bf16[1,4,400,128]{3,2,1,0:T(8,128)(2,1)S(1)} %maximum_bitcast_fusion.refs_2_.refs_0_), channel_id=1, source_target_pairs={{0,8},{8,0},{16,24},{24,16},{1,9},{9,1},{17,25},{25,17},{2,10},{10... | collective-permute-start | bytes 1228808 | tf_op jit(solution)/shard_map/ppermute | solution.py:926
  37.7 12.6 %collective-permute-start.5 = (bf16[1,4,400,128]{3,2,1,0:T(8,128)(2,1)S(1)}, bf16[1,4,400,128]{3,2,1,0:T(8,128)(2,1)S(1)}, u32[]{:S(2)}, u32[]{:S(2)}) collective-permute-start(bf16[1,4,400,128]{3,2,1,0:T(8,128)(2,1)S(1)} %maximum_bitcast_fusion.1), channel_id=1, source_target_pairs={{0,16},{8,24},{16,0},{24,8},{1,17},{9,25},{17,1},{25,9},{2,18},{10... | collective-permute-start | bytes 1228808 | tf_op jit(solution)/shard_map/ppermute | solution.py:926
  48.5 4.2 %copy-start.8 = (bf16[2,4,400,128]{3,2,1,0:T(8,128)(2,1)}, bf16[2,4,400,128]{3,2,1,0:T(8,128)(2,1)S(1)}, u32[]{:S(2)}) copy-start(bf16[2,4,400,128]{3,2,1,0:T(8,128)(2,1)S(1)} %pad_maximum_fusion.2.refs_4_.refs_0_) | copy-start | bytes 2457604
  48.5 23.2 %collective-permute-start.4 = (bf16[2,4,400,128]{3,2,1,0:T(8,128)(2,1)S(1)}, bf16[2,4,400,128]{3,2,1,0:T(8,128)(2,1)S(1)}, u32[]{:S(2)}, u32[]{:S(2)}) collective-permute-start(bf16[2,4,400,128]{3,2,1,0:T(8,128)(2,1)S(1)} %pad_maximum_fusion.2.refs_4_.refs_0_), channel_id=1, source_target_pairs={{0,16},{8,24},{16,0},{24,8},{1,17},{9,25},{17,1},{25,9},{2,18},{10... | collective-permute-start | bytes 2457608 | tf_op jit(solution)/shard_map/ppermute | solution.py:926
  51.2 25.2 %collective-permute-start.6 = (bf16[2,4,400,128]{3,2,1,0:T(8,128)(2,1)}, bf16[2,4,400,128]{3,2,1,0:T(8,128)(2,1)S(1)}, u32[]{:S(2)}, u32[]{:S(2)}) collective-permute-start(bf16[2,4,400,128]{3,2,1,0:T(8,128)(2,1)} %pad_maximum_fusion.3), channel_id=1, source_target_pairs={{0,8},{8,0},{16,24},{24,16},{1,9},{9,1},{17,25},{25,17},{2,10},{10... | collective-permute-start | bytes 2457608 | tf_op jit(solution)/shard_map/ppermute | solution.py:926
  74.2 9.6 %copy-start.12 = (bf16[4,4,400,128]{3,2,1,0:T(8,128)(2,1)}, bf16[4,4,400,128]{3,2,1,0:T(8,128)(2,1)S(1)}, u32[]{:S(2)}) copy-start(bf16[4,4,400,128]{3,2,1,0:T(8,128)(2,1)S(1)} %pad_maximum_fusion.refs_3_.refs_7_) | copy-start | bytes 4915204
  74.2 3.7 collective-permute-start.7
  77.7 6.0 %collective-permute-start.8 = (bf16[4,4,400,128]{3,2,1,0:T(8,128)(2,1)}, bf16[4,4,400,128]{3,2,1,0:T(8,128)(2,1)}, u32[]{:S(2)}, u32[]{:S(2)}) collective-permute-start(bf16[4,4,400,128]{3,2,1,0:T(8,128)(2,1)} %pad_maximum_fusion.1.refs_4_), channel_id=1, source_target_pairs={{0,1},{1,0},{2,3},{3,2},{4,5},{5,4},{6,7},{7,6},{8,9},{9,8},{10,11... | collective-permute-start | bytes 4915208 | tf_op jit(solution)/shard_map/ppermute | solution.py:946
  77.9 5.8 %copy-start.24 = (s32[4,4]{1,0:T(4,128)}, s32[4,4]{1,0:T(4,128)S(1)}, u32[]{:S(2)}) copy-start(s32[4,4]{1,0:T(4,128)S(1)} %scatter.19.refs_0_) | copy-start | bytes 196
  162.1 10.1 %collective-permute-start.9 = (bf16[4,4,1024,128]{3,2,1,0:T(8,128)(2,1)}, bf16[4,4,1024,128]{3,2,1,0:T(8,128)(2,1)S(1)}, u32[]{:S(2)}, u32[]{:S(2)}) collective-permute-start(bf16[4,4,1024,128]{3,2,1,0:T(8,128)(2,1)} %get-tuple-element.111), channel_id=1, source_target_pairs={{0,1},{1,0},{2,3},{3,2},{4,5},{5,4},{6,7},{7,6},{8,9},{9,8},{10,11... | collective-permute-start | bytes 12582920 | tf_op jit(solution)/shard_map/ppermute | solution.py:1005
  172.2 2.2 copy-start.3
  175.5 2.0 copy-start.1
  177.5 155.1 %reduce-scatter.6.cloned.1.call-start = ((), (), s32[]{:S(2)}) async-start(), calls=%async_computation.6 | async-start | bytes 6553600 | tf_op jit(solution)/shard_map/reduce_scatter | solution.py:1009
  241.3 22.1 %collective-permute-start.10 = (bf16[4,4,1024,128]{3,2,1,0:T(8,128)(2,1)}, bf16[4,4,1024,128]{3,2,1,0:T(8,128)(2,1)}, u32[]{:S(2)}, u32[]{:S(2)}) collective-permute-start(bf16[4,4,1024,128]{3,2,1,0:T(8,128)(2,1)} %get-tuple-element.121), channel_id=1, source_target_pairs={{0,1},{1,0},{2,3},{3,2},{4,5},{5,4},{6,7},{7,6},{8,9},{9,8},{10,11... | collective-permute-start | bytes 12582920 | tf_op jit(solution)/shard_map/ppermute | solution.py:1005
  241.7 21.8 %copy-start.2 = (bf16[4,4,1024,128]{3,2,1,0:T(8,128)(2,1)S(1)}, bf16[4,4,1024,128]{3,2,1,0:T(8,128)(2,1)}, u32[]{:S(2)}) copy-start(bf16[4,4,1024,128]{3,2,1,0:T(8,128)(2,1)} %get-tuple-element.119.refs_0_) | copy-start | bytes 12582916
  260.6 2.9 collective-permute-start.11
  263.5 1.7 copy-start.5
  270.0 2.3 copy-start
  272.3 109.3 %reduce-scatter.8.cloned.1.call-start = ((), (), s32[]{:S(2)}) async-start(), calls=%async_computation.7 | async-start | bytes 4014080 | tf_op jit(solution)/shard_map/reduce_scatter | solution.py:1009
  274.4 5.0 %copy-start.20 = (bf16[1024,128]{1,0:T(8,128)(2,1)}, bf16[1024,128]{1,0:T(8,128)(2,1)S(1)}, u32[]{:S(2)}) copy-start(bf16[1024,128]{1,0:T(8,128)(2,1)S(1)} %get-tuple-element.137.refs_7_) | copy-start | bytes 786436
  274.4 5.0 %copy-start.21 = (bf16[1024,128]{1,0:T(8,128)(2,1)}, bf16[1024,128]{1,0:T(8,128)(2,1)S(1)}, u32[]{:S(2)}) copy-start(bf16[1024,128]{1,0:T(8,128)(2,1)S(1)} %get-tuple-element.138.refs_6_) | copy-start | bytes 786436
  274.4 5.0 %copy-start.22 = (bf16[1024,128]{1,0:T(8,128)(2,1)}, bf16[1024,128]{1,0:T(8,128)(2,1)S(1)}, u32[]{:S(2)}) copy-start(bf16[1024,128]{1,0:T(8,128)(2,1)S(1)} %get-tuple-element.139.refs_5_) | copy-start | bytes 786436
  274.4 19.1 %collective-permute-start.12 = (bf16[1024,128]{1,0:T(8,128)(2,1)S(1)}, bf16[1024,128]{1,0:T(8,128)(2,1)S(1)}, u32[]{:S(2)}, u32[]{:S(2)}) collective-permute-start(bf16[1024,128]{1,0:T(8,128)(2,1)S(1)} %get-tuple-element.139.refs_5_), channel_id=1, source_target_pairs={{0,2},{1,3},{2,4},{3,5},{4,6},{5,7},{6,0},{7,1},{8,10},{9,11},{10,... | collective-permute-start | bytes 786440 | tf_op jit(solution)/shard_map/ppermute | solution.py:926
  276.0 20.1 %collective-permute-start.13 = (bf16[1024,128]{1,0:T(8,128)(2,1)S(1)}, bf16[1024,128]{1,0:T(8,128)(2,1)S(1)}, u32[]{:S(2)}, u32[]{:S(2)}) collective-permute-start(bf16[1024,128]{1,0:T(8,128)(2,1)S(1)} %get-tuple-element.138.refs_6_), channel_id=1, source_target_pairs={{0,4},{1,5},{2,6},{3,7},{4,0},{5,1},{6,2},{7,3},{8,12},{9,13},{10,... | collective-permute-start | bytes 786440 | tf_op jit(solution)/shard_map/ppermute | solution.py:926
  277.0 19.2 %collective-permute-start.14 = (bf16[1024,128]{1,0:T(8,128)(2,1)S(1)}, bf16[1024,128]{1,0:T(8,128)(2,1)S(1)}, u32[]{:S(2)}, u32[]{:S(2)}) collective-permute-start(bf16[1024,128]{1,0:T(8,128)(2,1)S(1)} %get-tuple-element.137.refs_7_), channel_id=1, source_target_pairs={{0,6},{1,7},{2,0},{3,1},{4,2},{5,3},{6,4},{7,5},{8,14},{9,15},{10,... | collective-permute-start | bytes 786440 | tf_op jit(solution)/shard_map/ppermute | solution.py:926
  315.0 6.0 %collective-permute-start.15 = (bf16[4,4,768,128]{3,2,1,0:T(8,128)(2,1)}, bf16[4,4,768,128]{3,2,1,0:T(8,128)(2,1)S(1)}, u32[]{:S(2)}, u32[]{:S(2)}) collective-permute-start(bf16[4,4,768,128]{3,2,1,0:T(8,128)(2,1)} %get-tuple-element.131), channel_id=1, source_target_pairs={{0,1},{1,0},{2,3},{3,2},{4,5},{5,4},{6,7},{7,6},{8,9},{9,8},{10,11... | collective-permute-start | bytes 9437192 | tf_op jit(solution)/shard_map/ppermute | solution.py:1005
  315.1 6.0 %collective-permute-start.16 = (bf16[4,4,16,128]{3,2,1,0:T(8,128)(2,1)}, bf16[4,4,16,128]{3,2,1,0:T(8,128)(2,1)S(1)}, u32[]{:S(2)}, u32[]{:S(2)}) collective-permute-start(bf16[4,4,16,128]{3,2,1,0:T(8,128)(2,1)} %get-tuple-element.132), channel_id=1, source_target_pairs={{0,1},{1,0},{2,3},{3,2},{4,5},{5,4},{6,7},{7,6},{8,9},{9,8},{10,11... | collective-permute-start | bytes 196616 | tf_op jit(solution)/shard_map/ppermute | solution.py:1005
  321.0 2.0 copy-start.4
  334.7 5.4 %copy-start.13 = (bf16[1280,128]{1,0:T(8,128)(2,1)}, bf16[1280,128]{1,0:T(8,128)(2,1)S(1)}, u32[]{:S(2)}) copy-start(bf16[1280,128]{1,0:T(8,128)(2,1)S(1)} %get-tuple-element.133.refs_14_) | copy-start | bytes 983044
  334.7 5.4 %copy-start.14 = (bf16[1280,128]{1,0:T(8,128)(2,1)}, bf16[1280,128]{1,0:T(8,128)(2,1)S(1)}, u32[]{:S(2)}) copy-start(bf16[1280,128]{1,0:T(8,128)(2,1)S(1)} %get-tuple-element.134.refs_13_) | copy-start | bytes 983044
  334.7 5.4 %copy-start.15 = (bf16[1280,128]{1,0:T(8,128)(2,1)}, bf16[1280,128]{1,0:T(8,128)(2,1)S(1)}, u32[]{:S(2)}) copy-start(bf16[1280,128]{1,0:T(8,128)(2,1)S(1)} %get-tuple-element.135.refs_12_) | copy-start | bytes 983044
  334.7 44.1 %collective-permute-start.17 = (bf16[1280,128]{1,0:T(8,128)(2,1)S(1)}, bf16[1280,128]{1,0:T(8,128)(2,1)S(1)}, u32[]{:S(2)}, u32[]{:S(2)}) collective-permute-start(bf16[1280,128]{1,0:T(8,128)(2,1)S(1)} %get-tuple-element.135.refs_12_), channel_id=1, source_target_pairs={{0,2},{1,3},{2,4},{3,5},{4,6},{5,7},{6,0},{7,1},{8,10},{9,11},{10,... | collective-permute-start | bytes 983048 | tf_op jit(solution)/shard_map/ppermute | solution.py:926
  336.6 42.2 %collective-permute-start.18 = (bf16[1280,128]{1,0:T(8,128)(2,1)S(1)}, bf16[1280,128]{1,0:T(8,128)(2,1)S(1)}, u32[]{:S(2)}, u32[]{:S(2)}) collective-permute-start(bf16[1280,128]{1,0:T(8,128)(2,1)S(1)} %get-tuple-element.134.refs_13_), channel_id=1, source_target_pairs={{0,4},{1,5},{2,6},{3,7},{4,0},{5,1},{6,2},{7,3},{8,12},{9,13},{10,... | collective-permute-start | bytes 983048 | tf_op jit(solution)/shard_map/ppermute | solution.py:926
  338.6 40.2 %collective-permute-start.19 = (bf16[1280,128]{1,0:T(8,128)(2,1)S(1)}, bf16[1280,128]{1,0:T(8,128)(2,1)S(1)}, u32[]{:S(2)}, u32[]{:S(2)}) collective-permute-start(bf16[1280,128]{1,0:T(8,128)(2,1)S(1)} %get-tuple-element.133.refs_14_), channel_id=1, source_target_pairs={{0,6},{1,7},{2,0},{3,1},{4,2},{5,3},{6,4},{7,5},{8,14},{9,15},{10,... | collective-permute-start | bytes 983048 | tf_op jit(solution)/shard_map/ppermute | solution.py:926
  379.9 7.6 %copy-start.10 = (f32[1280,128]{1,0:T(8,128)}, f32[1280,128]{1,0:T(8,128)S(1)}, u32[]{:S(2)}) copy-start(f32[1280,128]{1,0:T(8,128)S(1)} %convert_add_fusion.refs_3_) | copy-start | bytes 1966084
  383.6 4.0 copy-start.17
  383.6 4.0 copy-start.18
  383.6 4.0 copy-start.19
  383.6 22.9 %collective-permute-start.20 = (bf16[784,128]{1,0:T(8,128)(2,1)S(1)}, bf16[784,128]{1,0:T(8,128)(2,1)S(1)}, u32[]{:S(2)}, u32[]{:S(2)}) collective-permute-start(bf16[784,128]{1,0:T(8,128)(2,1)S(1)} %get-tuple-element.143.refs_5_), channel_id=1, source_target_pairs={{0,2},{1,3},{2,4},{3,5},{4,6},{5,7},{6,0},{7,1},{8,10},{9,11},{10,... | collective-permute-start | bytes 602120 | tf_op jit(solution)/shard_map/ppermute | solution.py:926
  384.0 22.5 %collective-permute-start.21 = (bf16[784,128]{1,0:T(8,128)(2,1)S(1)}, bf16[784,128]{1,0:T(8,128)(2,1)S(1)}, u32[]{:S(2)}, u32[]{:S(2)}) collective-permute-start(bf16[784,128]{1,0:T(8,128)(2,1)S(1)} %get-tuple-element.142.refs_6_), channel_id=1, source_target_pairs={{0,4},{1,5},{2,6},{3,7},{4,0},{5,1},{6,2},{7,3},{8,12},{9,13},{10,... | collective-permute-start | bytes 602120 | tf_op jit(solution)/shard_map/ppermute | solution.py:926
  386.1 20.3 %collective-permute-start.22 = (bf16[784,128]{1,0:T(8,128)(2,1)S(1)}, bf16[784,128]{1,0:T(8,128)(2,1)S(1)}, u32[]{:S(2)}, u32[]{:S(2)}) collective-permute-start(bf16[784,128]{1,0:T(8,128)(2,1)S(1)} %get-tuple-element.141.refs_7_), channel_id=1, source_target_pairs={{0,6},{1,7},{2,0},{3,1},{4,2},{5,3},{6,4},{7,5},{8,14},{9,15},{10,... | collective-permute-start | bytes 602120 | tf_op jit(solution)/shard_map/ppermute | solution.py:926
  (5 other events, 5.0 us)
Sparse Core Ops, SparseCore 0:
  11.4 101.8 all-gather.2
  116.9 76.2 all-gather.4
  196.2 51.2 reduce-scatter.3
  272.4 60.1 reduce-scatter.5
  335.7 44.4 reduce-scatter.7

commit v3 on v2

--- a/solution.py
+++ b/solution.py
@@ -164,7 +164,7 @@
 
 def project_body(
     kb, wp, count, spots, picked, grows, own_a, own_b, other_a, other_b, own_s, other_s,
-    out, natural, normed, gmlp, gate, small,
+    out, natural, normed_turned, gmlp, gate, small, normed,
 ):
     rs, zs = own_s.shape[:2]
     tall = kb * count // 2
@@ -187,7 +187,9 @@
             value = picked[at, :].astype(F32)
             opened = jax.nn.sigmoid(jnp.sum(value * small[0:1, :], axis=-1, keepdims=True))
             inverse = lax.rsqrt(jnp.mean(value * value, axis=-1, keepdims=True) + EPSILON)
-            normed[at, :] = (value * inverse * small[1:2, :]).astype(BF16)
+            scaled = (value * inverse * small[1:2, :]).astype(BF16)
+            normed[at, :] = scaled
+            normed_turned[:, at] = scaled.T
             gmlp[at, :] = (grows[at, :].astype(F32) * opened).astype(BF16)
             gate[at, :] = opened
             return carry
@@ -221,7 +223,7 @@
         [
             pl.BlockSpec((rows, step), lambda j, _: (0, j)),
             pl.BlockSpec((depth, step), lambda j, _: (0, j)),
-            whole(picked.shape),
+            whole((depth, rows)),
             whole(picked.shape),
             whole((rows, 1)),
             whole((3, depth)),
@@ -229,11 +231,12 @@
         [
             shaped((rows, zs * step), BF16),
             shaped((depth, zs * step), BF16),
-            shaped(picked.shape, BF16),
+            shaped((depth, rows), BF16),
             shaped(picked.shape, BF16),
             shaped((rows, 1), F32),
             shaped((3, depth), F32),
         ],
+        [pltpu.VMEM((rows, depth), BF16)],
         prefetch=1,
         flops=2 * rows * depth * zs * step,
         nbytes=2 * (4 * picked.size + 2 * depth * zs * step + rows * zs * step),
@@ -298,7 +301,7 @@
     )(projected)
 
 
-def mix_body(kb, context, w, picked, gain, attn, normed, natural):
+def mix_body(kb, context, w, picked, gain, attn, normed, turned_out, natural):
     @pl.when(pl.program_id(0) == 0)
     def _():
         lay_cr(w, natural, kb)
@@ -307,7 +310,9 @@
     attn[...] = out
     middle = picked[...].astype(F32) + out
     inverse = lax.rsqrt(jnp.mean(middle * middle, axis=-1, keepdims=True) + EPSILON)
-    normed[...] = (middle * inverse * gain[...]).astype(BF16)
+    value = (middle * inverse * gain[...]).astype(BF16)
+    normed[...] = value
+    turned_out[...] = value.T
 
 
 def mix(context, w, at, tall, kb, picked, gain, steps):
@@ -319,8 +324,13 @@
         "mix",
         (steps,),
         [part, pl.BlockSpec((rs, cs, tall, wp), lambda s: (0, 0, at, 0)), part, whole(gain.shape)],
-        [part, part, whole((width, width))],
-        [shaped((rows, width), F32), shaped((rows, width), BF16), shaped((width, width), BF16)],
+        [part, part, pl.BlockSpec((width, rows // steps), lambda s: (0, s)), whole((width, width))],
+        [
+            shaped((rows, width), F32),
+            shaped((rows, width), BF16),
+            shaped((width, rows), BF16),
+            shaped((width, width), BF16),
+        ],
         flops=2 * rows * width * width,
         nbytes=14 * rows * width,
     )(context, w, picked, gain)
@@ -403,19 +413,6 @@
         send[at] = first
 
 
-def grad_rc(bit, total, send, keep, kb, nb):
-    rs, zs, _, wp = send.shape
-    for r in range(rs):
-        for j in range(zs):
-            for t in range(nb // wp):
-                at = 2 * j * nb + t * wp
-                down = slice(r * kb, (r + 1) * kb)
-                where = (r, j, slice(t * kb, (t + 1) * kb))
-                split_out(
-                    bit, total[down, at : at + wp], total[down, at + nb : at + nb + wp], keep, send, where
-                )
-
-
 def grad_cr(bit, total, send, keep, kb, nb):
     rs, zs, _, wp = send.shape
     for r in range(rs):
@@ -429,18 +426,44 @@
                 )
 
 
-def qkv_grad_body(
-    kb, nb, bit, x, y, w, gsmall, gain, send, keep, little_send, little_keep, first
-):
+def qkv_grad_body(kb, nb, last, many, bit, x, *refs):
+    y, w, refs = refs[:many], refs[many : 2 * many], refs[2 * many :]
+    if last:
+        gsmall, gain, before, out, little_send, little_keep, first, columns, weights = refs
+    else:
+        out, first, columns, weights = refs
     step = pl.program_id(0)
-    total = mul(x[...], y[...], TN)
+    rs, zs, _, wp = out.shape
+    side_here = bit[0] if last else 1 - bit[0]
+    if many > 1:
+        for j in range(zs):
+            columns[:, j * nb : (j + 1) * nb] = y[j][...]
+            weights[:, j * nb : (j + 1) * nb] = w[j][...]
+    else:
+        for side in range(2):
+
+            @pl.when(side_here == side)
+            def _():
+                for j in range(zs):
+                    source = slice((2 * j + side) * nb, (2 * j + side + 1) * nb)
+                    target = slice(j * nb, (j + 1) * nb)
+                    columns[:, target] = y[0][:, source]
+                    weights[:, target] = w[0][:, source]
 
     @pl.when(step == 0)
     def _():
-        first[...] = jnp.zeros_like(first)
-
-    first[...] += jnp.sum(total * w[...].astype(F32), axis=-1, keepdims=True)
-    grad_rc(bit[0], total.astype(BF16), send, keep, kb, nb)
+        first[...] = before[...] if last else jnp.zeros_like(first)
+
+    total = mul(x[...], columns[...])
+    first[...] += jnp.sum(total * weights[...].astype(F32), axis=-1, keepdims=True)
+    total = total.astype(BF16)
+    for r in range(rs):
+        for j in range(zs):
+            for t in range(nb // wp):
+                at = j * nb + t * wp
+                out[r, j, t * kb : (t + 1) * kb, :] = total[r * kb : (r + 1) * kb, at : at + wp]
+    if not last:
+        return
 
     @pl.when(step == pl.num_programs(0) - 1)
     def _():
@@ -466,8 +489,8 @@
                 split_out(bit[0], *pair, little_keep, little_send, (r, z))
 
 
-def qkv_weight_grad(bit, x, y, w, gsmall, gain, shape, wp, count, deps=()):
-    rows, depth = x.shape
+def qkv_weight_grad(name, bit, x, y, w, shape, wp, count, small=(), deps=()):
+    depth, rows = x.shape
     rs, cs, kb, nb = shape
     zs = cs // 2
     many = zs // count
@@ -475,30 +498,45 @@
     step = 2 * many * nb
     out = pl.BlockSpec((rs, many, tall, wp), lambda j, _: (0, j, 0, 0))
     little = (rs, zs, 16, wp)
-    return call(
-        functools.partial(qkv_grad_body, kb, nb),
-        "qkv_grad",
+    grad = shaped((rs, zs, tall, wp), BF16)
+    buffers = [pltpu.VMEM((rows, step // 2), BF16), pltpu.VMEM((depth, step // 2), BF16)]
+    column = pltpu.VMEM((depth, 1), F32)
+    if nb % 128 == 0:
+        fetched = many
+
+        def cut(tall, k):
+            def place_of(j, bit):
+                return 0, 2 * (many * j + k) + (bit[0] if small else 1 - bit[0])
+
+            return pl.BlockSpec((tall, nb), place_of)
+
+    else:
+        fetched = 1
+
+        def cut(tall, _):
+            return pl.BlockSpec((tall, step), lambda j, _: (0, j))
+
+    return call(
+        functools.partial(qkv_grad_body, kb, nb, bool(small), fetched),
+        name,
         (count,),
-        [
-            whole(x.shape),
-            pl.BlockSpec((rows, step), lambda j, _: (0, j)),
-            pl.BlockSpec((depth, step), lambda j, _: (0, j)),
-            whole(gsmall.shape),
-            whole(gain.shape),
-        ],
-        [out, out, whole(little), whole(little)],
-        [shaped((rs, zs, tall, wp), BF16)] * 2 + [shaped(little, BF16)] * 2,
-        [pltpu.VMEM((depth, 1), F32)],
+        [once(x.shape)]
+        + [cut(rows, k) for k in range(fetched)]
+        + [cut(depth, k) for k in range(fetched)]
+        + [whole(each.shape) for each in small],
+        [out, whole(little), whole(little)] if small else [out, whole((depth, 1))],
+        [grad] + ([shaped(little, BF16)] * 2 if small else [shaped((depth, 1), F32)]),
+        ([column] if small else []) + buffers,
         prefetch=1,
-        flops=2 * rows * depth * cs * nb,
-        nbytes=2 * (x.size + y.size + 2 * w.size),
+        flops=rows * depth * cs * nb,
+        nbytes=x.size + y.size + 2 * w.size,
         deps=deps,
-    )(bit, x, y, w, gsmall, gain)
+    )(bit, x, *[y] * fetched, *[w] * fetched, *small)
 
 
 def feed_back_body(
-    kb, ub, bit, grows, w, slope, hidden, gate, x, w_up,
-    natural, dots, send, keep, total, x_turned,
+    kb, ub, bit, grows, w, slope, hidden, gate, x_turned, w_up,
+    natural, dots, send, keep, total,
 ):
     rs, _, tall, wp = w.shape
     pieces_up = kb // wp
@@ -507,12 +545,11 @@
 
     @pl.when(step == 0)
     def _():
-        x_turned[...] = x[...].T
         dots[...] = jnp.zeros_like(dots)
         total[...] = jnp.zeros_like(total)
 
     def half(h, carry):
-        at = pl.ds(pl.multiple_of(h * kb, kb), kb)
+        at = slice(h * kb, (h + 1) * kb)
         back = mul(grows[...], natural[at, :], NT)
         gpre = (back * gate[...] * slope[:, at].astype(F32)).astype(BF16)
         product = back * hidden[:, at].astype(F32)
@@ -539,10 +576,11 @@
         total[...] += mul(gpre, w_up[:, at], NT)
         return carry
 
-    lax.fori_loop(0, 2, half, 0)
-
-
-def feed_back(bit, grows, w, slope, hidden, gate, x, w_up, kb, ub, deps=()):
+    half(0, 0)
+    half(1, 0)
+
+
+def feed_back(bit, grows, w, slope, hidden, gate, x_turned, w_up, kb, ub, deps=()):
     rows, width = grows.shape
     rs, cs, tall, wp = w.shape
     zs = cs // 2
@@ -556,7 +594,7 @@
         "feed_back",
         (zs,),
         [once(grows.shape), pl.BlockSpec((rs, 2, tall, wp), lambda j, _: (0, j, 0, 0)), cut, cut]
-        + [once(gate.shape), once(x.shape), pl.BlockSpec((width, fb), lambda j, _: (0, j))],
+        + [once(gate.shape), once(x_turned.shape), pl.BlockSpec((width, fb), lambda j, _: (0, j))],
         [
             pl.BlockSpec((fb, width), lambda j, _: (j, 0)),
             whole((rows, 128)),
@@ -567,12 +605,11 @@
         [shaped((deep, width), BF16), shaped((rows, 128), F32)]
         + [shaped(half, BF16)] * 2
         + [shaped((rows, width), F32)],
-        [pltpu.VMEM((width, rows), BF16)],
         prefetch=1,
         flops=6 * rows * width * deep,
         nbytes=2 * (3 * width * deep + 2 * rows * deep + 4 * rows * width),
         deps=deps,
-    )(bit, grows, w, slope, hidden, gate, x, w_up)
+    )(bit, grows, w, slope, hidden, gate, x_turned, w_up)
 
 
 def norm_back(grad, v, inverse, gain):
@@ -621,7 +658,9 @@
         grad_cr(bit[0], gout[...].astype(BF16), send, keep, kb, nb)
 
 
-def context_back(bit, total, attn, picked, grows, gate, dots, context, gain, w, shape, wp, steps):
+def context_back(
+    bit, total, attn, picked, grows, gate, dots, context, gain, w, shape, wp, steps, deps=()
+):
     rows, width = attn.shape
     rs, cs, kb, nb = shape
     half = (rs, cs // 2, kb * nb // wp, wp)
@@ -648,6 +687,7 @@
         prefetch=1,
         flops=4 * rows * width * width,
         nbytes=26 * rows * width + 6 * width * width,
+        deps=deps,
     )(bit, total, attn, picked, grows, gate, dots, context, gain, w)
 
 
@@ -812,12 +852,12 @@
         (rs,),
         blocks * 2,
         pl.BlockSpec((1, zs, tall, wp), lambda r: (r, 0, 0, 0)),
-        shaped((rs, zs, tall, wp), BF16),
+        pltpu.HBM((rs, zs, tall, wp), BF16),
         flops=rs * zs * tall * wp,
         nbytes=6 * rs * zs * tall * wp,
-        vmem=16,
+        vmem=40,
         deps=deps,
-    )(*keeps, *gots)
+    )(*[pltpu.with_memory_space_constraint(keep, pltpu.HBM) for keep in keeps], *gots)
 
 
 def lower_body(hidden, w, attn, picked, gate, kept):
@@ -1027,12 +1067,12 @@
         kb, nb = shape[2:]
         return jnp.concatenate([total[i : i + kb] for i in range(0, kb * nb // wp, kb)], axis=1)
 
-    projected, w_qkv, normed, gmlp, gate, small = project(
+    projected, w_qkv, turned_normed, gmlp, gate, small = project(
         spots, picked, grows, parts, blocks[0][0], blocks[0][1] // wp
     )
     router, first_gain, second_gain = small[0:1], small[1:2], small[2:3]
     context, probs = attend(projected, seqs)
-    attn, normed_mid, w_out = mix(
+    attn, normed_mid, mid_turned, w_out = mix(
         context, next_parts, tall_up // tall_out, tall_out, blocks[1][0], picked, second_gain, 3
     )
     hidden, slope, w_up, down_send, down_keep = raised(
@@ -1042,44 +1082,47 @@
     down_rows = by_row(down_keep)
 
     w_down, dots, up_send, up_keep, gnormed = feed_back(
-        bit, grows, down_parts, slope, hidden, gate, normed_mid, w_up,
+        bit, grows, down_parts, slope, hidden, gate, mid_turned, w_up,
         blocks[3][0], blocks[2][0], deps=(down_keep,),
     )
+    up_keep = joined([up_keep], [exchanged(up_send)])
+    up_rows = by_row(up_keep)
     gmid, gcontext, logit, gsmall, out_send, out_keep = context_back(
-        bit, gnormed, attn, picked, grows, gate, dots, context, second_gain, w_out, shape_out, wp, 3
-    )
-    up_keep = joined(
-        [up_keep, out_keep], [exchanged(up_send), exchanged(out_send)], deps=(gcontext,)
-    )
-    up_rows = by_row(up_keep)
-    down_sums = depth_parts(down_rows)
-
-    gproj = attend_back(projected, gcontext, probs, seqs, deps=(up_keep, *down_sums))
-    down_total = depth_sum(down_sums, gproj)
-    qkv_send, qkv_keep, little_send, little_keep = qkv_weight_grad(
-        bit, normed, gproj, w_qkv, gsmall, first_gain, shape_qkv, wp, 4, deps=(down_total,)
+        bit, gnormed, attn, picked, grows, gate, dots, context, second_gain, w_out, shape_out,
+        wp, 3, deps=(up_keep,),
+    )
+
+    gproj = attend_back(projected, gcontext, probs, seqs)
+    qkv_send, gfirst = qkv_weight_grad(
+        "qkv_send", bit, turned_normed, gproj, w_qkv, shape_qkv, wp, 2
+    )
+    qkv_keep, little_send, little_keep = qkv_weight_grad(
+        "qkv_keep", bit, turned_normed, gproj, w_qkv, shape_qkv, wp, 2,
+        (gsmall, first_gain, gfirst), deps=(qkv_send,),
     )
     qkv_keep = joined(
-        [qkv_keep, little_keep], [exchanged(qkv_send), exchanged(little_send)]
+        [qkv_keep, out_keep, little_keep],
+        [exchanged(qkv_send), exchanged(out_send), exchanged(little_send)],
     )
     qkv_rows = by_row(qkv_keep)
 
-    up_parts = depth_parts(up_rows)
+    feed_parts = depth_parts(jnp.concatenate([down_rows, up_rows], axis=1))
     starts = jnp.arange(seqs, dtype=jnp.int32) * (tokens.shape[0] // seqs)
     places = (route_index + starts[:, None]).reshape(-1)
     input_grad = picked_back(
         places, gproj, w_qkv, picked, gmid, logit, grows, first_gain, router, base, 256,
-        deps=(qkv_keep, *up_parts),
+        deps=(qkv_keep, *feed_parts),
     )
     kept = lowered(hidden, w_down, attn, picked, gate, 256, deps=(input_grad,))
-    up_total = depth_sum(up_parts, kept)
+    feed_total = depth_sum(feed_parts, kept)
     qkv_parts = depth_parts(qkv_rows)
-    output = place(tokens, index, kept, deps=(up_total, *qkv_parts))
-    down_grad, up_grad = block(down_total, shape_down), block(up_total[:tall_up], shape_up)
+    output = place(tokens, index, kept, deps=(*qkv_parts, feed_total))
     qkv_total = depth_sum(qkv_parts, output)
-    out_grad = block(up_total[tall_up:], shape_out)
+    down_grad = block(feed_total[:tall_down], shape_down)
+    up_grad = block(feed_total[tall_down:], shape_up)
+    out_grad = block(qkv_total[tall_qkv : tall_qkv + tall_out], shape_out)
     qkv_grad = block(qkv_total[:tall_qkv], shape_qkv)
-    sums = qkv_total[tall_qkv, : 3 * width // (rs * cs)].reshape(3, -1)
+    sums = qkv_total[tall_qkv + tall_out, : 3 * width // (rs * cs)].reshape(3, -1)
     return (
         output,
         input_grad,

time: 417 us -> 408 us (0.978)
  local copies, waits for them, and re-layouts: 25 us -> 10.4 us
  Pallas kernels: 277 us -> 288 us
  waiting for transfers between devices: 56.1 us -> 48.5 us
    unnamed x50 -> x30, local copies, waits for them, and re-layouts: 13.8 us -> 2.74 us
    pallas_call x24, Pallas kernels: 277 us -> 288 us  [call(): return lambda *args: made(*args, *deps)]
    ppermute x16 -> x13, starting transfers between devices: 27.7 us -> 25 us  [shifted(): return lax.ppermute(value, 'col' if part == 'z' else 'row', moves)]
    ppermute x16 -> x13, waiting for transfers between devices: 12 us -> 9.45 us  [shifted(): return lax.ppermute(value, 'col' if part == 'z' else 'row', moves)]
  transfers between devices with their start and end apart: 28 -> 25, of which waited for: 10 -> 9; matrix products, arithmetic and copies ran while one was open for 5% -> 4% of each run, Pallas kernels for 66% -> 71%
where the time goes in v3:
time: 408 us; the launch traced here: 403 us
  Pallas kernels  288 us (71%)
  waiting for transfers between devices  48.5 us (12%)
  starting transfers between devices  27 us (7%)
  other arithmetic  14.5 us (4%)
  between operations  14.4 us (4%)
  local copies, waits for them, and re-layouts  10.4 us (3%)
    pallas_call x24, Pallas kernels, call(): return lambda *args: made(*args, *deps)  288 us
    ppermute x13, starting transfers between devices, shifted(): return lax.ppermute(value, 'col' if part == 'z' else 'row', moves)  25 us
    ppermute x5, waiting for transfers between devices, exchanged(): return lax.ppermute(send, 'col', pairs)  15.5 us
    all_gather x2, waiting for transfers between devices, gathered(): lax.all_gather(flat, BOTH, axis=0, tiled=True).reshape(rs, cs, *flat.shape)  15 us
    ppermute x13, waiting for transfers between devices, shifted(): return lax.ppermute(value, 'col' if part == 'z' else 'row', moves)  9.45 us
  transfers between devices with their start and end apart: 25, of which 9 were waited for; matrix products, arithmetic and copies ran while one was open for 4% of the time, Pallas kernels for 71%

profile of v3, /device:TPU:0, one launch (start us, length us, event | category | flops | bytes accessed | tf_op | source)
XLA Modules:
  0.0 402.7 jit_solution(16549003616924761541)
XLA Ops:
  8.6 2.2 pieces.1
  11.6 3.1 collective-permute-start
  14.7 2.6 collective-permute-start.1
  17.3 1.3 collective-permute-start.2
  18.6 1.3 reshape.262.refs_0_
  19.9 11.9 %pick.1.refs_1_.refs_2_.refs_3_.refs_6_ = bf16[1152,1024]{1,0:T(8,128)(2,1)} custom-call(s32[9,1,128]{2,1,0:T(1,128)} %reshape.262.refs_0_, bf16[9216,1024]{1,0:T(8,128)(2,1)} %refs_1_.9), custom_call_target="tpu_custom_call" | custom-call | flops 2415919104 | bytes 56623104 | tf_op jit(solution)/shard_map/pick/pallas_call | solution.py:56
  31.8 3.1 collective-permute-done.1
  36.1 1.5 collective-permute-start.3
  37.7 1.6 collective-permute-start.5
  39.3 8.1 %pick_first.1 = (bf16[1152,1024]{1,0:T(8,128)(2,1)}, f32[9216,1024]{1,0:T(8,128)}) custom-call(s32[9,1,128]{2,1,0:T(1,128)} %reshape.262.refs_0_, bf16[9216,1024]{1,0:T(8,128)(2,1)} %refs_1_.8, bf16[1,4,400,128]{3,2,1,0:T(8,128)(2,1)} %copy-done.2), custom_call_target="tpu_custom_call" | custom-call | flops 2415919104 | bytes 56623104 | tf_op jit(solution)/shard_map/pick_first/pallas_call | solution.py:56
  48.5 1.7 collective-permute-start.4
  51.2 1.5 collective-permute-start.6
  52.7 14.9 %pick_rest.1 = (bf16[1152,1024]{1,0:T(8,128)(2,1)}, f32[9216,1024]{1,0:T(8,128)}) custom-call(s32[9,1,128]{2,1,0:T(1,128)} %reshape.262.refs_0_, bf16[9216,1024]{1,0:T(8,128)(2,1)} %refs_1_.8, bf16[1152,1024]{1,0:T(8,128)(2,1)} %get-tuple-element.98.refs_1_.refs_2_, ...), custom_call_target="tpu_custom_call", output_to_operand_aliasing={{0}: (2, {}), {1}: (3, {})} | custom-call | flops 2415919104 | bytes 56623104 | tf_op jit(solution)/shard_map/pick_rest/pallas_call | solution.py:56
  67.6 4.2 %collective-permute-done.4 = bf16[2,4,400,128]{3,2,1,0:T(8,128)(2,1)S(1)} collective-permute-done((bf16[2,4,400,128]{3,2,1,0:T(8,128)(2,1)S(1)}, bf16[2,4,400,128]{3,2,1,0:T(8,128)(2,1)S(1)}, u32[]{:S(2)}, u32[]{:S(2)}) %collective-permute-start.4) | collective-permute-done | bytes 819232 | tf_op jit(solution)/shard_map/ppermute | solution.py:966
  72.7 1.5 pad_maximum_fusion.refs_3_.refs_7_
  74.3 2.1 collective-permute-done.6
  76.4 1.3 pad_maximum_fusion.1.refs_4_
  78.5 5.2 %collective-permute-done.8.refs_6_ = bf16[4,4,400,128]{3,2,1,0:T(8,128)(2,1)S(1)} collective-permute-done((bf16[4,4,400,128]{3,2,1,0:T(8,128)(2,1)}, bf16[4,4,400,128]{3,2,1,0:T(8,128)(2,1)S(1)}, u32[]{:S(2)}, u32[]{:S(2)}) %collective-permute-start.8) | collective-permute-done | bytes 1638432 | tf_op jit(solution)/shard_map/ppermute | solution.py:986
  83.6 1.2 copy-done.13
  84.8 17.8 %project.1 = (bf16[1152,3072]{1,0:T(8,128)(2,1)}, bf16[1024,3072]{1,0:T(8,128)(2,1)}, bf16[1024,1152]{1,0:T(8,128)(2,1)}, bf16[1152,1024]{1,0:T(8,128)(2,1)}, f32[1152,1]{1,0:T(8,128)}, /*index=5*/f32[3,1024]{1,0:T(4,128)}) custom-call(s32[4,4]{1,0:T(4,128)} %copy-done.12, bf16[1152,1024]{1,0:T(8,128)(2,1)} %pick.1.refs_1_.refs_2_.refs_3_.refs_6_, ...), custom_call_target="tpu_custom_call" | custom-call | flops 7247757312 | bytes 29097984 | tf_op jit(solution)/shard_map/project/pallas_call | solution.py:56
  102.6 1.4 fusion.16
  104.0 11.4 %attend.1 = (bf16[1152,1024]{1,0:T(8,128)(2,1)}, bf16[9,2048,128]{2,1,0:T(8,128)(2,1)}) custom-call(bf16[1152,3072]{1,0:T(8,128)(2,1)} %get-tuple-element.101.refs_0_), custom_call_target="tpu_custom_call" | custom-call | flops 9059696640 | bytes 28311552 | tf_op jit(solution)/shard_map/attend/pallas_call | solution.py:56
  115.4 10.0 %mix.1 = (f32[1152,1024]{1,0:T(8,128)}, bf16[1152,1024]{1,0:T(8,128)(2,1)}, bf16[1024,1152]{1,0:T(8,128)(2,1)}, bf16[1024,1024]{1,0:T(8,128)(2,1)}) custom-call(bf16[1152,1024]{1,0:T(8,128)(2,1)} %get-tuple-element.102.refs_0_.refs_7_, bf16[4,8,1280,128]{3,2,1,0:T(8,128)(2,1)} %bitcast.58, bf16[1152,1024]{1,0:T(8,128)(2,1)} %pick.1.refs_1_.refs_2_.refs_3_.refs_6_, ...), custom_call_target="tpu_custom_call" | custom-call | flops 2415919104 | bytes 16515072 | tf_op jit(solution)/shard_map/mix/pallas_call | solution.py:56
  125.4 40.2 %raise.1 = (bf16[1152,4096]{1,0:T(8,128)(2,1)}, bf16[1152,4096]{1,0:T(8,128)(2,1)}, bf16[1024,4096]{1,0:T(8,128)(2,1)}, bf16[4,4,1024,128]{3,2,1,0:T(8,128)(2,1)}, bf16[4,4,1024,128]{3,2,1,0:T(8,128)(2,1)}) custom-call(s32[1]{0:T(128)} %bitcast.refs_0_, bf16[1152,1024]{1,0:T(8,128)(2,1)} %get-tuple-element.105.refs_1_, ...), custom_call_target="tpu_custom_call" | custom-call | flops 24159191040 | bytes 46399488 | tf_op jit(solution)/shard_map/raise/pallas_call | solution.py:56
  165.7 7.3 %collective-permute-done.9.refs_1_ = bf16[4,4,1024,128]{3,2,1,0:T(8,128)(2,1)S(1)} collective-permute-done((bf16[4,4,1024,128]{3,2,1,0:T(8,128)(2,1)}, bf16[4,4,1024,128]{3,2,1,0:T(8,128)(2,1)S(1)}, u32[]{:S(2)}, u32[]{:S(2)}) %collective-permute-start.9) | collective-permute-done | bytes 4194336 | tf_op jit(solution)/shard_map/ppermute | solution.py:1045
  172.9 5.1 %join.3.refs_8_ = bf16[4,4,1024,128]{3,2,1,0:T(8,128)(2,1)} custom-call(bf16[4,4,1024,128]{3,2,1,0:T(8,128)(2,1)} %get-tuple-element.113.refs_0_, bf16[4,4,1024,128]{3,2,1,0:T(8,128)(2,1)S(1)} %collective-permute-done.9.refs_1_), custom_call_target="tpu_custom_call" | custom-call | flops 2097152 | bytes 12582912 | tf_op jit(solution)/shard_map/join/pallas_call | solution.py:56
  178.3 15.0 %all-gather.5.cloned.1.call-done = bf16[32768,128]{1,0:T(8,128)(2,1)} async-done(((bf16[1024,128]{1,0:T(8,128)(2,1)}), bf16[32768,128]{1,0:T(8,128)(2,1)}) %all-gather.5.cloned.1.call-update) | async-done | bytes 8388624 | tf_op jit(solution)/shard_map/all_gather | solution.py:955
  193.3 45.5 %feed_back.1 = (bf16[4096,1024]{1,0:T(8,128)(2,1)}, f32[1152,128]{1,0:T(8,128)}, bf16[4,4,1024,128]{3,2,1,0:T(8,128)(2,1)}, bf16[4,4,1024,128]{3,2,1,0:T(8,128)(2,1)}, f32[1152,1024]{1,0:T(8,128)}) custom-call(s32[1]{0:T(128)} %bitcast.refs_0_, bf16[1152,1024]{1,0:T(8,128)(2,1)} %get-tuple-element.100.refs_1_.refs_2_.refs_4_.refs_8_, ...), custom_call_target="tpu_custom_call" | custom-call | flops 28991029248 | bytes 53477376 | tf_op jit(solution)/shard_map/feed_back/pallas_call | solution.py:56
  239.1 7.1 %collective-permute-done.10.refs_1_ = bf16[4,4,1024,128]{3,2,1,0:T(8,128)(2,1)S(1)} collective-permute-done((bf16[4,4,1024,128]{3,2,1,0:T(8,128)(2,1)}, bf16[4,4,1024,128]{3,2,1,0:T(8,128)(2,1)S(1)}, u32[]{:S(2)}, u32[]{:S(2)}) %collective-permute-start.10) | collective-permute-done | bytes 4194336 | tf_op jit(solution)/shard_map/ppermute | solution.py:1045
  246.3 5.1 %join.4.refs_10_ = bf16[4,4,1024,128]{3,2,1,0:T(8,128)(2,1)} custom-call(bf16[4,4,1024,128]{3,2,1,0:T(8,128)(2,1)} %get-tuple-element.120.refs_0_, bf16[4,4,1024,128]{3,2,1,0:T(8,128)(2,1)S(1)} %collective-permute-done.10.refs_1_), custom_call_target="tpu_custom_call" | custom-call | flops 2097152 | bytes 12582912 | tf_op jit(solution)/shard_map/join/pallas_call | solution.py:56
  251.6 18.6 %context_back.1 = (f32[1152,1024]{1,0:T(8,128)}, bf16[1152,1024]{1,0:T(8,128)(2,1)}, f32[1152,1]{1,0:T(8,128)}, f32[2,1024]{1,0:T(2,128)}, bf16[4,4,256,128]{3,2...) custom-call(s32[1]{0:T(128)} %bitcast.refs_0_, f32[1152,1024]{1,0:T(8,128)} %get-tuple-element.117.refs_1_, ...), custom_call_target="tpu_custom_call" | custom-call | flops 4831838208 | bytes 36962304 | tf_op jit(solution)/shard_map/context_back/pallas_call | solution.py:56
  270.2 14.0 %attend_back.1.refs_2_.refs_3_.refs_1_ = bf16[1152,3072]{1,0:T(8,128)(2,1)} custom-call(bf16[1152,3072]{1,0:T(8,128)(2,1)} %get-tuple-element.101.refs_0_, bf16[1152,1024]{1,0:T(8,128)(2,1)} %get-tuple-element.122.refs_1_, bf16[9,2048,128]{2,1,0:T(8,128)(2,1)} %get-tuple-element.123.refs_2_), custom_call_target="tpu_custom_call" | custom-call | flops 18119393280 | bytes 56623104 | tf_op jit(solution)/shard_map/attend_back/pallas_call | solution.py:56
  284.2 9.7 %qkv_send.1 = (bf16[4,4,768,128]{3,2,1,0:T(8,128)(2,1)}, f32[1024,1]{1,0:T(8,128)}) custom-call(s32[1]{0:T(128)} %bitcast.refs_0_, bf16[1024,1152]{1,0:T(8,128)(2,1)} %get-tuple-element.128.refs_1_, bf16[1152,3072]{1,0:T(8,128)(2,1)} %attend_back.1.refs_2_.refs_3_.refs_1_, bf16[1152,3072]{1,0:T(8,128)(2,1)} %attend_back.1.refs_2_.refs_3_.refs_1_, ...), custom_call_target="tpu_custom_call" | custom-call | flops 3623878656 | bytes 11010048 | tf_op jit(solution)/shard_map/qkv_send/pallas_call | solution.py:56
  294.4 10.9 %qkv_keep.1 = (bf16[4,4,768,128]{3,2,1,0:T(8,128)(2,1)}, bf16[4,4,16,128]{3,2,1,0:T(8,128)(2,1)}, bf16[4,4,16,128]{3,2,1,0:T(8,128)(2,1)}) custom-call(s32[1]{0:T(128)} %bitcast.refs_0_, bf16[1024,1152]{1,0:T(8,128)(2,1)} %get-tuple-element.128.refs_1_, bf16[1152,3072]{1,0:T(8,128)(2,1)} %attend_back.1.refs_2_.refs_3_.refs_1_, ...), custom_call_target="tpu_custom_call" | custom-call | flops 3623878656 | bytes 11010048 | tf_op jit(solution)/shard_map/qkv_keep/pallas_call | solution.py:56
  305.7 1.1 collective-permute-done.13.refs_5_
  306.8 5.2 %join.5.refs_10_ = bf16[4,4,1040,128]{3,2,1,0:T(8,128)(2,1)} custom-call(bf16[4,4,768,128]{3,2,1,0:T(8,128)(2,1)} %get-tuple-element.132.refs_0_, bf16[4,4,256,128]{3,2,1,0:T(8,128)(2,1)} %get-tuple-element.133.refs_1_, bf16[4,4,16,128]{3,2,1,0:T(8,128)(2,1)} %get-tuple-element.134.refs_2_, bf16[4,4,768,128]{3,2,1,0:T(8,128)(2,1)S(1)} %collective-permute-done.11.refs_3_, ...), custom_call_target="tpu_custom_call" | custom-call | flops 2129920 | bytes 12779520 | tf_op jit(solution)/shard_map/join/pallas_call | solution.py:56
  313.3 2.4 fusion.1
  315.8 1.6 collective-permute-start.14
  317.4 1.3 collective-permute-start.15
  318.7 2.2 collective-permute-start.16
  320.9 21.4 %picked_back.1.refs_5_ = f32[9216,1024]{1,0:T(8,128)} custom-call(s32[1152]{0:T(1024)} %add_bitcast_fusion.refs_0_, bf16[1152,3072]{1,0:T(8,128)(2,1)} %attend_back.1.refs_2_.refs_3_.refs_1_, bf16[1024,3072]{1,0:T(8,128)(2,1)} %get-tuple-element.124.refs_4_.refs_5_.refs_2_, f32[1152,1]{1,0:T(8,128)} %get-tuple-element.125.refs_3_, ...), custom_call_target="tpu_custom_call", output_to_operand_aliasing={{}: (9, {})} | custom-call | flops 7247757312 | bytes 25165824 | tf_op jit(solution)/shard_map/picked_back/pallas_call | solution.py:56
  342.3 17.2 %lower.1.refs_1_.refs_2_ = bf16[1152,1024]{1,0:T(8,128)(2,1)} custom-call(bf16[1152,4096]{1,0:T(8,128)(2,1)} %get-tuple-element.107.refs_4_.refs_0_, bf16[4096,1024]{1,0:T(8,128)(2,1)} %get-tuple-element.115.refs_1_, f32[1152,1024]{1,0:T(8,128)} %get-tuple-element.116.refs_2_, bf16[1152,1024]{1,0:T(8,128)(2,1)} %pick.1.refs_1_.refs_2_.refs_3_.refs_6_, ...), custom_call_target="tpu_custom_call" | custom-call | flops 9663676416 | bytes 27262976 | tf_op jit(solution)/shard_map/lower/pallas_call | solution.py:56
  359.6 1.3 convert_add_fusion.refs_7_
  361.9 2.5 reduce-scatter.8.cloned.1.call-done
  364.4 2.0 dynamic-slice_bitcast_fusion
  366.4 4.1 %collective-permute-start.17 = (bf16[1040,128]{1,0:T(8,128)(2,1)S(1)}, bf16[1040,128]{1,0:T(8,128)(2,1)S(1)}, u32[]{:S(2)}, u32[]{:S(2)}) collective-permute-start(bf16[1040,128]{1,0:T(8,128)(2,1)S(1)} %get-tuple-element.143.refs_4_), channel_id=1, source_target_pairs={{0,2},{1,3},{2,4},{3,5},{4,6},{5,7},{6,0},{7,1},{8,10},{9,11},{10,... | collective-permute-start | bytes 798728 | tf_op jit(solution)/shard_map/ppermute | solution.py:966
  371.3 1.6 collective-permute-start.19
  373.8 18.9 %place.1.refs_1_ = bf16[9216,1024]{1,0:T(8,128)(2,1)} custom-call(s32[9,1,128]{2,1,0:T(1,128)} %reshape.262.refs_0_, bf16[9216,1024]{1,0:T(8,128)(2,1)} %refs_1_.9, bf16[1152,1024]{1,0:T(8,128)(2,1)} %lower.1.refs_1_.refs_2_, bf16[1040,128]{1,0:T(8,128)(2,1)} %get-tuple-element.144.refs_3_.refs_0_, bf16[1040,128]{1,0:T(8,128)(2,1)} %copy-done.9, ...), custom_call_target="tpu_custom_call" | custom-call | flops 2415919104 | bytes 37748736 | tf_op jit(solution)/shard_map/place/pallas_call | solution.py:56
  (97 shorter events, 16.0 us)
Async XLA Ops:
  7.2 108.3 %all-gather.3.cloned.1.call-start = ((), (), s32[]{:S(2)}) async-start(), calls=%async_computation.3 | async-start | bytes 10813440 | tf_op jit(solution)/shard_map/all_gather | solution.py:955
  10.8 182.5 %all-gather.5.cloned.1.call-start = ((), (), s32[]{:S(2)}) async-start(), calls=%async_computation.4 | async-start | bytes 8650752 | tf_op jit(solution)/shard_map/all_gather | solution.py:955
  11.5 301.8 %reduce-scatter.4.cloned.1.call-start = ((), (), s32[]{:S(2)}) async-start(), calls=%async_computation.5 | async-start | bytes 5242880 | tf_op jit(solution)/shard_map/reduce_scatter | solution.py:1049
  11.6 20.2 %collective-permute-start = (bf16[800,128]{1,0:T(8,128)(2,1)}, bf16[800,128]{1,0:T(8,128)(2,1)S(1)}, u32[]{:S(2)}, u32[]{:S(2)}) collective-permute-start(bf16[800,128]{1,0:T(8,128)(2,1)} %get-tuple-element.97.refs_0_), channel_id=1, source_target_pairs={{0,2},{1,3},{2,4},{3,5},{4,6},{5,7},{6,0},{7,1},{8,10},{9,11},{10,... | collective-permute-start | bytes 614408 | tf_op jit(solution)/shard_map/ppermute | solution.py:966
  14.7 20.3 %collective-permute-start.1 = (bf16[800,128]{1,0:T(8,128)(2,1)}, bf16[800,128]{1,0:T(8,128)(2,1)S(1)}, u32[]{:S(2)}, u32[]{:S(2)}) collective-permute-start(bf16[800,128]{1,0:T(8,128)(2,1)} %get-tuple-element.97.refs_0_), channel_id=1, source_target_pairs={{0,4},{1,5},{2,6},{3,7},{4,0},{5,1},{6,2},{7,3},{8,12},{9,13},{10,... | collective-permute-start | bytes 614408 | tf_op jit(solution)/shard_map/ppermute | solution.py:966
  17.3 17.7 %collective-permute-start.2 = (bf16[800,128]{1,0:T(8,128)(2,1)}, bf16[800,128]{1,0:T(8,128)(2,1)S(1)}, u32[]{:S(2)}, u32[]{:S(2)}) collective-permute-start(bf16[800,128]{1,0:T(8,128)(2,1)} %get-tuple-element.97.refs_0_), channel_id=1, source_target_pairs={{0,6},{1,7},{2,0},{3,1},{4,2},{5,3},{6,4},{7,5},{8,14},{9,15},{10,... | collective-permute-start | bytes 614408 | tf_op jit(solution)/shard_map/ppermute | solution.py:966
  36.1 3.2 copy-start.2
  36.1 11.3 %collective-permute-start.3 = (bf16[1,4,400,128]{3,2,1,0:T(8,128)(2,1)S(1)}, bf16[1,4,400,128]{3,2,1,0:T(8,128)(2,1)S(1)}, u32[]{:S(2)}, u32[]{:S(2)}) collective-permute-start(bf16[1,4,400,128]{3,2,1,0:T(8,128)(2,1)S(1)} %maximum_bitcast_fusion.refs_2_.refs_0_), channel_id=1, source_target_pairs={{0,8},{8,0},{16,24},{24,16},{1,9},{9,1},{17,25},{25,17},{2,10},{10... | collective-permute-start | bytes 1228808 | tf_op jit(solution)/shard_map/ppermute | solution.py:966
  37.7 12.6 %collective-permute-start.5 = (bf16[1,4,400,128]{3,2,1,0:T(8,128)(2,1)S(1)}, bf16[1,4,400,128]{3,2,1,0:T(8,128)(2,1)S(1)}, u32[]{:S(2)}, u32[]{:S(2)}) collective-permute-start(bf16[1,4,400,128]{3,2,1,0:T(8,128)(2,1)S(1)} %maximum_bitcast_fusion.1), channel_id=1, source_target_pairs={{0,16},{8,24},{16,0},{24,8},{1,17},{9,25},{17,1},{25,9},{2,18},{10... | collective-permute-start | bytes 1228808 | tf_op jit(solution)/shard_map/ppermute | solution.py:966
  48.5 4.2 %copy-start = (bf16[2,4,400,128]{3,2,1,0:T(8,128)(2,1)}, bf16[2,4,400,128]{3,2,1,0:T(8,128)(2,1)S(1)}, u32[]{:S(2)}) copy-start(bf16[2,4,400,128]{3,2,1,0:T(8,128)(2,1)S(1)} %pad_maximum_fusion.2.refs_4_.refs_0_) | copy-start | bytes 2457604
  48.5 23.3 %collective-permute-start.4 = (bf16[2,4,400,128]{3,2,1,0:T(8,128)(2,1)S(1)}, bf16[2,4,400,128]{3,2,1,0:T(8,128)(2,1)S(1)}, u32[]{:S(2)}, u32[]{:S(2)}) collective-permute-start(bf16[2,4,400,128]{3,2,1,0:T(8,128)(2,1)S(1)} %pad_maximum_fusion.2.refs_4_.refs_0_), channel_id=1, source_target_pairs={{0,16},{8,24},{16,0},{24,8},{1,17},{9,25},{17,1},{25,9},{2,18},{10... | collective-permute-start | bytes 2457608 | tf_op jit(solution)/shard_map/ppermute | solution.py:966
  51.2 25.2 %collective-permute-start.6 = (bf16[2,4,400,128]{3,2,1,0:T(8,128)(2,1)}, bf16[2,4,400,128]{3,2,1,0:T(8,128)(2,1)S(1)}, u32[]{:S(2)}, u32[]{:S(2)}) collective-permute-start(bf16[2,4,400,128]{3,2,1,0:T(8,128)(2,1)} %pad_maximum_fusion.3), channel_id=1, source_target_pairs={{0,8},{8,0},{16,24},{24,16},{1,9},{9,1},{17,25},{25,17},{2,10},{10... | collective-permute-start | bytes 2457608 | tf_op jit(solution)/shard_map/ppermute | solution.py:966
  71.8 0.9 copy-start.10
  74.2 9.4 %copy-start.6 = (bf16[4,4,400,128]{3,2,1,0:T(8,128)(2,1)}, bf16[4,4,400,128]{3,2,1,0:T(8,128)(2,1)S(1)}, u32[]{:S(2)}) copy-start(bf16[4,4,400,128]{3,2,1,0:T(8,128)(2,1)S(1)} %pad_maximum_fusion.refs_3_.refs_7_) | copy-start | bytes 4915204
  74.2 4.2 %collective-permute-start.7 = (bf16[4,4,400,128]{3,2,1,0:T(8,128)(2,1)S(1)}, bf16[4,4,400,128]{3,2,1,0:T(8,128)(2,1)}, u32[]{:S(2)}, u32[]{:S(2)}) collective-permute-start(bf16[4,4,400,128]{3,2,1,0:T(8,128)(2,1)S(1)} %pad_maximum_fusion.refs_3_.refs_7_), channel_id=1, source_target_pairs={{0,1},{1,0},{2,3},{3,2},{4,5},{5,4},{6,7},{7,6},{8,9},{9,8},{10,11... | collective-permute-start | bytes 4915208 | tf_op jit(solution)/shard_map/ppermute | solution.py:986
  77.7 5.9 %collective-permute-start.8 = (bf16[4,4,400,128]{3,2,1,0:T(8,128)(2,1)}, bf16[4,4,400,128]{3,2,1,0:T(8,128)(2,1)S(1)}, u32[]{:S(2)}, u32[]{:S(2)}) collective-permute-start(bf16[4,4,400,128]{3,2,1,0:T(8,128)(2,1)} %pad_maximum_fusion.1.refs_4_), channel_id=1, source_target_pairs={{0,1},{1,0},{2,3},{3,2},{4,5},{5,4},{6,7},{7,6},{8,9},{9,8},{10,11... | collective-permute-start | bytes 4915208 | tf_op jit(solution)/shard_map/ppermute | solution.py:986
  78.4 5.2 %copy-start.12 = (s32[4,4]{1,0:T(4,128)}, s32[4,4]{1,0:T(4,128)S(1)}, u32[]{:S(2)}) copy-start(s32[4,4]{1,0:T(4,128)S(1)} %scatter.19.refs_0_) | copy-start | bytes 196
  83.6 1.2 copy-start.13
  165.6 7.4 %collective-permute-start.9 = (bf16[4,4,1024,128]{3,2,1,0:T(8,128)(2,1)}, bf16[4,4,1024,128]{3,2,1,0:T(8,128)(2,1)S(1)}, u32[]{:S(2)}, u32[]{:S(2)}) collective-permute-start(bf16[4,4,1024,128]{3,2,1,0:T(8,128)(2,1)} %get-tuple-element.114), channel_id=1, source_target_pairs={{0,1},{1,0},{2,3},{3,2},{4,5},{5,4},{6,7},{7,6},{8,9},{9,8},{10,11... | collective-permute-start | bytes 12582920 | tf_op jit(solution)/shard_map/ppermute | solution.py:1045
  178.1 135.3 %reduce-scatter.6.cloned.1.call-start = ((), (), s32[]{:S(2)}) async-start(), calls=%async_computation.6 | async-start | bytes 5242880 | tf_op jit(solution)/shard_map/reduce_scatter | solution.py:1049
  238.8 7.4 %collective-permute-start.10 = (bf16[4,4,1024,128]{3,2,1,0:T(8,128)(2,1)}, bf16[4,4,1024,128]{3,2,1,0:T(8,128)(2,1)S(1)}, u32[]{:S(2)}, u32[]{:S(2)}) collective-permute-start(bf16[4,4,1024,128]{3,2,1,0:T(8,128)(2,1)} %get-tuple-element.121), channel_id=1, source_target_pairs={{0,1},{1,0},{2,3},{3,2},{4,5},{5,4},{6,7},{7,6},{8,9},{9,8},{10,11... | collective-permute-start | bytes 12582920 | tf_op jit(solution)/shard_map/ppermute | solution.py:1045
  251.4 113.1 %reduce-scatter.8.cloned.1.call-start = ((), (), s32[]{:S(2)}) async-start(), calls=%async_computation.7 | async-start | bytes 5324800 | tf_op jit(solution)/shard_map/reduce_scatter | solution.py:1049
  284.2 10.1 %copy-start.14 = (bf16[4,4,256,128]{3,2,1,0:T(8,128)(2,1)S(1)}, bf16[4,4,256,128]{3,2,1,0:T(8,128)(2,1)}, u32[]{:S(2)}) copy-start(bf16[4,4,256,128]{3,2,1,0:T(8,128)(2,1)} %get-tuple-element.135) | copy-start | bytes 3145732
  293.9 12.9 %collective-permute-start.11 = (bf16[4,4,768,128]{3,2,1,0:T(8,128)(2,1)}, bf16[4,4,768,128]{3,2,1,0:T(8,128)(2,1)S(1)}, u32[]{:S(2)}, u32[]{:S(2)}) collective-permute-start(bf16[4,4,768,128]{3,2,1,0:T(8,128)(2,1)} %get-tuple-element.131.refs_9_), channel_id=1, source_target_pairs={{0,1},{1,0},{2,3},{3,2},{4,5},{5,4},{6,7},{7,6},{8,9},{9,8},{10,11... | collective-permute-start | bytes 9437192 | tf_op jit(solution)/shard_map/ppermute | solution.py:1045
  294.3 12.5 %collective-permute-start.12 = (bf16[4,4,256,128]{3,2,1,0:T(8,128)(2,1)S(1)}, bf16[4,4,256,128]{3,2,1,0:T(8,128)(2,1)S(1)}, u32[]{:S(2)}, u32[]{:S(2)}) collective-permute-start(bf16[4,4,256,128]{3,2,1,0:T(8,128)(2,1)S(1)} %copy-done.14), channel_id=1, source_target_pairs={{0,1},{1,0},{2,3},{3,2},{4,5},{5,4},{6,7},{7,6},{8,9},{9,8},{10,11... | collective-permute-start | bytes 3145736 | tf_op jit(solution)/shard_map/ppermute | solution.py:1045
  305.2 1.5 collective-permute-start.13
  312.0 0.7 copy-start.11
  315.8 5.1 %copy-start.3 = (bf16[2048,128]{1,0:T(8,128)(2,1)}, bf16[2048,128]{1,0:T(8,128)(2,1)S(1)}, u32[]{:S(2)}) copy-start(bf16[2048,128]{1,0:T(8,128)(2,1)S(1)} %get-tuple-element.137.refs_14_) | copy-start | bytes 1572868
  315.8 5.1 %copy-start.4 = (bf16[2048,128]{1,0:T(8,128)(2,1)}, bf16[2048,128]{1,0:T(8,128)(2,1)S(1)}, u32[]{:S(2)}) copy-start(bf16[2048,128]{1,0:T(8,128)(2,1)S(1)} %get-tuple-element.140.refs_13_) | copy-start | bytes 1572868
  315.8 5.1 %copy-start.5 = (bf16[2048,128]{1,0:T(8,128)(2,1)}, bf16[2048,128]{1,0:T(8,128)(2,1)S(1)}, u32[]{:S(2)}) copy-start(bf16[2048,128]{1,0:T(8,128)(2,1)S(1)} %get-tuple-element.139.refs_12_) | copy-start | bytes 1572868
  315.8 43.8 %collective-permute-start.14 = (bf16[2048,128]{1,0:T(8,128)(2,1)S(1)}, bf16[2048,128]{1,0:T(8,128)(2,1)S(1)}, u32[]{:S(2)}, u32[]{:S(2)}) collective-permute-start(bf16[2048,128]{1,0:T(8,128)(2,1)S(1)} %get-tuple-element.139.refs_12_), channel_id=1, source_target_pairs={{0,2},{1,3},{2,4},{3,5},{4,6},{5,7},{6,0},{7,1},{8,10},{9,11},{10,... | collective-permute-start | bytes 1572872 | tf_op jit(solution)/shard_map/ppermute | solution.py:966
  317.4 42.2 %collective-permute-start.15 = (bf16[2048,128]{1,0:T(8,128)(2,1)S(1)}, bf16[2048,128]{1,0:T(8,128)(2,1)S(1)}, u32[]{:S(2)}, u32[]{:S(2)}) collective-permute-start(bf16[2048,128]{1,0:T(8,128)(2,1)S(1)} %get-tuple-element.140.refs_13_), channel_id=1, source_target_pairs={{0,4},{1,5},{2,6},{3,7},{4,0},{5,1},{6,2},{7,3},{8,12},{9,13},{10,... | collective-permute-start | bytes 1572872 | tf_op jit(solution)/shard_map/ppermute | solution.py:966
  318.7 40.8 %collective-permute-start.16 = (bf16[2048,128]{1,0:T(8,128)(2,1)S(1)}, bf16[2048,128]{1,0:T(8,128)(2,1)S(1)}, u32[]{:S(2)}, u32[]{:S(2)}) collective-permute-start(bf16[2048,128]{1,0:T(8,128)(2,1)S(1)} %get-tuple-element.137.refs_14_), channel_id=1, source_target_pairs={{0,6},{1,7},{2,0},{3,1},{4,2},{5,3},{6,4},{7,5},{8,14},{9,15},{10,... | collective-permute-start | bytes 1572872 | tf_op jit(solution)/shard_map/ppermute | solution.py:966
  360.9 5.5 %copy-start.1 = (f32[2048,128]{1,0:T(8,128)}, f32[2048,128]{1,0:T(8,128)S(1)}, u32[]{:S(2)}) copy-start(f32[2048,128]{1,0:T(8,128)S(1)} %convert_add_fusion.refs_7_) | copy-start | bytes 3145732
  366.4 7.4 %copy-start.7 = (bf16[1040,128]{1,0:T(8,128)(2,1)}, bf16[1040,128]{1,0:T(8,128)(2,1)S(1)}, u32[]{:S(2)}) copy-start(bf16[1040,128]{1,0:T(8,128)(2,1)S(1)} %get-tuple-element.141.refs_6_) | copy-start | bytes 798724
  366.4 7.4 %copy-start.8 = (bf16[1040,128]{1,0:T(8,128)(2,1)}, bf16[1040,128]{1,0:T(8,128)(2,1)S(1)}, u32[]{:S(2)}) copy-start(bf16[1040,128]{1,0:T(8,128)(2,1)S(1)} %get-tuple-element.142.refs_5_) | copy-start | bytes 798724
  366.4 7.4 %copy-start.9 = (bf16[1040,128]{1,0:T(8,128)(2,1)}, bf16[1040,128]{1,0:T(8,128)(2,1)S(1)}, u32[]{:S(2)}) copy-start(bf16[1040,128]{1,0:T(8,128)(2,1)S(1)} %get-tuple-element.143.refs_4_) | copy-start | bytes 798724
  366.4 26.3 %collective-permute-start.17 = (bf16[1040,128]{1,0:T(8,128)(2,1)S(1)}, bf16[1040,128]{1,0:T(8,128)(2,1)S(1)}, u32[]{:S(2)}, u32[]{:S(2)}) collective-permute-start(bf16[1040,128]{1,0:T(8,128)(2,1)S(1)} %get-tuple-element.143.refs_4_), channel_id=1, source_target_pairs={{0,2},{1,3},{2,4},{3,5},{4,6},{5,7},{6,0},{7,1},{8,10},{9,11},{10,... | collective-permute-start | bytes 798728 | tf_op jit(solution)/shard_map/ppermute | solution.py:966
  370.5 22.2 %collective-permute-start.18 = (bf16[1040,128]{1,0:T(8,128)(2,1)S(1)}, bf16[1040,128]{1,0:T(8,128)(2,1)S(1)}, u32[]{:S(2)}, u32[]{:S(2)}) collective-permute-start(bf16[1040,128]{1,0:T(8,128)(2,1)S(1)} %get-tuple-element.142.refs_5_), channel_id=1, source_target_pairs={{0,4},{1,5},{2,6},{3,7},{4,0},{5,1},{6,2},{7,3},{8,12},{9,13},{10,... | collective-permute-start | bytes 798728 | tf_op jit(solution)/shard_map/ppermute | solution.py:966
  371.3 21.4 %collective-permute-start.19 = (bf16[1040,128]{1,0:T(8,128)(2,1)S(1)}, bf16[1040,128]{1,0:T(8,128)(2,1)S(1)}, u32[]{:S(2)}, u32[]{:S(2)}) collective-permute-start(bf16[1040,128]{1,0:T(8,128)(2,1)S(1)} %get-tuple-element.141.refs_6_), channel_id=1, source_target_pairs={{0,6},{1,7},{2,0},{3,1},{4,2},{5,3},{6,4},{7,5},{8,14},{9,15},{10,... | collective-permute-start | bytes 798728 | tf_op jit(solution)/shard_map/ppermute | solution.py:966
Sparse Core Ops, SparseCore 0:
  11.4 101.8 all-gather.2
  116.9 76.3 all-gather.4
  196.3 51.2 reduce-scatter.3
  251.5 51.9 reduce-scatter.5
  312.1 52.2 reduce-scatter.7

commit v4 on v3

--- a/solution.py
+++ b/solution.py
@@ -260,7 +260,7 @@
     )
 
 
-def attend_body(proj, context, probs):
+def attend_body(proj, context, probs, context_turned):
     routed = proj.shape[0]
     low, high = halves()
     causal = causal_of(routed)
@@ -279,7 +279,9 @@
         both = jnp.concatenate(weights[2 * pair : 2 * pair + 2], axis=0)
         probs[0, 2 * pair * routed : 2 * (pair + 1) * routed, :] = both
         mixed = mul(both, jnp.concatenate([b * low, c * high], axis=0), TN)
-        context[:, pair * 2 * HD : (pair + 1) * 2 * HD] = mixed.astype(BF16)
+        mixed = mixed.astype(BF16)
+        context[:, pair * 2 * HD : (pair + 1) * 2 * HD] = mixed
+        context_turned[pair * 2 * HD : (pair + 1) * 2 * HD, :] = mixed.T
 
 
 def attend(projected, seqs):
@@ -294,8 +296,13 @@
         [
             pl.BlockSpec((routed, width), lambda s: (s, 0)),
             pl.BlockSpec((1, HEADS * routed, routed), lambda s: (s, 0, 0)),
+            pl.BlockSpec((width, routed), lambda s: (0, s)),
         ],
-        [shaped((rows, width), BF16), shaped((seqs, HEADS * routed, routed), BF16)],
+        [
+            shaped((rows, width), BF16),
+            shaped((seqs, HEADS * routed, routed), BF16),
+            shaped((width, rows), BF16),
+        ],
         flops=20 * rows * wide * routed,
         nbytes=8 * projected.size,
     )(projected)
@@ -651,7 +658,7 @@
 
     lax.fori_loop(0, total.shape[0] // chunk, rows_back, 0)
     gcontext[...] = mul(gattn[...], w[...], NT).astype(BF16)
-    gout[...] += mul(context[...], gattn[...], TN)
+    gout[...] += mul(context[...], gattn[...])
 
     @pl.when(step == pl.num_programs(0) - 1)
     def _():
@@ -672,7 +679,8 @@
         "context_back",
         (steps,),
         [part] * 4
-        + [thin, pl.BlockSpec((size, 128), lambda j, _: (j, 0)), part]
+        + [thin, pl.BlockSpec((size, 128), lambda j, _: (j, 0))]
+        + [pl.BlockSpec((width, size), lambda j, _: (0, j))]
         + [once(gain.shape), once(w.shape)],
         [part, part, thin, whole((2, width)), whole(half), whole(half)],
         [
@@ -1071,7 +1079,7 @@
         spots, picked, grows, parts, blocks[0][0], blocks[0][1] // wp
     )
     router, first_gain, second_gain = small[0:1], small[1:2], small[2:3]
-    context, probs = attend(projected, seqs)
+    context, probs, context_turned = attend(projected, seqs)
     attn, normed_mid, mid_turned, w_out = mix(
         context, next_parts, tall_up // tall_out, tall_out, blocks[1][0], picked, second_gain, 3
     )
@@ -1088,7 +1096,7 @@
     up_keep = joined([up_keep], [exchanged(up_send)])
     up_rows = by_row(up_keep)
     gmid, gcontext, logit, gsmall, out_send, out_keep = context_back(
-        bit, gnormed, attn, picked, grows, gate, dots, context, second_gain, w_out, shape_out,
+        bit, gnormed, attn, picked, grows, gate, dots, context_turned, second_gain, w_out, shape_out,
         wp, 3, deps=(up_keep,),
     )
 

time: 408 us -> 407 us (level)
  no operation moved by 1% of the time
where the time goes in v4:
time: 407 us; the launch traced here: 402 us
  Pallas kernels  288 us (71%)
  waiting for transfers between devices  47.9 us (12%)
  starting transfers between devices  27 us (7%)
  other arithmetic  14.5 us (4%)
  between operations  14.4 us (4%)
  local copies, waits for them, and re-layouts  10.4 us (3%)
    pallas_call x24, Pallas kernels, call(): return lambda *args: made(*args, *deps)  288 us
    ppermute x13, starting transfers between devices, shifted(): return lax.ppermute(value, 'col' if part == 'z' else 'row', moves)  25.1 us
    ppermute x5, waiting for transfers between devices, exchanged(): return lax.ppermute(send, 'col', pairs)  15.8 us
    all_gather x2, waiting for transfers between devices, gathered(): lax.all_gather(flat, BOTH, axis=0, tiled=True).reshape(rs, cs, *flat.shape)  14.5 us
    ppermute x13, waiting for transfers between devices, shifted(): return lax.ppermute(value, 'col' if part == 'z' else 'row', moves)  9.45 us
  transfers between devices with their start and end apart: 25, of which 9 were waited for; matrix products, arithmetic and copies ran while one was open for 4% of the time, Pallas kernels for 71%

profile of v4, /device:TPU:0, one launch (start us, length us, event | category | flops | bytes accessed | tf_op | source)
XLA Modules:
  0.0 402.1 jit_solution(8099852883659087564)
XLA Ops:
  8.6 2.2 pieces.1
  11.6 3.1 collective-permute-start
  14.7 2.6 collective-permute-start.1
  17.3 1.3 collective-permute-start.2
  18.6 1.3 reshape.262.refs_0_
  19.9 11.9 %pick.1.refs_1_.refs_2_.refs_3_.refs_6_ = bf16[1152,1024]{1,0:T(8,128)(2,1)} custom-call(s32[9,1,128]{2,1,0:T(1,128)} %reshape.262.refs_0_, bf16[9216,1024]{1,0:T(8,128)(2,1)} %refs_1_.9), custom_call_target="tpu_custom_call" | custom-call | flops 2415919104 | bytes 56623104 | tf_op jit(solution)/shard_map/pick/pallas_call | solution.py:56
  31.8 3.1 collective-permute-done.1
  36.1 1.5 collective-permute-start.3
  37.7 1.6 collective-permute-start.5
  39.3 8.1 %pick_first.1 = (bf16[1152,1024]{1,0:T(8,128)(2,1)}, f32[9216,1024]{1,0:T(8,128)}) custom-call(s32[9,1,128]{2,1,0:T(1,128)} %reshape.262.refs_0_, bf16[9216,1024]{1,0:T(8,128)(2,1)} %refs_1_.8, bf16[1,4,400,128]{3,2,1,0:T(8,128)(2,1)} %copy-done.2), custom_call_target="tpu_custom_call" | custom-call | flops 2415919104 | bytes 56623104 | tf_op jit(solution)/shard_map/pick_first/pallas_call | solution.py:56
  48.5 1.7 collective-permute-start.4
  51.2 1.5 collective-permute-start.6
  52.7 14.9 %pick_rest.1 = (bf16[1152,1024]{1,0:T(8,128)(2,1)}, f32[9216,1024]{1,0:T(8,128)}) custom-call(s32[9,1,128]{2,1,0:T(1,128)} %reshape.262.refs_0_, bf16[9216,1024]{1,0:T(8,128)(2,1)} %refs_1_.8, bf16[1152,1024]{1,0:T(8,128)(2,1)} %get-tuple-element.99.refs_1_.refs_2_, ...), custom_call_target="tpu_custom_call", output_to_operand_aliasing={{0}: (2, {}), {1}: (3, {})} | custom-call | flops 2415919104 | bytes 56623104 | tf_op jit(solution)/shard_map/pick_rest/pallas_call | solution.py:56
  67.6 4.2 %collective-permute-done.4 = bf16[2,4,400,128]{3,2,1,0:T(8,128)(2,1)S(1)} collective-permute-done((bf16[2,4,400,128]{3,2,1,0:T(8,128)(2,1)S(1)}, bf16[2,4,400,128]{3,2,1,0:T(8,128)(2,1)S(1)}, u32[]{:S(2)}, u32[]{:S(2)}) %collective-permute-start.4) | collective-permute-done | bytes 819232 | tf_op jit(solution)/shard_map/ppermute | solution.py:974
  72.7 1.5 pad_maximum_fusion.refs_3_.refs_7_
  74.3 2.1 collective-permute-done.6
  76.4 1.3 pad_maximum_fusion.1.refs_4_
  78.5 5.2 %collective-permute-done.8.refs_6_ = bf16[4,4,400,128]{3,2,1,0:T(8,128)(2,1)S(1)} collective-permute-done((bf16[4,4,400,128]{3,2,1,0:T(8,128)(2,1)}, bf16[4,4,400,128]{3,2,1,0:T(8,128)(2,1)S(1)}, u32[]{:S(2)}, u32[]{:S(2)}) %collective-permute-start.8) | collective-permute-done | bytes 1638432 | tf_op jit(solution)/shard_map/ppermute | solution.py:994
  83.6 1.2 copy-done.13
  84.8 17.8 %project.1 = (bf16[1152,3072]{1,0:T(8,128)(2,1)}, bf16[1024,3072]{1,0:T(8,128)(2,1)}, bf16[1024,1152]{1,0:T(8,128)(2,1)}, bf16[1152,1024]{1,0:T(8,128)(2,1)}, f32[1152,1]{1,0:T(8,128)}, /*index=5*/f32[3,1024]{1,0:T(4,128)}) custom-call(s32[4,4]{1,0:T(4,128)} %copy-done.12, bf16[1152,1024]{1,0:T(8,128)(2,1)} %pick.1.refs_1_.refs_2_.refs_3_.refs_6_, ...), custom_call_target="tpu_custom_call" | custom-call | flops 7247757312 | bytes 29097984 | tf_op jit(solution)/shard_map/project/pallas_call | solution.py:56
  102.6 1.4 fusion.16
  104.0 11.8 %attend.1 = (bf16[1152,1024]{1,0:T(8,128)(2,1)}, bf16[9,2048,128]{2,1,0:T(8,128)(2,1)}, bf16[1024,1152]{1,0:T(8,128)(2,1)}) custom-call(bf16[1152,3072]{1,0:T(8,128)(2,1)} %get-tuple-element.102.refs_0_), custom_call_target="tpu_custom_call" | custom-call | flops 9059696640 | bytes 28311552 | tf_op jit(solution)/shard_map/attend/pallas_call | solution.py:56
  115.9 10.0 %mix.1 = (f32[1152,1024]{1,0:T(8,128)}, bf16[1152,1024]{1,0:T(8,128)(2,1)}, bf16[1024,1152]{1,0:T(8,128)(2,1)}, bf16[1024,1024]{1,0:T(8,128)(2,1)}) custom-call(bf16[1152,1024]{1,0:T(8,128)(2,1)} %get-tuple-element.103.refs_0_, bf16[4,8,1280,128]{3,2,1,0:T(8,128)(2,1)} %bitcast.58, bf16[1152,1024]{1,0:T(8,128)(2,1)} %pick.1.refs_1_.refs_2_.refs_3_.refs_6_, ...), custom_call_target="tpu_custom_call" | custom-call | flops 2415919104 | bytes 16515072 | tf_op jit(solution)/shard_map/mix/pallas_call | solution.py:56
  125.8 40.2 %raise.1 = (bf16[1152,4096]{1,0:T(8,128)(2,1)}, bf16[1152,4096]{1,0:T(8,128)(2,1)}, bf16[1024,4096]{1,0:T(8,128)(2,1)}, bf16[4,4,1024,128]{3,2,1,0:T(8,128)(2,1)}, bf16[4,4,1024,128]{3,2,1,0:T(8,128)(2,1)}) custom-call(s32[1]{0:T(128)} %bitcast.refs_0_, bf16[1152,1024]{1,0:T(8,128)(2,1)} %get-tuple-element.106.refs_1_, ...), custom_call_target="tpu_custom_call" | custom-call | flops 24159191040 | bytes 46399488 | tf_op jit(solution)/shard_map/raise/pallas_call | solution.py:56
  166.1 7.4 %collective-permute-done.9.refs_1_ = bf16[4,4,1024,128]{3,2,1,0:T(8,128)(2,1)S(1)} collective-permute-done((bf16[4,4,1024,128]{3,2,1,0:T(8,128)(2,1)}, bf16[4,4,1024,128]{3,2,1,0:T(8,128)(2,1)S(1)}, u32[]{:S(2)}, u32[]{:S(2)}) %collective-permute-start.9) | collective-permute-done | bytes 4194336 | tf_op jit(solution)/shard_map/ppermute | solution.py:1053
  173.5 5.1 %join.3.refs_8_ = bf16[4,4,1024,128]{3,2,1,0:T(8,128)(2,1)} custom-call(bf16[4,4,1024,128]{3,2,1,0:T(8,128)(2,1)} %get-tuple-element.114.refs_0_, bf16[4,4,1024,128]{3,2,1,0:T(8,128)(2,1)S(1)} %collective-permute-done.9.refs_1_), custom_call_target="tpu_custom_call" | custom-call | flops 2097152 | bytes 12582912 | tf_op jit(solution)/shard_map/join/pallas_call | solution.py:56
  178.9 14.5 %all-gather.5.cloned.1.call-done = bf16[32768,128]{1,0:T(8,128)(2,1)} async-done(((bf16[1024,128]{1,0:T(8,128)(2,1)}), bf16[32768,128]{1,0:T(8,128)(2,1)}) %all-gather.5.cloned.1.call-update) | async-done | bytes 8388624 | tf_op jit(solution)/shard_map/all_gather | solution.py:963
  193.3 45.5 %feed_back.1 = (bf16[4096,1024]{1,0:T(8,128)(2,1)}, f32[1152,128]{1,0:T(8,128)}, bf16[4,4,1024,128]{3,2,1,0:T(8,128)(2,1)}, bf16[4,4,1024,128]{3,2,1,0:T(8,128)(2,1)}, f32[1152,1024]{1,0:T(8,128)}) custom-call(s32[1]{0:T(128)} %bitcast.refs_0_, bf16[1152,1024]{1,0:T(8,128)(2,1)} %get-tuple-element.101.refs_1_.refs_2_.refs_4_.refs_8_, ...), custom_call_target="tpu_custom_call" | custom-call | flops 28991029248 | bytes 53477376 | tf_op jit(solution)/shard_map/feed_back/pallas_call | solution.py:56
  239.1 7.2 %collective-permute-done.10.refs_1_ = bf16[4,4,1024,128]{3,2,1,0:T(8,128)(2,1)S(1)} collective-permute-done((bf16[4,4,1024,128]{3,2,1,0:T(8,128)(2,1)}, bf16[4,4,1024,128]{3,2,1,0:T(8,128)(2,1)S(1)}, u32[]{:S(2)}, u32[]{:S(2)}) %collective-permute-start.10) | collective-permute-done | bytes 4194336 | tf_op jit(solution)/shard_map/ppermute | solution.py:1053
  246.3 5.1 %join.4.refs_10_ = bf16[4,4,1024,128]{3,2,1,0:T(8,128)(2,1)} custom-call(bf16[4,4,1024,128]{3,2,1,0:T(8,128)(2,1)} %get-tuple-element.122.refs_0_, bf16[4,4,1024,128]{3,2,1,0:T(8,128)(2,1)S(1)} %collective-permute-done.10.refs_1_), custom_call_target="tpu_custom_call" | custom-call | flops 2097152 | bytes 12582912 | tf_op jit(solution)/shard_map/join/pallas_call | solution.py:56
  251.7 18.1 %context_back.1 = (f32[1152,1024]{1,0:T(8,128)}, bf16[1152,1024]{1,0:T(8,128)(2,1)}, f32[1152,1]{1,0:T(8,128)}, f32[2,1024]{1,0:T(2,128)}, bf16[4,4,256,128]{3,2...) custom-call(s32[1]{0:T(128)} %bitcast.refs_0_, f32[1152,1024]{1,0:T(8,128)} %get-tuple-element.118.refs_1_, ...), custom_call_target="tpu_custom_call" | custom-call | flops 4831838208 | bytes 36962304 | tf_op jit(solution)/shard_map/context_back/pallas_call | solution.py:56
  269.8 14.0 %attend_back.1.refs_2_.refs_3_.refs_1_ = bf16[1152,3072]{1,0:T(8,128)(2,1)} custom-call(bf16[1152,3072]{1,0:T(8,128)(2,1)} %get-tuple-element.102.refs_0_, bf16[1152,1024]{1,0:T(8,128)(2,1)} %get-tuple-element.124.refs_1_, bf16[9,2048,128]{2,1,0:T(8,128)(2,1)} %get-tuple-element.125.refs_2_), custom_call_target="tpu_custom_call" | custom-call | flops 18119393280 | bytes 56623104 | tf_op jit(solution)/shard_map/attend_back/pallas_call | solution.py:56
  283.8 9.7 %qkv_send.1 = (bf16[4,4,768,128]{3,2,1,0:T(8,128)(2,1)}, f32[1024,1]{1,0:T(8,128)}) custom-call(s32[1]{0:T(128)} %bitcast.refs_0_, bf16[1024,1152]{1,0:T(8,128)(2,1)} %get-tuple-element.130.refs_1_, bf16[1152,3072]{1,0:T(8,128)(2,1)} %attend_back.1.refs_2_.refs_3_.refs_1_, bf16[1152,3072]{1,0:T(8,128)(2,1)} %attend_back.1.refs_2_.refs_3_.refs_1_, ...), custom_call_target="tpu_custom_call" | custom-call | flops 3623878656 | bytes 11010048 | tf_op jit(solution)/shard_map/qkv_send/pallas_call | solution.py:56
  293.9 10.9 %qkv_keep.1 = (bf16[4,4,768,128]{3,2,1,0:T(8,128)(2,1)}, bf16[4,4,16,128]{3,2,1,0:T(8,128)(2,1)}, bf16[4,4,16,128]{3,2,1,0:T(8,128)(2,1)}) custom-call(s32[1]{0:T(128)} %bitcast.refs_0_, bf16[1024,1152]{1,0:T(8,128)(2,1)} %get-tuple-element.130.refs_1_, bf16[1152,3072]{1,0:T(8,128)(2,1)} %attend_back.1.refs_2_.refs_3_.refs_1_, ...), custom_call_target="tpu_custom_call" | custom-call | flops 3623878656 | bytes 11010048 | tf_op jit(solution)/shard_map/qkv_keep/pallas_call | solution.py:56
  305.1 1.2 collective-permute-done.13.refs_5_
  306.4 5.2 %join.5.refs_10_ = bf16[4,4,1040,128]{3,2,1,0:T(8,128)(2,1)} custom-call(bf16[4,4,768,128]{3,2,1,0:T(8,128)(2,1)} %get-tuple-element.134.refs_0_, bf16[4,4,256,128]{3,2,1,0:T(8,128)(2,1)} %get-tuple-element.135.refs_1_, bf16[4,4,16,128]{3,2,1,0:T(8,128)(2,1)} %get-tuple-element.136.refs_2_, bf16[4,4,768,128]{3,2,1,0:T(8,128)(2,1)S(1)} %collective-permute-done.11.refs_3_, ...), custom_call_target="tpu_custom_call" | custom-call | flops 2129920 | bytes 12779520 | tf_op jit(solution)/shard_map/join/pallas_call | solution.py:56
  312.9 2.4 fusion.1
  315.4 1.6 collective-permute-start.14
  316.9 1.2 collective-permute-start.15
  318.1 2.5 collective-permute-start.16
  320.6 21.5 %picked_back.1.refs_5_ = f32[9216,1024]{1,0:T(8,128)} custom-call(s32[1152]{0:T(1024)} %add_bitcast_fusion.refs_0_, bf16[1152,3072]{1,0:T(8,128)(2,1)} %attend_back.1.refs_2_.refs_3_.refs_1_, bf16[1024,3072]{1,0:T(8,128)(2,1)} %get-tuple-element.126.refs_4_.refs_5_.refs_2_, f32[1152,1]{1,0:T(8,128)} %get-tuple-element.127.refs_3_, ...), custom_call_target="tpu_custom_call", output_to_operand_aliasing={{}: (9, {})} | custom-call | flops 7247757312 | bytes 25165824 | tf_op jit(solution)/shard_map/picked_back/pallas_call | solution.py:56
  342.1 17.2 %lower.1.refs_1_.refs_2_ = bf16[1152,1024]{1,0:T(8,128)(2,1)} custom-call(bf16[1152,4096]{1,0:T(8,128)(2,1)} %get-tuple-element.108.refs_4_.refs_0_, bf16[4096,1024]{1,0:T(8,128)(2,1)} %get-tuple-element.116.refs_1_, f32[1152,1024]{1,0:T(8,128)} %get-tuple-element.117.refs_2_, bf16[1152,1024]{1,0:T(8,128)(2,1)} %pick.1.refs_1_.refs_2_.refs_3_.refs_6_, ...), custom_call_target="tpu_custom_call" | custom-call | flops 9663676416 | bytes 27262976 | tf_op jit(solution)/shard_map/lower/pallas_call | solution.py:56
  359.4 1.3 convert_add_fusion.refs_7_
  361.7 2.3 reduce-scatter.8.cloned.1.call-done
  363.9 2.0 dynamic-slice_bitcast_fusion
  365.9 4.1 %collective-permute-start.17 = (bf16[1040,128]{1,0:T(8,128)(2,1)S(1)}, bf16[1040,128]{1,0:T(8,128)(2,1)S(1)}, u32[]{:S(2)}, u32[]{:S(2)}) collective-permute-start(bf16[1040,128]{1,0:T(8,128)(2,1)S(1)} %get-tuple-element.145.refs_4_), channel_id=1, source_target_pairs={{0,2},{1,3},{2,4},{3,5},{4,6},{5,7},{6,0},{7,1},{8,10},{9,11},{10,... | collective-permute-start | bytes 798728 | tf_op jit(solution)/shard_map/ppermute | solution.py:974
  371.0 1.4 collective-permute-start.19
  373.2 18.9 %place.1.refs_1_ = bf16[9216,1024]{1,0:T(8,128)(2,1)} custom-call(s32[9,1,128]{2,1,0:T(1,128)} %reshape.262.refs_0_, bf16[9216,1024]{1,0:T(8,128)(2,1)} %refs_1_.9, bf16[1152,1024]{1,0:T(8,128)(2,1)} %lower.1.refs_1_.refs_2_, bf16[1040,128]{1,0:T(8,128)(2,1)} %get-tuple-element.146.refs_3_.refs_0_, bf16[1040,128]{1,0:T(8,128)(2,1)} %copy-done.9, ...), custom_call_target="tpu_custom_call" | custom-call | flops 2415919104 | bytes 37748736 | tf_op jit(solution)/shard_map/place/pallas_call | solution.py:56
  (97 shorter events, 16.1 us)
Async XLA Ops:
  7.2 108.7 %all-gather.3.cloned.1.call-start = ((), (), s32[]{:S(2)}) async-start(), calls=%async_computation.3 | async-start | bytes 10813440 | tf_op jit(solution)/shard_map/all_gather | solution.py:963
  10.8 182.6 %all-gather.5.cloned.1.call-start = ((), (), s32[]{:S(2)}) async-start(), calls=%async_computation.4 | async-start | bytes 8650752 | tf_op jit(solution)/shard_map/all_gather | solution.py:963
  11.5 301.4 %reduce-scatter.4.cloned.1.call-start = ((), (), s32[]{:S(2)}) async-start(), calls=%async_computation.5 | async-start | bytes 5242880 | tf_op jit(solution)/shard_map/reduce_scatter | solution.py:1057
  11.6 20.2 %collective-permute-start = (bf16[800,128]{1,0:T(8,128)(2,1)}, bf16[800,128]{1,0:T(8,128)(2,1)S(1)}, u32[]{:S(2)}, u32[]{:S(2)}) collective-permute-start(bf16[800,128]{1,0:T(8,128)(2,1)} %get-tuple-element.98.refs_0_), channel_id=1, source_target_pairs={{0,2},{1,3},{2,4},{3,5},{4,6},{5,7},{6,0},{7,1},{8,10},{9,11},{10,... | collective-permute-start | bytes 614408 | tf_op jit(solution)/shard_map/ppermute | solution.py:974
  14.7 20.3 %collective-permute-start.1 = (bf16[800,128]{1,0:T(8,128)(2,1)}, bf16[800,128]{1,0:T(8,128)(2,1)S(1)}, u32[]{:S(2)}, u32[]{:S(2)}) collective-permute-start(bf16[800,128]{1,0:T(8,128)(2,1)} %get-tuple-element.98.refs_0_), channel_id=1, source_target_pairs={{0,4},{1,5},{2,6},{3,7},{4,0},{5,1},{6,2},{7,3},{8,12},{9,13},{10,... | collective-permute-start | bytes 614408 | tf_op jit(solution)/shard_map/ppermute | solution.py:974
  17.3 17.7 %collective-permute-start.2 = (bf16[800,128]{1,0:T(8,128)(2,1)}, bf16[800,128]{1,0:T(8,128)(2,1)S(1)}, u32[]{:S(2)}, u32[]{:S(2)}) collective-permute-start(bf16[800,128]{1,0:T(8,128)(2,1)} %get-tuple-element.98.refs_0_), channel_id=1, source_target_pairs={{0,6},{1,7},{2,0},{3,1},{4,2},{5,3},{6,4},{7,5},{8,14},{9,15},{10,... | collective-permute-start | bytes 614408 | tf_op jit(solution)/shard_map/ppermute | solution.py:974
  36.1 3.2 copy-start.2
  36.1 11.3 %collective-permute-start.3 = (bf16[1,4,400,128]{3,2,1,0:T(8,128)(2,1)S(1)}, bf16[1,4,400,128]{3,2,1,0:T(8,128)(2,1)S(1)}, u32[]{:S(2)}, u32[]{:S(2)}) collective-permute-start(bf16[1,4,400,128]{3,2,1,0:T(8,128)(2,1)S(1)} %maximum_bitcast_fusion.refs_2_.refs_0_), channel_id=1, source_target_pairs={{0,8},{8,0},{16,24},{24,16},{1,9},{9,1},{17,25},{25,17},{2,10},{10... | collective-permute-start | bytes 1228808 | tf_op jit(solution)/shard_map/ppermute | solution.py:974
  37.7 12.6 %collective-permute-start.5 = (bf16[1,4,400,128]{3,2,1,0:T(8,128)(2,1)S(1)}, bf16[1,4,400,128]{3,2,1,0:T(8,128)(2,1)S(1)}, u32[]{:S(2)}, u32[]{:S(2)}) collective-permute-start(bf16[1,4,400,128]{3,2,1,0:T(8,128)(2,1)S(1)} %maximum_bitcast_fusion.1), channel_id=1, source_target_pairs={{0,16},{8,24},{16,0},{24,8},{1,17},{9,25},{17,1},{25,9},{2,18},{10... | collective-permute-start | bytes 1228808 | tf_op jit(solution)/shard_map/ppermute | solution.py:974
  48.5 4.2 %copy-start = (bf16[2,4,400,128]{3,2,1,0:T(8,128)(2,1)}, bf16[2,4,400,128]{3,2,1,0:T(8,128)(2,1)S(1)}, u32[]{:S(2)}) copy-start(bf16[2,4,400,128]{3,2,1,0:T(8,128)(2,1)S(1)} %pad_maximum_fusion.2.refs_4_.refs_0_) | copy-start | bytes 2457604
  48.5 23.3 %collective-permute-start.4 = (bf16[2,4,400,128]{3,2,1,0:T(8,128)(2,1)S(1)}, bf16[2,4,400,128]{3,2,1,0:T(8,128)(2,1)S(1)}, u32[]{:S(2)}, u32[]{:S(2)}) collective-permute-start(bf16[2,4,400,128]{3,2,1,0:T(8,128)(2,1)S(1)} %pad_maximum_fusion.2.refs_4_.refs_0_), channel_id=1, source_target_pairs={{0,16},{8,24},{16,0},{24,8},{1,17},{9,25},{17,1},{25,9},{2,18},{10... | collective-permute-start | bytes 2457608 | tf_op jit(solution)/shard_map/ppermute | solution.py:974
  51.2 25.2 %collective-permute-start.6 = (bf16[2,4,400,128]{3,2,1,0:T(8,128)(2,1)}, bf16[2,4,400,128]{3,2,1,0:T(8,128)(2,1)S(1)}, u32[]{:S(2)}, u32[]{:S(2)}) collective-permute-start(bf16[2,4,400,128]{3,2,1,0:T(8,128)(2,1)} %pad_maximum_fusion.3), channel_id=1, source_target_pairs={{0,8},{8,0},{16,24},{24,16},{1,9},{9,1},{17,25},{25,17},{2,10},{10... | collective-permute-start | bytes 2457608 | tf_op jit(solution)/shard_map/ppermute | solution.py:974
  71.8 0.9 copy-start.10
  74.2 9.4 %copy-start.6 = (bf16[4,4,400,128]{3,2,1,0:T(8,128)(2,1)}, bf16[4,4,400,128]{3,2,1,0:T(8,128)(2,1)S(1)}, u32[]{:S(2)}) copy-start(bf16[4,4,400,128]{3,2,1,0:T(8,128)(2,1)S(1)} %pad_maximum_fusion.refs_3_.refs_7_) | copy-start | bytes 4915204
  74.2 4.2 %collective-permute-start.7 = (bf16[4,4,400,128]{3,2,1,0:T(8,128)(2,1)S(1)}, bf16[4,4,400,128]{3,2,1,0:T(8,128)(2,1)}, u32[]{:S(2)}, u32[]{:S(2)}) collective-permute-start(bf16[4,4,400,128]{3,2,1,0:T(8,128)(2,1)S(1)} %pad_maximum_fusion.refs_3_.refs_7_), channel_id=1, source_target_pairs={{0,1},{1,0},{2,3},{3,2},{4,5},{5,4},{6,7},{7,6},{8,9},{9,8},{10,11... | collective-permute-start | bytes 4915208 | tf_op jit(solution)/shard_map/ppermute | solution.py:994
  77.7 5.9 %collective-permute-start.8 = (bf16[4,4,400,128]{3,2,1,0:T(8,128)(2,1)}, bf16[4,4,400,128]{3,2,1,0:T(8,128)(2,1)S(1)}, u32[]{:S(2)}, u32[]{:S(2)}) collective-permute-start(bf16[4,4,400,128]{3,2,1,0:T(8,128)(2,1)} %pad_maximum_fusion.1.refs_4_), channel_id=1, source_target_pairs={{0,1},{1,0},{2,3},{3,2},{4,5},{5,4},{6,7},{7,6},{8,9},{9,8},{10,11... | collective-permute-start | bytes 4915208 | tf_op jit(solution)/shard_map/ppermute | solution.py:994
  78.4 5.2 %copy-start.12 = (s32[4,4]{1,0:T(4,128)}, s32[4,4]{1,0:T(4,128)S(1)}, u32[]{:S(2)}) copy-start(s32[4,4]{1,0:T(4,128)S(1)} %scatter.19.refs_0_) | copy-start | bytes 196
  83.6 1.2 copy-start.13
  166.0 7.5 %collective-permute-start.9 = (bf16[4,4,1024,128]{3,2,1,0:T(8,128)(2,1)}, bf16[4,4,1024,128]{3,2,1,0:T(8,128)(2,1)S(1)}, u32[]{:S(2)}, u32[]{:S(2)}) collective-permute-start(bf16[4,4,1024,128]{3,2,1,0:T(8,128)(2,1)} %get-tuple-element.115), channel_id=1, source_target_pairs={{0,1},{1,0},{2,3},{3,2},{4,5},{5,4},{6,7},{7,6},{8,9},{9,8},{10,11... | collective-permute-start | bytes 12582920 | tf_op jit(solution)/shard_map/ppermute | solution.py:1053
  178.6 134.3 %reduce-scatter.6.cloned.1.call-start = ((), (), s32[]{:S(2)}) async-start(), calls=%async_computation.6 | async-start | bytes 5242880 | tf_op jit(solution)/shard_map/reduce_scatter | solution.py:1057
  238.9 7.4 %collective-permute-start.10 = (bf16[4,4,1024,128]{3,2,1,0:T(8,128)(2,1)}, bf16[4,4,1024,128]{3,2,1,0:T(8,128)(2,1)S(1)}, u32[]{:S(2)}, u32[]{:S(2)}) collective-permute-start(bf16[4,4,1024,128]{3,2,1,0:T(8,128)(2,1)} %get-tuple-element.123), channel_id=1, source_target_pairs={{0,1},{1,0},{2,3},{3,2},{4,5},{5,4},{6,7},{7,6},{8,9},{9,8},{10,11... | collective-permute-start | bytes 12582920 | tf_op jit(solution)/shard_map/ppermute | solution.py:1053
  251.4 112.5 %reduce-scatter.8.cloned.1.call-start = ((), (), s32[]{:S(2)}) async-start(), calls=%async_computation.7 | async-start | bytes 5324800 | tf_op jit(solution)/shard_map/reduce_scatter | solution.py:1057
  283.8 10.0 %copy-start.14 = (bf16[4,4,256,128]{3,2,1,0:T(8,128)(2,1)S(1)}, bf16[4,4,256,128]{3,2,1,0:T(8,128)(2,1)}, u32[]{:S(2)}) copy-start(bf16[4,4,256,128]{3,2,1,0:T(8,128)(2,1)} %get-tuple-element.137) | copy-start | bytes 3145732
  293.4 12.9 %collective-permute-start.11 = (bf16[4,4,768,128]{3,2,1,0:T(8,128)(2,1)}, bf16[4,4,768,128]{3,2,1,0:T(8,128)(2,1)S(1)}, u32[]{:S(2)}, u32[]{:S(2)}) collective-permute-start(bf16[4,4,768,128]{3,2,1,0:T(8,128)(2,1)} %get-tuple-element.133.refs_9_), channel_id=1, source_target_pairs={{0,1},{1,0},{2,3},{3,2},{4,5},{5,4},{6,7},{7,6},{8,9},{9,8},{10,11... | collective-permute-start | bytes 9437192 | tf_op jit(solution)/shard_map/ppermute | solution.py:1053
  293.7 12.6 %collective-permute-start.12 = (bf16[4,4,256,128]{3,2,1,0:T(8,128)(2,1)S(1)}, bf16[4,4,256,128]{3,2,1,0:T(8,128)(2,1)S(1)}, u32[]{:S(2)}, u32[]{:S(2)}) collective-permute-start(bf16[4,4,256,128]{3,2,1,0:T(8,128)(2,1)S(1)} %copy-done.14), channel_id=1, source_target_pairs={{0,1},{1,0},{2,3},{3,2},{4,5},{5,4},{6,7},{7,6},{8,9},{9,8},{10,11... | collective-permute-start | bytes 3145736 | tf_op jit(solution)/shard_map/ppermute | solution.py:1053
  304.8 1.5 collective-permute-start.13
  311.5 0.7 copy-start.11
  315.4 5.3 %copy-start.3 = (bf16[2048,128]{1,0:T(8,128)(2,1)}, bf16[2048,128]{1,0:T(8,128)(2,1)S(1)}, u32[]{:S(2)}) copy-start(bf16[2048,128]{1,0:T(8,128)(2,1)S(1)} %get-tuple-element.139.refs_14_) | copy-start | bytes 1572868
  315.4 5.3 %copy-start.4 = (bf16[2048,128]{1,0:T(8,128)(2,1)}, bf16[2048,128]{1,0:T(8,128)(2,1)S(1)}, u32[]{:S(2)}) copy-start(bf16[2048,128]{1,0:T(8,128)(2,1)S(1)} %get-tuple-element.142.refs_13_) | copy-start | bytes 1572868
  315.4 5.3 %copy-start.5 = (bf16[2048,128]{1,0:T(8,128)(2,1)}, bf16[2048,128]{1,0:T(8,128)(2,1)S(1)}, u32[]{:S(2)}) copy-start(bf16[2048,128]{1,0:T(8,128)(2,1)S(1)} %get-tuple-element.141.refs_12_) | copy-start | bytes 1572868
  315.4 44.0 %collective-permute-start.14 = (bf16[2048,128]{1,0:T(8,128)(2,1)S(1)}, bf16[2048,128]{1,0:T(8,128)(2,1)S(1)}, u32[]{:S(2)}, u32[]{:S(2)}) collective-permute-start(bf16[2048,128]{1,0:T(8,128)(2,1)S(1)} %get-tuple-element.141.refs_12_), channel_id=1, source_target_pairs={{0,2},{1,3},{2,4},{3,5},{4,6},{5,7},{6,0},{7,1},{8,10},{9,11},{10,... | collective-permute-start | bytes 1572872 | tf_op jit(solution)/shard_map/ppermute | solution.py:974
  316.9 42.4 %collective-permute-start.15 = (bf16[2048,128]{1,0:T(8,128)(2,1)S(1)}, bf16[2048,128]{1,0:T(8,128)(2,1)S(1)}, u32[]{:S(2)}, u32[]{:S(2)}) collective-permute-start(bf16[2048,128]{1,0:T(8,128)(2,1)S(1)} %get-tuple-element.142.refs_13_), channel_id=1, source_target_pairs={{0,4},{1,5},{2,6},{3,7},{4,0},{5,1},{6,2},{7,3},{8,12},{9,13},{10,... | collective-permute-start | bytes 1572872 | tf_op jit(solution)/shard_map/ppermute | solution.py:974
  318.1 41.2 %collective-permute-start.16 = (bf16[2048,128]{1,0:T(8,128)(2,1)S(1)}, bf16[2048,128]{1,0:T(8,128)(2,1)S(1)}, u32[]{:S(2)}, u32[]{:S(2)}) collective-permute-start(bf16[2048,128]{1,0:T(8,128)(2,1)S(1)} %get-tuple-element.139.refs_14_), channel_id=1, source_target_pairs={{0,6},{1,7},{2,0},{3,1},{4,2},{5,3},{6,4},{7,5},{8,14},{9,15},{10,... | collective-permute-start | bytes 1572872 | tf_op jit(solution)/shard_map/ppermute | solution.py:974
  360.6 5.2 %copy-start.1 = (f32[2048,128]{1,0:T(8,128)}, f32[2048,128]{1,0:T(8,128)S(1)}, u32[]{:S(2)}) copy-start(f32[2048,128]{1,0:T(8,128)S(1)} %convert_add_fusion.refs_7_) | copy-start | bytes 3145732
  365.9 7.4 %copy-start.7 = (bf16[1040,128]{1,0:T(8,128)(2,1)}, bf16[1040,128]{1,0:T(8,128)(2,1)S(1)}, u32[]{:S(2)}) copy-start(bf16[1040,128]{1,0:T(8,128)(2,1)S(1)} %get-tuple-element.143.refs_6_) | copy-start | bytes 798724
  365.9 7.4 %copy-start.8 = (bf16[1040,128]{1,0:T(8,128)(2,1)}, bf16[1040,128]{1,0:T(8,128)(2,1)S(1)}, u32[]{:S(2)}) copy-start(bf16[1040,128]{1,0:T(8,128)(2,1)S(1)} %get-tuple-element.144.refs_5_) | copy-start | bytes 798724
  365.9 7.4 %copy-start.9 = (bf16[1040,128]{1,0:T(8,128)(2,1)}, bf16[1040,128]{1,0:T(8,128)(2,1)S(1)}, u32[]{:S(2)}) copy-start(bf16[1040,128]{1,0:T(8,128)(2,1)S(1)} %get-tuple-element.145.refs_4_) | copy-start | bytes 798724
  365.9 26.2 %collective-permute-start.17 = (bf16[1040,128]{1,0:T(8,128)(2,1)S(1)}, bf16[1040,128]{1,0:T(8,128)(2,1)S(1)}, u32[]{:S(2)}, u32[]{:S(2)}) collective-permute-start(bf16[1040,128]{1,0:T(8,128)(2,1)S(1)} %get-tuple-element.145.refs_4_), channel_id=1, source_target_pairs={{0,2},{1,3},{2,4},{3,5},{4,6},{5,7},{6,0},{7,1},{8,10},{9,11},{10,... | collective-permute-start | bytes 798728 | tf_op jit(solution)/shard_map/ppermute | solution.py:974
  370.0 22.2 %collective-permute-start.18 = (bf16[1040,128]{1,0:T(8,128)(2,1)S(1)}, bf16[1040,128]{1,0:T(8,128)(2,1)S(1)}, u32[]{:S(2)}, u32[]{:S(2)}) collective-permute-start(bf16[1040,128]{1,0:T(8,128)(2,1)S(1)} %get-tuple-element.144.refs_5_), channel_id=1, source_target_pairs={{0,4},{1,5},{2,6},{3,7},{4,0},{5,1},{6,2},{7,3},{8,12},{9,13},{10,... | collective-permute-start | bytes 798728 | tf_op jit(solution)/shard_map/ppermute | solution.py:974
  371.0 21.1 %collective-permute-start.19 = (bf16[1040,128]{1,0:T(8,128)(2,1)S(1)}, bf16[1040,128]{1,0:T(8,128)(2,1)S(1)}, u32[]{:S(2)}, u32[]{:S(2)}) collective-permute-start(bf16[1040,128]{1,0:T(8,128)(2,1)S(1)} %get-tuple-element.143.refs_6_), channel_id=1, source_target_pairs={{0,6},{1,7},{2,0},{3,1},{4,2},{5,3},{6,4},{7,5},{8,14},{9,15},{10,... | collective-permute-start | bytes 798728 | tf_op jit(solution)/shard_map/ppermute | solution.py:974
Sparse Core Ops, SparseCore 0:
  11.4 101.8 all-gather.2
  116.9 76.3 all-gather.4
  196.3 51.2 reduce-scatter.3
  251.5 51.9 reduce-scatter.5
  311.7 52.1 reduce-scatter.7
